TPU v7x, 768 devices: a whole 4x8x12 slice. The times are simulated.
768 devices in a mesh: dp: 32 (over x, y), member: 2 (over core), expert: 12 (over z).
Axes of the slice: x: 4, y: 8, z: 12, core: 2. Of those that a mesh axis runs over, the one named last changes fastest.
Arguments:
- tokens: bfloat16 [8192, 1280], P(('dp', 'member')), may hold values from -6 to 6
- route_ids: int32 [2, 8192, 1], P(None, ('dp', 'member')), may hold values from 0 to 31; in each aligned block of 128 rows (0 to 127, 128 to 255, ..., all dimensions but the last counted through in order) at most 6 rows name the same one
- router: float32 [2, 1280, 32], replicated, may hold values from -0.15625 to 0.15625
- w_in: bfloat16 [2, 32, 1280, 4608], P('member', 'dp', None, 'expert'), may hold values from -0.15625 to 0.15625
- w_out: bfloat16 [2, 32, 4608, 1280], P('member', 'dp', 'expert'), may hold values from -0.09375 to 0.09375
- out_grad: bfloat16 [2, 8192, 1280], P(None, ('dp', 'member')), may hold values from -6 to 6
Outputs:
- moe_out: bfloat16 [2, 8192, 1280], P(None, ('dp', 'member'))
- token_grad: float32 [8192, 1280], P(('dp', 'member'))
- first_grad: bfloat16 [2, 32, 1280, 4608], P('member', 'dp', None, 'expert')
- second_grad: bfloat16 [2, 32, 4608, 1280], P('member', 'dp', 'expert')
- router_grad: float32 [2, 1280, 32], replicated
Inputs may be any that keep to these rules, and one draw needn't show every extreme that they name: `route_ids`: in each aligned block of 128 rows of one member no expert is named by more than 6 rows, and some block names some expert exactly 6 times.
All inputs are finite; a program needn't handle non-finite values.
Results may differ from a plain program's by a relative error of at most 0.022.
Values may be sent and summed in bfloat16 or wider, within the bound.
No kernel may reach another device: no remote copies, remote signals or barrier semaphores. Data moves between devices by JAX's collectives and lax.ppermute only.
A program may use at most 64 MiB of HBM per device.

v0:
```python
import jax
import jax.numpy as jnp
from jax import lax
from jax.sharding import PartitionSpec as P

tanh_scale = 0.7978845608028654
cubic_term = 0.044715


def gelu_pair(pre_act):
    inner = tanh_scale * (pre_act + cubic_term * pre_act * pre_act * pre_act)
    tanh_value = jnp.tanh(inner)
    value = 0.5 * pre_act * (1.0 + tanh_value)
    gelu_slope = 0.5 * (1.0 + tanh_value) + 0.5 * pre_act * (
        1.0 - tanh_value * tanh_value
    ) * tanh_scale * (1.0 + 3.0 * cubic_term * pre_act * pre_act)
    return (value, gelu_slope)


def slot_rank(expert_ids, experts):
    hot_table = (expert_ids[..., None] == jnp.arange(experts, dtype=jnp.int32)).astype(jnp.int32)
    earlier = jnp.cumsum(hot_table, axis=-2) - hot_table
    return jnp.sum(earlier * hot_table, axis=-1)


def dispatch(x_send, g_send, experts, members, capacity):
    row_width = x_send.shape[1]
    arrived = (
        lax.all_to_all(
            x_send.reshape(experts * members, capacity, row_width),
            ("dp", "member"),
            split_axis=0,
            concat_axis=0,
            tiled=True,
        ),
        lax.all_to_all(
            g_send.reshape(experts * members, capacity, row_width),
            ("dp", "member"),
            split_axis=0,
            concat_axis=0,
            tiled=True,
        ),
    )
    return (arrived[0].reshape(-1, row_width), arrived[1].reshape(-1, row_width))


def send_back(first_rows, second_rows, capacity):
    row_width = first_rows.shape[1]
    dp_count = lax.axis_size("dp")
    member_count = lax.axis_size("member")
    arrived = (
        lax.all_to_all(
            first_rows.reshape(dp_count * member_count, capacity, row_width),
            ("dp", "member"),
            split_axis=0,
            concat_axis=0,
            tiled=True,
        ),
        lax.all_to_all(
            second_rows.reshape(dp_count * member_count, capacity, row_width),
            ("dp", "member"),
            split_axis=0,
            concat_axis=0,
            tiled=True,
        ),
    )
    return (arrived[0].reshape(-1, row_width), arrived[1].reshape(-1, row_width))


def block_sums(first_part, second_part):
    return (
        lax.psum(first_part, "expert").astype(jnp.float32),
        lax.psum(second_part, "expert").astype(jnp.float32),
    )


def shards(tokens, route_ids, router, w_in, w_out, out_grad):
    members = route_ids.shape[0]
    tok_rows = route_ids.shape[1]
    experts = router.shape[2]
    model_width = tokens.shape[1]
    capacity = max(2, 3 * tok_rows // (2 * experts))
    expert_ids = route_ids[:, :, 0]
    slot_rows = slot_rank(expert_ids, experts)
    member_index = jnp.arange(members, dtype=jnp.int32)[:, None]
    buffer_index = ((expert_ids * members + member_index) * capacity + slot_rows).reshape(-1)
    tokens_f = tokens.astype(jnp.float32)
    hot_table = (expert_ids[..., None] == jnp.arange(experts, dtype=jnp.int32)).astype(jnp.float32)
    logits = jnp.einsum("td,mde->mte", tokens_f, router, precision=lax.Precision.HIGHEST)
    gate_value = jax.nn.sigmoid(jnp.sum(logits * hot_table, axis=-1))
    scaled = (gate_value[..., None] * out_grad.astype(jnp.float32)).astype(jnp.bfloat16)
    total_rows = experts * members * capacity
    token_copies = jnp.broadcast_to(tokens[None], (members, tok_rows, model_width)).reshape(
        -1, model_width
    )
    x_send = jnp.zeros((total_rows, model_width), jnp.bfloat16).at[buffer_index].set(token_copies)
    g_send = (
        jnp.zeros((total_rows, model_width), jnp.bfloat16)
        .at[buffer_index]
        .set(scaled.reshape(-1, model_width))
    )
    x_rows, g_rows = dispatch(x_send, g_send, experts, members, capacity)
    w_first = w_in[0, 0]
    w_second = w_out[0, 0]
    pre_act = jnp.dot(x_rows, w_first, preferred_element_type=jnp.float32)
    act_value, gelu_slope = gelu_pair(pre_act)
    activation = act_value.astype(jnp.bfloat16)
    hidden_grad = jnp.einsum("rd,hd->rh", g_rows, w_second, preferred_element_type=jnp.float32)
    pre_grad = (hidden_grad * gelu_slope).astype(jnp.bfloat16)
    grad_first = jnp.einsum("rd,rh->dh", x_rows, pre_grad, preferred_element_type=jnp.float32)
    grad_second = jnp.einsum("rh,rd->hd", activation, g_rows, preferred_element_type=jnp.float32)
    part_out = jnp.dot(activation, w_second, preferred_element_type=jnp.float32).astype(
        jnp.bfloat16
    )
    part_dx = jnp.einsum("rh,dh->rd", pre_grad, w_first, preferred_element_type=jnp.float32).astype(
        jnp.bfloat16
    )
    out_total, dx_total = block_sums(part_out, part_dx)
    back_out, back_dx = send_back(
        out_total.astype(jnp.bfloat16), dx_total.astype(jnp.bfloat16), capacity
    )
    expert_output = back_out[buffer_index].reshape(members, tok_rows, model_width)
    expert_dx = back_dx[buffer_index].reshape(members, tok_rows, model_width)
    output_f = expert_output.astype(jnp.float32)
    moe_out = (gate_value[..., None] * output_f).astype(jnp.bfloat16)
    gate_grad = jnp.sum(out_grad.astype(jnp.float32) * output_f, axis=-1)
    logit_grad = gate_grad * gate_value * (1.0 - gate_value)
    weighted = hot_table * logit_grad[..., None]
    router_local = jnp.einsum("td,mte->mde", tokens_f, weighted, precision=lax.Precision.HIGHEST)
    router_grad = lax.psum(router_local, ("dp", "member"))
    router_term = jnp.einsum("mte,mde->td", weighted, router, precision=lax.Precision.HIGHEST)
    token_grad = router_term + jnp.sum(expert_dx.astype(jnp.float32), axis=0)
    first_grad = grad_first.astype(jnp.bfloat16)[None, None]
    second_grad = grad_second.astype(jnp.bfloat16)[None, None]
    return (moe_out, token_grad, first_grad, second_grad, router_grad)


def solution(mesh):
    in_specs = (
        P(("dp", "member"), None),
        P(None, ("dp", "member"), None),
        P(),
        P("member", "dp", None, "expert"),
        P("member", "dp", "expert", None),
        P(None, ("dp", "member"), None),
    )
    out_specs = (
        P(None, ("dp", "member"), None),
        P(("dp", "member"), None),
        P("member", "dp", None, "expert"),
        P("member", "dp", "expert", None),
        P(),
    )
    return jax.shard_map(shards, mesh=mesh, in_specs=in_specs, out_specs=out_specs, check_vma=False)
```

profile of v0, /device:TPU:6, one launch (start us, length us, event | category | flops | bytes accessed | tf_op | source)
XLA Modules:
  0.0 528.3 jit_solution(18190696972112532995)
XLA Ops:
  10.7 2.0 scatter_custom_fusion
  14.0 14.0 %all-to-all-start = ((bf16[64,6,1280]{2,1,0:T(8,128)(2,1)}), bf16[64,6,1280]{2,1,0:T(8,128)(2,1)S(1)}, u32[]{:S(2)}, u32[]{:S(2)}) async-start(bf16[64,6,1280]{2,1,0:T(8,128)(2,1)} %reshape.109), calls=%async_computation | async-start | bytes 2621440 | tf_op jit(solution)/shard_map/all_to_all | solution.py:29
  28.1 1.5 fusion.8
  30.6 2.5 scatter_custom_fusion.1
  34.4 26.0 %all-to-all-done = bf16[64,6,1280]{2,1,0:T(8,128)(2,1)S(1)} async-done(((bf16[64,6,1280]{2,1,0:T(8,128)(2,1)}), bf16[64,6,1280]{2,1,0:T(8,128)(2,1)S(1)}, u32[]{:S(2)}, u32[]{:S(2)}) %all-to-all-start) | async-done | bytes 983072 | tf_op jit(solution)/shard_map/all_to_all | solution.py:29
  60.4 8.2 %all-to-all-start.2 = ((bf16[64,6,1280]{2,1,0:T(8,128)(2,1)}), bf16[64,6,1280]{2,1,0:T(8,128)(2,1)}, u32[]{:S(2)}, u32[]{:S(2)}) async-start(bf16[64,6,1280]{2,1,0:T(8,128)(2,1)} %reshape.114), calls=%async_computation.2 | async-start | bytes 2621440 | tf_op jit(solution)/shard_map/all_to_all | solution.py:36
  69.0 1.9 fusion.12
  71.7 1.7 convolution_convert_fusion.3
  73.4 27.4 %all-to-all-done.2 = bf16[64,6,1280]{2,1,0:T(8,128)(2,1)} async-done(((bf16[64,6,1280]{2,1,0:T(8,128)(2,1)}), bf16[64,6,1280]{2,1,0:T(8,128)(2,1)}, u32[]{:S(2)}, u32[]{:S(2)}) %all-to-all-start.2) | async-done | bytes 983072 | tf_op jit(solution)/shard_map/all_to_all | solution.py:36
  100.8 1.5 reshape.115
  103.3 1.9 fusion.6
  105.2 2.4 reshape.111
  107.6 1.6 convolution_convert_fusion.2
  109.3 2.3 reshape.116
  111.5 125.6 %all-reduce.6.cloned.1.call-done = (bf16[64,6,1280]{2,1,0:T(8,128)(2,1)}, bf16[64,6,1280]{2,1,0:T(8,128)(2,1)}) async-done(((bf16[64,6,1280]{2,1,0:T(8,128)(2,1)}, bf16[64,6,1280]{2,1,0:T(8,128)(2,1)}), (bf16[64,6,1280]{2,1,0:T(8,128)(2,1)}, bf16[64,6,1280]{2,1,0:T(8,128)(2,1)})) %all-reduce.6.cloned.1.call-update) | async-done | bytes 1966096 | tf_op jit(solution)/shard_map/psum | solution.py:72
  237.1 42.7 %all_to_all.20 = bf16[64,6,1280]{2,1,0:T(8,128)(2,1)S(1)} all-to-all(bf16[64,6,1280]{2,1,0:T(8,128)(2,1)} %get-tuple-element.5), channel_id=1, replica_groups=mesh['dp'=32,'member'=2,'expert'=12] {'dp','member'}, dimensions={0} | all-to-all | bytes 1966080 | tf_op jit(solution)/shard_map/all_to_all | solution.py:52
  279.9 8.2 %all-to-all-start.3 = ((bf16[64,6,1280]{2,1,0:T(8,128)(2,1)}), bf16[64,6,1280]{2,1,0:T(8,128)(2,1)}, u32[]{:S(2)}, u32[]{:S(2)}) async-start(bf16[64,6,1280]{2,1,0:T(8,128)(2,1)} %get-tuple-element.6), calls=%async_computation.3 | async-start | bytes 2621440 | tf_op jit(solution)/shard_map/all_to_all | solution.py:59
  288.4 2.8 fusion
  291.2 1.7 fusion.1
  295.8 24.5 %all-to-all-done.3 = bf16[64,6,1280]{2,1,0:T(8,128)(2,1)} async-done(((bf16[64,6,1280]{2,1,0:T(8,128)(2,1)}), bf16[64,6,1280]{2,1,0:T(8,128)(2,1)}, u32[]{:S(2)}, u32[]{:S(2)}) %all-to-all-start.3) | async-done | bytes 983072 | tf_op jit(solution)/shard_map/all_to_all | solution.py:59
  320.3 1.5 reshape.117
  325.1 1.6 fusion.2
  326.6 193.1 %all-reduce.4.cloned.1.call-done = f32[2,1280,32]{1,2,0:T(8,128)} async-done(((f32[2,1280,32]{1,2,0:T(8,128)}), f32[2,1280,32]{1,2,0:T(8,128)}) %all-reduce.4.cloned.1.call-update) | async-done | bytes 327696 | tf_op jit(solution)/shard_map/psum | solution.py:130
  519.7 1.7 copy.18
  (52 shorter events, 15.7 us)
Async XLA Ops:
  7.2 64.5 %copy-start = (bf16[1,1,384,1280]{3,2,1,0:T(8,128)(2,1)S(1)}, bf16[1,1,384,1280]{3,2,1,0:T(8,128)(2,1)}, u32[]{:S(2)}) copy-start(bf16[1,1,384,1280]{3,2,1,0:T(8,128)(2,1)} %param.10) | copy-start | bytes 2949124
  14.0 14.1 %copy-start.2 = (bf16[128,1280]{1,0:T(8,128)(2,1)S(1)}, bf16[128,1280]{1,0:T(8,128)(2,1)}, u32[]{:S(2)}) copy-start(bf16[128,1280]{1,0:T(8,128)(2,1)} %param.6) | copy-start | bytes 983044
  14.0 14.1 %copy-start.12 = (s32[2,128,1]{1,2,0:T(1,128)S(1)}, s32[2,128,1]{1,2,0:T(1,128)}, u32[]{:S(2)}) copy-start(s32[2,128,1]{1,2,0:T(1,128)} %param.7) | copy-start | bytes 3076
  14.0 15.5 %copy-start.4 = (bf16[2,128,1280]{2,1,0:T(8,128)(2,1)S(1)}, bf16[2,128,1280]{2,1,0:T(8,128)(2,1)}, u32[]{:S(2)}) copy-start(bf16[2,128,1280]{2,1,0:T(8,128)(2,1)} %param.11) | copy-start | bytes 1966084
  14.0 46.3 %all-to-all-start = ((bf16[64,6,1280]{2,1,0:T(8,128)(2,1)}), bf16[64,6,1280]{2,1,0:T(8,128)(2,1)S(1)}, u32[]{:S(2)}, u32[]{:S(2)}) async-start(bf16[64,6,1280]{2,1,0:T(8,128)(2,1)} %reshape.109), calls=%async_computation | async-start | bytes 2621440 | tf_op jit(solution)/shard_map/all_to_all | solution.py:29
  60.4 40.5 %all-to-all-start.2 = ((bf16[64,6,1280]{2,1,0:T(8,128)(2,1)}), bf16[64,6,1280]{2,1,0:T(8,128)(2,1)}, u32[]{:S(2)}, u32[]{:S(2)}) async-start(bf16[64,6,1280]{2,1,0:T(8,128)(2,1)} %reshape.114), calls=%async_computation.2 | async-start | bytes 2621440 | tf_op jit(solution)/shard_map/all_to_all | solution.py:36
  68.6 168.5 %all-reduce.6.cloned.1.call-start = ((), (), s32[]{:S(2)}) async-start(), calls=%async_computation.5 | async-start | bytes 5242880 | tf_op jit(solution)/shard_map/psum | solution.py:72
  70.9 0.8 copy-start.10
  102.3 1.0 copy-start.8
  105.2 4.1 copy-start.7
  105.2 2.4 copy-start.1
  279.9 40.5 %all-to-all-start.3 = ((bf16[64,6,1280]{2,1,0:T(8,128)(2,1)}), bf16[64,6,1280]{2,1,0:T(8,128)(2,1)}, u32[]{:S(2)}, u32[]{:S(2)}) async-start(bf16[64,6,1280]{2,1,0:T(8,128)(2,1)} %get-tuple-element.6), calls=%async_computation.3 | async-start | bytes 2621440 | tf_op jit(solution)/shard_map/all_to_all | solution.py:59
  288.1 231.6 %all-reduce.4.cloned.1.call-start = ((), (), s32[]{:S(2)}) async-start(), calls=%async_computation.4 | async-start | bytes 655360 | tf_op jit(solution)/shard_map/psum | solution.py:130
  288.3 2.9 copy-start.9
  288.3 2.9 copy-start.11
  293.3 1.3 copy-start.5
  323.0 1.0 copy-start.3
  323.0 2.0 copy-start.6
Sparse Core Ops, SparseCore 0:
  111.7 125.4 all-reduce.5
  325.2 194.4 all-reduce.3
where the time goes:
time: 531 us; the launch traced here: 528 us
  waiting for transfers between devices  397 us (75%)
  blocking collectives  42.7 us (8%)
  starting transfers between devices  30.7 us (6%)
  local copies, waits for them, and re-layouts  23.4 us (4%)
  matrix products  15.7 us (3%)
  between operations  14.3 us (3%)
    psum x1, waiting for transfers between devices, shards(): router_grad = lax.psum(router_local, ('dp', 'member'))  193 us
    psum x1, waiting for transfers between devices, block_sums(): lax.psum(first_part, 'expert').astype(jnp.float32)  126 us
    all_to_all x1, blocking collectives, send_back(): lax.all_to_all(first_rows.reshape(dp_count * member_count, capacity, row_...  42.7 us
    all_to_all x1, waiting for transfers between devices, dispatch(): lax.all_to_all(g_send.reshape(experts * members, capacity, row_width), ('...  27.4 us
    all_to_all x1, waiting for transfers between devices, dispatch(): lax.all_to_all(x_send.reshape(experts * members, capacity, row_width), ('...  26 us
    all_to_all x1, waiting for transfers between devices, send_back(): lax.all_to_all(second_rows.reshape(dp_count * member_count, capacity, row...  24.5 us
    all_to_all x1, starting transfers between devices, dispatch(): lax.all_to_all(x_send.reshape(experts * members, capacity, row_width), ('...  14 us
  transfers between devices with their start and end apart: 5, of which 5 were waited for; matrix products, arithmetic and copies ran while one was open for 4% of the time, Pallas kernels for 0%

commit v1 on v0

v1 whole, which is shorter than its diff:
```python
import functools

import jax
import jax.numpy as jnp
from jax import lax
from jax.experimental import pallas as pl
from jax.experimental.pallas import tpu as pltpu
from jax.sharding import PartitionSpec as P

BF = jnp.bfloat16
F32 = jnp.float32
tanh_scale = 0.7978845608028654
cubic_term = 0.044715
LIMIT = 44 << 20
VM = pl.BlockSpec(memory_space=pltpu.VMEM)
SM = pl.BlockSpec(memory_space=pltpu.SMEM)


def iota(shape, axis):
    return lax.broadcasted_iota(jnp.int32, shape, axis)


def one(mask):
    return jnp.where(mask, 1.0, 0.0).astype(BF)


def to_column(row):
    n = row.shape[1]
    eye = iota((n, n), 0) == iota((n, n), 1)
    return jnp.sum(jnp.where(eye, row, 0), axis=1, keepdims=True)


def dispatch_kernel(ids_ref, tok_ref, grad_ref, msg_ref, code_ref):
    tok_rows, width = tok_ref.shape
    half = width // 2
    codes = []
    for m in range(2):
        ids = ids_ref[m : m + 1, :]
        same = to_column(ids) == ids
        earlier = iota((tok_rows, tok_rows), 0) < iota((tok_rows, tok_rows), 1)
        slot = jnp.sum(jnp.where(same & earlier, 1, 0), axis=0, keepdims=True)
        code = ids * 8 + slot
        code_ref[m : m + 1, :] = code
        codes.append(code)
    sides = [
        jnp.concatenate([v[:, :half], v[:, half:]], axis=0)
        for v in (tok_ref[...], grad_ref[0], grad_ref[1])
    ]
    block = 256
    for b in range(msg_ref.shape[0] // block):
        row = iota((block, tok_rows), 0) + b * block
        dest = lax.shift_right_logical(row * 2731, 16)
        rest = row - dest * 24
        slot = 2 * lax.shift_right_logical(rest, 3) + (rest & 1)
        kind = lax.shift_right_logical(rest & 7, 1)
        code = lax.shift_right_logical(dest, 1) * 8 + slot
        member = dest & 1
        hit0 = (code == codes[0]) & (member == 0)
        hit1 = (code == codes[1]) & (member == 1)
        hit = hit0 | hit1
        parts = (
            [hit & (kind == 0), hit & (kind == 1)],
            [hit0 & (kind == 2), hit0 & (kind == 3)],
            [hit1 & (kind == 2), hit1 & (kind == 3)],
        )
        total = None
        for pair, side in zip(parts, sides):
            pick = jnp.concatenate([one(p) for p in pair], axis=1)
            term = jnp.dot(pick, side, preferred_element_type=F32)
            total = term if total is None else total + term
        msg_ref[pl.ds(b * block, block), :] = total.astype(BF)


def nt(a, b):
    return lax.dot_general(a, b, (((1,), (1,)), ((), ())), preferred_element_type=F32)


def tn(a, b):
    return lax.dot_general(a, b, (((0,), (0,)), ((), ())), preferred_element_type=F32)


def expert_kernel(
    stride, msg_ref, first_ref, second_ref, router_ref, part_ref, x_ref, g_ref, pre_ref, act_ref
):
    rows, width = x_ref.shape
    half = width // 2
    chunks = width // 128
    first = first_ref[...]
    second = second_ref[...]
    router = router_ref[...]
    p = iota((256, 256), 0)
    source = (
        lax.shift_right_logical(p & 63, 1) * 8 + lax.shift_right_logical(p, 6) * 2 + (p & 1)
    )
    sort = one(source == iota((256, 256), 1))
    router_sum = jnp.zeros((1, width), F32)
    block = 128
    for b in range(rows // block):
        for k in range(2):
            part = jnp.dot(
                sort, msg_ref[pl.ds((2 * b + k) * 256, 256), :], preferred_element_type=F32
            ).astype(BF)
            here = pl.ds(b * block + k * 64, 64)
            x_ref[here, 0:half] = part[0:64]
            x_ref[here, half:width] = part[64:128]
            g_ref[here, 0:half] = part[128:192]
            g_ref[here, half:width] = part[192:256]
        here = pl.ds(b * block, block)
        x = x_ref[here, :]
        g = g_ref[here, :]
        xf = x.astype(F32)
        logit = jnp.sum(xf * router, axis=1, keepdims=True)
        gate = 1.0 / (1.0 + jnp.exp(-logit))
        pre = jnp.dot(x, first, preferred_element_type=F32)
        hidden = nt(g, second)
        tanh_value = jnp.tanh(tanh_scale * (pre + cubic_term * pre * pre * pre))
        act = 0.5 * pre * (1.0 + tanh_value)
        slope = 0.5 * (1.0 + tanh_value) + 0.5 * pre * (
            1.0 - tanh_value * tanh_value
        ) * tanh_scale * (1.0 + 3.0 * cubic_term * pre * pre)
        gate_grad = jnp.sum(act * hidden, axis=1, keepdims=True)
        logit_grad = gate_grad * gate * (1.0 - gate)
        pre_grad = (hidden * gate * slope).astype(BF)
        scaled_act = (act * gate).astype(BF)
        pre_ref[here, :] = pre_grad
        act_ref[here, :] = scaled_act
        router_sum = router_sum + jnp.sum(xf * logit_grad, axis=0, keepdims=True)
        out = jnp.dot(scaled_act, second, preferred_element_type=F32).astype(BF)
        dx = (nt(pre_grad, first) + logit_grad * router).astype(BF)
        for c in range(chunks):
            lanes = slice(c * 128, (c + 1) * 128)
            part_ref[pl.ds(c * stride + b * block, block), :] = out[:, lanes]
            part_ref[pl.ds(c * stride + rows + b * block, block), :] = dx[:, lanes]
    for c in range(chunks):
        lanes = slice(c * 128, (c + 1) * 128)
        tail = jnp.where(iota((16, 128), 0) == 0, router_sum[:, lanes], 0.0)
        part_ref[pl.ds(c * stride + 2 * rows, 16), :] = tail.astype(BF)
    left = part_ref.shape[0] - chunks * stride
    part_ref[pl.ds(chunks * stride, left), :] = jnp.zeros((left, 128), BF)


def weight_kernel(x_ref, g_ref, pre_ref, act_ref, first_ref, second_ref):
    first_ref[...] = tn(x_ref[...], pre_ref[...]).astype(BF)
    second_ref[...] = tn(act_ref[...], g_ref[...]).astype(BF)


def return_kernel(rows, shift_ref, sum_ref, msg_ref, hold_ref):
    depth = hold_ref.shape[0]
    given = sum_ref.shape[0]
    base = given // 16 * 16
    hold_ref[pl.ds(base, depth - base), :] = jnp.zeros((depth - base, 128), BF)
    hold_ref[pl.ds(0, given), :] = sum_ref[...]
    shift = shift_ref[0]
    held = hold_ref[...]
    block = 256
    for b in range(msg_ref.shape[0] // block):
        row = iota((block, depth), 0) + b * block
        source = lax.shift_right_logical(row, 4)
        r = row & 15
        want = jnp.where(r < 6, source * 6 + r, rows + source * 6 + r - 6)
        want = jnp.where(r < 12, want, jnp.where(r == 12, 2 * rows, -depth)) + shift
        msg_ref[pl.ds(b * block, block), :] = jnp.dot(
            one(want == iota((block, depth), 1)), held, preferred_element_type=F32
        ).astype(BF)


def collect_kernel(code_ref, msg_ref, out_ref, rest_ref):
    held = msg_ref[...]
    depth = held.shape[0]
    tok_rows = code_ref.shape[1]
    picked = None
    for m in range(2):
        code = to_column(code_ref[m : m + 1, :])
        want = (lax.shift_right_logical(code, 3) * 2 + m) * 16 + (code & 7)
        lane = iota((tok_rows, depth), 1)
        out_ref[pl.ds(m * tok_rows, tok_rows), :] = jnp.dot(
            one(lane == want), held, preferred_element_type=F32
        ).astype(BF)
        pick = one(lane == want + 6)
        picked = pick if picked is None else picked + pick
    rest_ref[pl.ds(0, tok_rows), :] = jnp.dot(picked, held, preferred_element_type=F32).astype(BF)
    n = depth // 16
    row = iota((n, depth), 0)
    want = ((row & (n // 2 - 1)) * 2 + jnp.where(row >= n // 2, 1, 0)) * 16 + 12
    rest_ref[pl.ds(tok_rows, n), :] = jnp.dot(
        one(iota((n, depth), 1) == want), held, preferred_element_type=F32
    ).astype(BF)


def final_kernel(out_ref, rest_ref, moe_ref, token_ref, router_ref):
    tok_rows = token_ref.shape[0]
    for c in range(token_ref.shape[1] // 128):
        lanes = slice(c * 128, (c + 1) * 128)
        moe_ref[:, lanes] = out_ref[c]
        token_ref[:, lanes] = rest_ref[c, 0:tok_rows, :].astype(F32)
        router_ref[:, lanes] = rest_ref[c, tok_rows:, :].astype(F32)


def call(kernel, out, n_in, name, flops, size, scratch=(), smem_first=False):
    specs = [SM if smem_first and k == 0 else VM for k in range(n_in)]
    return pl.pallas_call(
        kernel,
        out_shape=[jax.ShapeDtypeStruct(s, d) for s, d in out],
        in_specs=specs,
        out_specs=[VM] * len(out),
        scratch_shapes=list(scratch),
        compiler_params=pltpu.CompilerParams(vmem_limit_bytes=LIMIT),
        cost_estimate=pl.CostEstimate(flops=flops, bytes_accessed=size, transcendentals=0),
        name=name,
    )


def shards(tokens, route_ids, router, w_in, w_out, out_grad):
    members, tok_rows = route_ids.shape[0], route_ids.shape[1]
    experts, width = router.shape[2], router.shape[1]
    hidden = w_in.shape[3]
    places = experts * members
    capacity = 3 * tok_rows // (2 * experts)
    rows = places * capacity
    half = width // 2
    plane = ("dp", "member")
    z_count = lax.axis_size("expert")
    z = lax.axis_index("expert")

    msg, codes = call(
        dispatch_kernel,
        [((rows * 4, half), BF), ((members, tok_rows), jnp.int32)],
        3, "dispatch", 3 << 30, 4 << 20,
    )(route_ids[:, :, 0], tokens, out_grad)
    arrived = lax.all_to_all(
        msg.reshape(places, 4 * capacity, half), plane, split_axis=0, concat_axis=0, tiled=True
    ).reshape(rows * 4, half)
    column = lax.dynamic_slice(
        router, (lax.axis_index("member"), 0, lax.axis_index("dp")), (1, width, 1)
    ).reshape(1, width)
    stride = 2 * rows + 16
    share = stride - 1
    part, x_rows, g_rows, pre_grad, scaled_act = call(
        functools.partial(expert_kernel, stride),
        [
            ((z_count * share, 128), BF),
            ((rows, width), BF),
            ((rows, width), BF),
            ((rows, hidden), BF),
            ((rows, hidden), BF),
        ],
        4, "expert", 3 << 30, 12 << 20,
    )(arrived, w_in[0, 0], w_out[0, 0], column)
    total = lax.psum_scatter(part, "expert", scatter_dimension=0, tiled=True)
    (back,) = call(
        functools.partial(return_kernel, rows),
        [((places * 16, 128), BF)],
        2, "to_tokens", 1 << 28, 1 << 20,
        scratch=[pltpu.VMEM((-(-share // 128) * 128, 128), BF)],
        smem_first=True,
    )(z.reshape(1), total)
    home = lax.all_to_all(
        back.reshape(places, 16, 128), plane, split_axis=0, concat_axis=0, tiled=True
    ).reshape(places * 16, 128)
    grad_first, grad_second = call(
        weight_kernel,
        [((width, hidden), BF), ((hidden, width), BF)],
        4, "weights", 1 << 30, 6 << 20,
    )(x_rows, g_rows, pre_grad, scaled_act)
    out_own, rest_own = call(
        collect_kernel,
        [((members * tok_rows, 128), BF), ((tok_rows + places, 128), BF)],
        2, "collect", 1 << 28, 1 << 20,
    )(codes, home)
    out_all = lax.all_gather(out_own, "expert")
    rest_all = lax.all_gather(rest_own, "expert")
    moe, token_grad, router_rows = call(
        final_kernel,
        [((members * tok_rows, width), BF), ((tok_rows, width), F32), ((places, width), F32)],
        2, "final", 1 << 20, 4 << 20,
    )(out_all, rest_all)
    router_grad = jnp.transpose(router_rows.reshape(members, experts, width), (0, 2, 1))
    return (
        moe.reshape(members, tok_rows, width),
        token_grad,
        grad_first[None, None],
        grad_second[None, None],
        router_grad,
    )


def solution(mesh):
    in_specs = (
        P(("dp", "member"), None),
        P(None, ("dp", "member"), None),
        P(),
        P("member", "dp", None, "expert"),
        P("member", "dp", "expert", None),
        P(None, ("dp", "member"), None),
    )
    out_specs = (
        P(None, ("dp", "member"), None),
        P(("dp", "member"), None),
        P("member", "dp", None, "expert"),
        P("member", "dp", "expert", None),
        P(),
    )
    return jax.shard_map(shards, mesh=mesh, in_specs=in_specs, out_specs=out_specs, check_vma=False)
```

time: 531 us -> 199 us (0.37)
  waiting for transfers between devices: 397 us -> 52.7 us
  blocking collectives: 42.7 us -> 91.8 us
  matrix products: 15.7 us -> 0 us
  between operations: 14.3 us -> 1.45 us
  Pallas kernels: 0 us -> 11.8 us
  local copies, waits for them, and re-layouts: 23.4 us -> 16 us
  starting transfers between devices: 30.7 us -> 24.3 us
    psum x2 -> x0, waiting for transfers between devices: 319 us -> none  [the longest x1 193 us: shards(): router_grad = lax.psum(router_local, ('dp', 'member'))]
    all_gather x0 -> x2, blocking collectives: none -> 51.2 us  [the longest x1 26 us: shards(): out_all = lax.all_gather(out_own, 'expert')]
    all_to_all x1 -> x0, blocking collectives: 42.7 us -> none  [send_back(): lax.all_to_all(first_rows.reshape(dp_count * member_count, capacity, row_...]
    unnamed x0 -> x1, blocking collectives: none -> 40.6 us
    all_to_all x3 -> x2, waiting for transfers between devices: 77.9 us -> 52.7 us  [the longest x1 45.9 us: shards(): lax.all_to_all(msg.reshape(places, 4 * capacity, half), plane, split_axis...]
    dot_general x9 -> x0, matrix products: 15.7 us -> none  [the longest x1 2.84 us: shards(): jnp.einsum('rd,rh->dh', x_rows, pre_grad, preferred_element_type=jnp.floa...]
    pallas_call x0 -> x6, Pallas kernels: none -> 11.8 us  [the longest x1 3.76 us: shards(): call(functools.partial(expert_kernel, stride), [((z_count * share, 128),...]
    unnamed x27 -> x30, local copies, waits for them, and re-layouts: 4.41 us -> 16 us
  transfers between devices with their start and end apart: 5 -> 3, of which waited for: 5 -> 2; matrix products, arithmetic and copies ran while one was open for 4% -> 1% of each run, Pallas kernels for 0% -> 1%
where the time goes in v1:
time: 199 us; the launch traced here: 198 us
  blocking collectives  91.8 us (46%)
  waiting for transfers between devices  52.7 us (26%)
  starting transfers between devices  24.3 us (12%)
  local copies, waits for them, and re-layouts  16 us (8%)
  Pallas kernels  11.8 us (6%)
    all_to_all x1, waiting for transfers between devices, shards(): lax.all_to_all(msg.reshape(places, 4 * capacity, half), plane, split_axis...  45.9 us
    unnamed x1, blocking collectives  40.6 us
    all_gather x1, blocking collectives, shards(): out_all = lax.all_gather(out_own, 'expert')  26 us
    all_gather x1, blocking collectives, shards(): rest_all = lax.all_gather(rest_own, 'expert')  25.2 us
    unnamed x30, local copies, waits for them, and re-layouts  16 us
    all_to_all x1, starting transfers between devices, shards(): lax.all_to_all(msg.reshape(places, 4 * capacity, half), plane, split_axis...  13.9 us
    all_to_all x1, starting transfers between devices, shards(): lax.all_to_all(back.reshape(places, 16, 128), plane, split_axis=0, concat...  8.11 us
    all_to_all x1, waiting for transfers between devices, shards(): lax.all_to_all(back.reshape(places, 16, 128), plane, split_axis=0, concat...  6.79 us
  transfers between devices with their start and end apart: 3, of which 2 were waited for; matrix products, arithmetic and copies ran while one was open for 1% of the time, Pallas kernels for 1%

profile of v1, /device:TPU:6, one launch (start us, length us, event | category | flops | bytes accessed | tf_op | source)
XLA Modules:
  0.0 198.0 jit_solution(273172332974677826)
XLA Ops:
  0.7 1.1 copy-done.6
  1.8 1.0 copy-done.7
  3.4 2.3 %dispatch.1 = (bf16[1536,640]{1,0:T(8,128)(2,1)S(1)}, s32[2,128]{1,0:T(2,128)S(1)}) custom-call(s32[2,128]{1,0:T(2,128)S(1)} %bitcast.28, bf16[128,1280]{1,0:T(8,128)(2,1)S(1)} %copy-done.7, bf16[2,128,1280]{2,1,0:T(8,128)(2,1)S(1)} %copy-done.6), custom_call_target="tpu_custom_call" | custom-call | flops 3221225472 | bytes 4194304 | tf_op jit(solution)/shard_map/dispatch/pallas_call | solution.py:225
  5.8 1.3 copy-done.3
  7.1 13.9 %all-to-all-start = ((bf16[64,24,640]{2,1,0:T(8,128)(2,1)}), bf16[64,24,640]{2,1,0:T(8,128)(2,1)S(1)}, u32[]{:S(2)}, u32[]{:S(2)}) async-start(bf16[64,24,640]{2,1,0:T(8,128)(2,1)} %bitcast.24), calls=%async_computation | async-start | bytes 3932160 | tf_op jit(solution)/shard_map/all_to_all | solution.py:230
  21.0 45.9 %all-to-all-done = bf16[64,24,640]{2,1,0:T(8,128)(2,1)S(1)} async-done(((bf16[64,24,640]{2,1,0:T(8,128)(2,1)}), bf16[64,24,640]{2,1,0:T(8,128)(2,1)S(1)}, u32[]{:S(2)}, u32[]{:S(2)}) %all-to-all-start) | async-done | bytes 1966112 | tf_op jit(solution)/shard_map/all_to_all | solution.py:230
  66.9 1.3 copy-done.1
  68.2 1.5 copy-done.2
  69.8 1.2 copy-done.4
  71.0 1.2 copy-done.5
  72.2 3.8 %expert.1 = (bf16[9396,128]{1,0:T(8,128)(2,1)S(1)}, bf16[384,1280]{1,0:T(8,128)(2,1)S(1)}, bf16[384,1280]{1,0:T(8,128)(2,1)S(1)}, bf16[384,384]{1,0:T(8,128)(2,1)S(1)}, bf16[384,384]{1,0:T(8,128)(2,1)S(1)}) custom-call(bf16[1536,640]{1,0:T(8,128)(2,1)S(1)} %bitcast.23, bf16[1280,384]{1,0:T(8,128)(2,1)S(1)} %bitcast.26, bf16[384,1280]{1,0:T(8,128)(2,1)S(1)} %bitcast.27, ...), custom_call_target="tpu_custom_call" | custom-call | flops 3221225472 | bytes 12582912 | tf_op jit(solution)/shard_map/expert/pallas_call | solution.py:238
  77.8 40.6 %fusion = bf16[784,128]{1,0:T(8,128)(2,1)S(1)} fusion(bf16[9396,128]{1,0:T(8,128)(2,1)S(1)} %get-tuple-element.21), kind=kCustom, calls=%all-reduce-scatter | all-reduce-scatter fusion | flops 1204225 | bytes 2610176
  118.5 2.3 %collective-permute-start = (bf16[11,128]{1,0:T(8,128)(2,1)S(1)}, bf16[11,128]{1,0:T(8,128)(2,1)S(1)}, u32[]{:S(2)}, u32[]{:S(2)}) collective-permute-start(bf16[11,128]{1,0:T(8,128)(2,1)S(1)} %slice), channel_id=1, source_target_pairs={{0,1},{1,2},{2,3},{3,4},{4,5},{5,6},{6,7},{7,8},{8,9},{9,10},{10,1... | collective-permute-start | bytes 8456
  120.8 1.3 dynamic-slice.4
  122.7 1.0 concatenate
  123.8 1.4 to_tokens.1
  125.3 8.1 %all-to-all-start.1 = ((bf16[64,16,128]{2,1,0:T(8,128)(2,1)}), bf16[64,16,128]{2,1,0:T(8,128)(2,1)S(1)}, u32[]{:S(2)}, u32[]{:S(2)}) async-start(bf16[64,16,128]{2,1,0:T(8,128)(2,1)} %bitcast.8), calls=%async_computation.1 | async-start | bytes 524288 | tf_op jit(solution)/shard_map/all_to_all | solution.py:257
  133.4 1.2 copy-done.10
  134.6 1.2 copy-done.12
  135.8 2.4 %weights.1 = (bf16[1280,384]{1,0:T(8,128)(2,1)}, bf16[384,1280]{1,0:T(8,128)(2,1)}) custom-call(bf16[384,1280]{1,0:T(8,128)(2,1)S(1)} %copy-done.10, bf16[384,1280]{1,0:T(8,128)(2,1)S(1)} %copy-done.12, bf16[384,384]{1,0:T(8,128)(2,1)S(1)} %get-tuple-element.28.pre_ref, bf16[384,384]{1,0:T(8,128)(2,1)S(1)} %get-tuple-element.29.act_ref), custom_call_target="tpu_custom_call" | custom-call | flops 1073741824 | bytes 6291456 | tf_op jit(solution)/shard_map/weights/pallas_call | solution.py:260
  138.1 6.8 %all-to-all-done.1 = bf16[64,16,128]{2,1,0:T(8,128)(2,1)S(1)} async-done(((bf16[64,16,128]{2,1,0:T(8,128)(2,1)}), bf16[64,16,128]{2,1,0:T(8,128)(2,1)S(1)}, u32[]{:S(2)}, u32[]{:S(2)}) %all-to-all-start.1) | async-done | bytes 262176 | tf_op jit(solution)/shard_map/all_to_all | solution.py:257
  145.6 26.0 %all-gather = bf16[3072,128]{1,0:T(8,128)(2,1)S(1)} all-gather(bf16[256,128]{1,0:T(8,128)(2,1)S(1)} %get-tuple-element.22), channel_id=2, replica_groups=mesh['dp'=32,'member'=2,'expert'=12] {'expert'}, dimensions={0}, use_global_device_ids=true | all-gather | bytes 851968 | tf_op jit(solution)/shard_map/all_gather | solution.py:270
  171.6 25.2 %all-gather.1 = bf16[2304,128]{1,0:T(8,128)(2,1)S(1)} all-gather(bf16[192,128]{1,0:T(8,128)(2,1)S(1)} %get-tuple-element.23), channel_id=3, replica_groups=mesh['dp'=32,'member'=2,'expert'=12] {'expert'}, dimensions={0}, use_global_device_ids=true | all-gather | bytes 638976 | tf_op jit(solution)/shard_map/all_gather | solution.py:271
  196.7 1.3 final.1
  (22 shorter events, 3.3 us)
Async XLA Ops:
  0.6 20.4 %copy-start = (f32[2,1280,32]{1,2,0:T(8,128)S(1)}, f32[2,1280,32]{1,2,0:T(8,128)}, u32[]{:S(2)}) copy-start(f32[2,1280,32]{1,2,0:T(8,128)} %param.8) | copy-start | bytes 983044
  0.6 1.1 copy-start.6
  1.8 1.0 copy-start.7
  2.8 0.7 copy-start.8
  5.8 1.3 copy-start.3
  7.1 59.9 %all-to-all-start = ((bf16[64,24,640]{2,1,0:T(8,128)(2,1)}), bf16[64,24,640]{2,1,0:T(8,128)(2,1)S(1)}, u32[]{:S(2)}, u32[]{:S(2)}) async-start(bf16[64,24,640]{2,1,0:T(8,128)(2,1)} %bitcast.24), calls=%async_computation | async-start | bytes 3932160 | tf_op jit(solution)/shard_map/all_to_all | solution.py:230
  66.9 1.3 copy-start.1
  68.2 1.5 copy-start.2
  69.8 1.2 copy-start.4
  71.0 1.2 copy-start.5
  75.9 0.9 copy-start.9
  76.9 0.9 copy-start.11
  118.5 4.2 %collective-permute-start = (bf16[11,128]{1,0:T(8,128)(2,1)S(1)}, bf16[11,128]{1,0:T(8,128)(2,1)S(1)}, u32[]{:S(2)}, u32[]{:S(2)}) collective-permute-start(bf16[11,128]{1,0:T(8,128)(2,1)S(1)} %slice), channel_id=1, source_target_pairs={{0,1},{1,2},{2,3},{3,4},{4,5},{5,6},{6,7},{7,8},{8,9},{9,10},{10,1... | collective-permute-start | bytes 8456
  125.3 19.7 %all-to-all-start.1 = ((bf16[64,16,128]{2,1,0:T(8,128)(2,1)}), bf16[64,16,128]{2,1,0:T(8,128)(2,1)S(1)}, u32[]{:S(2)}, u32[]{:S(2)}) async-start(bf16[64,16,128]{2,1,0:T(8,128)(2,1)} %bitcast.8), calls=%async_computation.1 | async-start | bytes 524288 | tf_op jit(solution)/shard_map/all_to_all | solution.py:257
  133.4 1.2 copy-start.10
  134.6 1.2 copy-start.12

commit v2 on v1

v2 whole, which is shorter than its diff:
```python
import functools

import jax
import jax.numpy as jnp
from jax import lax
from jax.experimental import pallas as pl
from jax.experimental.pallas import tpu as pltpu
from jax.sharding import PartitionSpec as P

BF = jnp.bfloat16
F32 = jnp.float32
tanh_scale = 0.7978845608028654
cubic_term = 0.044715
LIMIT = 44 << 20
FULL = 60 << 20
MOST = 52 << 20
LESS = 24 << 20
PARTS = 3
VM = pl.BlockSpec(memory_space=pltpu.VMEM)
HB = pl.BlockSpec(memory_space=pltpu.HBM)
SM = pl.BlockSpec(memory_space=pltpu.SMEM)


def iota(shape, axis):
    return lax.broadcasted_iota(jnp.int32, shape, axis)


def one(mask):
    return jnp.where(mask, 1.0, 0.0).astype(BF)


def to_column(row):
    n = row.shape[1]
    eye = iota((n, n), 0) == iota((n, n), 1)
    return jnp.sum(jnp.where(eye, row, 0), axis=1, keepdims=True)


def dispatch_kernel(
    part_ref, ids_hbm, tok_hbm, grad_hbm, msg_hbm, code_ref, ids_ref, tok_ref, grad_ref, msg_ref, sem, out_sem
):
    loads = [
        pltpu.make_async_copy(src, dst, sem.at[k])
        for k, (src, dst) in enumerate(
            ((ids_hbm, ids_ref), (tok_hbm, tok_ref), (grad_hbm, grad_ref))
        )
    ]
    for load in loads:
        load.start()
    tok_rows, width = tok_ref.shape
    half = width // 2
    loads[0].wait()
    codes = []
    for m in range(2):
        ids = ids_ref[m : m + 1, :]
        same = to_column(ids) == ids
        earlier = iota((tok_rows, tok_rows), 0) < iota((tok_rows, tok_rows), 1)
        slot = jnp.sum(jnp.where(same & earlier, 1, 0), axis=0, keepdims=True)
        code = ids * 8 + slot
        code_ref[m : m + 1, :] = code
        codes.append(code)
    loads[1].wait()
    loads[2].wait()
    sides = [
        jnp.concatenate([v[:, :half], v[:, half:]], axis=0)
        for v in (tok_ref[...], grad_ref[0], grad_ref[1])
    ]
    block = 256
    stores = []
    for b in range(msg_ref.shape[0] // block):
        row = iota((block, tok_rows), 0) + b * block
        dest = lax.shift_right_logical(row, 3)
        slot = 2 * part_ref[0] + (row & 1)
        kind = lax.shift_right_logical(row & 7, 1)
        code = lax.shift_right_logical(dest, 1) * 8 + slot
        member = dest & 1
        hit0 = (code == codes[0]) & (member == 0)
        hit1 = (code == codes[1]) & (member == 1)
        hit = hit0 | hit1
        parts = (
            [hit & (kind == 0), hit & (kind == 1)],
            [hit0 & (kind == 2), hit0 & (kind == 3)],
            [hit1 & (kind == 2), hit1 & (kind == 3)],
        )
        total = None
        for pair, side in zip(parts, sides):
            pick = jnp.concatenate([one(p) for p in pair], axis=1)
            term = jnp.dot(pick, side, preferred_element_type=F32)
            total = term if total is None else total + term
        here = pl.ds(b * block, block)
        msg_ref[here, :] = total.astype(BF)
        store = pltpu.make_async_copy(msg_ref.at[here], msg_hbm.at[here], out_sem.at[b])
        store.start()
        stores.append(store)
    for store in stores:
        store.wait()


def nt(a, b):
    return lax.dot_general(a, b, (((1,), (1,)), ((), ())), preferred_element_type=F32)


def tn(a, b):
    return lax.dot_general(a, b, (((0,), (0,)), ((), ())), preferred_element_type=F32)


def sorting():
    p = iota((256, 256), 0)
    source = (
        lax.shift_right_logical(p & 63, 1) * 8 + lax.shift_right_logical(p, 6) * 2 + (p & 1)
    )
    return one(source == iota((256, 256), 1))


def unpack(sort, msg_ref, k, x_ref, g_ref):
    half = msg_ref.shape[1]
    width = 2 * half
    part = jnp.dot(sort, msg_ref[pl.ds(k * 256, 256), :], preferred_element_type=F32).astype(BF)
    here = pl.ds(k * 64, 64)
    x_ref[here, 0:half] = part[0:64]
    x_ref[here, half:width] = part[64:128]
    g_ref[here, 0:half] = part[128:192]
    g_ref[here, half:width] = part[192:256]


def fetch(sources, msg_ref, sem):
    copies = []
    for n, source in enumerate(sources):
        for k in range(2):
            index = 2 * n + k
            copies.append(
                pltpu.make_async_copy(
                    source.at[pl.ds(k * 256, 256)],
                    msg_ref.at[pl.ds(index * 256, 256)],
                    sem.at[index],
                )
            )
    return copies


def wrap(part):
    return jnp.where(part >= PARTS, part - PARTS, part)


def expert_kernel(
    stride, part_index_ref, own_hbm, up_hbm, down_hbm, first_hbm, second_hbm, router_ref, part_ref, pre_ref, act_ref,
    msg_ref, first_ref, second_ref, x_ref, g_ref, sem, weight_sem,
):
    loads = fetch((own_hbm, up_hbm, down_hbm), msg_ref, sem)
    weights = [
        pltpu.make_async_copy(first_hbm, first_ref, weight_sem.at[0]),
        pltpu.make_async_copy(second_hbm, second_ref, weight_sem.at[1]),
    ]
    for copy in loads[:2] + weights + loads[2:]:
        copy.start()
    rows, width = x_ref.shape
    chunks = width // 128
    router = router_ref[...]
    sort = sorting()
    router_sum = jnp.zeros((1, width), F32)
    block = 128
    left = part_ref.shape[0] - chunks * stride
    part_ref[pl.ds(chunks * stride, left), :] = jnp.zeros((left, 128), BF)
    for b in range(rows // block):
        for k in range(2 * b, 2 * b + 2):
            loads[k].wait()
            unpack(sort, msg_ref, k, x_ref, g_ref)
        if b == 0:
            for copy in weights:
                copy.wait()
            first = first_ref[...]
            second = second_ref[...]
        here = pl.ds(b * block, block)
        x = x_ref[here, :]
        g = g_ref[here, :]
        xf = x.astype(F32)
        logit = jnp.sum(xf * router, axis=1, keepdims=True)
        gate = 1.0 / (1.0 + jnp.exp(-logit))
        pre = jnp.dot(x, first, preferred_element_type=F32)
        hidden = nt(g, second)
        tanh_value = jnp.tanh(tanh_scale * (pre + cubic_term * pre * pre * pre))
        act = 0.5 * pre * (1.0 + tanh_value)
        slope = 0.5 * (1.0 + tanh_value) + 0.5 * pre * (
            1.0 - tanh_value * tanh_value
        ) * tanh_scale * (1.0 + 3.0 * cubic_term * pre * pre)
        gate_grad = jnp.sum(act * hidden, axis=1, keepdims=True)
        logit_grad = gate_grad * gate * (1.0 - gate)
        pre_grad = (hidden * gate * slope).astype(BF)
        scaled_act = (act * gate).astype(BF)
        pre_ref[here, :] = pre_grad
        act_ref[here, :] = scaled_act
        router_sum = router_sum + jnp.sum(xf * logit_grad, axis=0, keepdims=True)
        place = wrap(part_index_ref[0] + (0, 2, 1)[b]) * block
        out = jnp.dot(scaled_act, second, preferred_element_type=F32).astype(BF)
        dx = (nt(pre_grad, first) + logit_grad * router).astype(BF)
        for c in range(chunks):
            lanes = slice(c * 128, (c + 1) * 128)
            at_out = pl.multiple_of(place + c * stride, 16)
            at_dx = pl.multiple_of(place + c * stride + rows, 16)
            part_ref[pl.ds(at_out, block), :] = out[:, lanes]
            part_ref[pl.ds(at_dx, block), :] = dx[:, lanes]
    for c in range(chunks):
        lanes = slice(c * 128, (c + 1) * 128)
        tail = jnp.where(iota((16, 128), 0) == 0, router_sum[:, lanes], 0.0)
        part_ref[pl.ds(c * stride + 2 * rows, 16), :] = tail.astype(BF)


def weight_kernel(
    own_hbm, up_hbm, down_hbm, pre_ref, act_ref, first_ref, second_ref, msg_ref, x_ref, g_ref, sem
):
    loads = fetch((own_hbm, up_hbm, down_hbm), msg_ref, sem)
    for load in loads:
        load.start()
    sort = sorting()
    for k, load in enumerate(loads):
        load.wait()
        unpack(sort, msg_ref, k, x_ref, g_ref)
    first_ref[...] = tn(x_ref[...], pre_ref[...]).astype(BF)
    second_ref[...] = tn(act_ref[...], g_ref[...]).astype(BF)


def return_kernel(rows, shift_ref, sum_ref, msg_ref, hold_ref):
    depth = hold_ref.shape[0]
    given = sum_ref.shape[0]
    base = given // 16 * 16
    hold_ref[pl.ds(base, depth - base), :] = jnp.zeros((depth - base, 128), BF)
    hold_ref[pl.ds(0, given), :] = sum_ref[...]
    shift = shift_ref[0]
    held = hold_ref[...]
    block = 256
    for b in range(msg_ref.shape[0] // block):
        row = iota((block, depth), 0) + b * block
        source = lax.shift_right_logical(row, 4)
        r = row & 15
        slot = jnp.where(r < 6, r, r - 6)
        want = lax.shift_right_logical(slot, 1) * (rows // PARTS) + source * 2 + (slot & 1)
        want = jnp.where(r < 6, want, rows + want)
        want = jnp.where(r < 12, want, jnp.where(r == 12, 2 * rows, -depth)) + shift
        msg_ref[pl.ds(b * block, block), :] = jnp.dot(
            one(want == iota((block, depth), 1)), held, preferred_element_type=F32
        ).astype(BF)


def collect_kernel(code_ref, msg_ref, out_ref):
    held = msg_ref[...]
    depth = held.shape[0]
    tok_rows = code_ref.shape[1]
    picked = None
    for m in range(2):
        code = to_column(code_ref[m : m + 1, :])
        want = (lax.shift_right_logical(code, 3) * 2 + m) * 16 + (code & 7)
        lane = iota((tok_rows, depth), 1)
        out_ref[pl.ds(m * tok_rows, tok_rows), :] = jnp.dot(
            one(lane == want), held, preferred_element_type=F32
        ).astype(BF)
        pick = one(lane == want + 6)
        picked = pick if picked is None else picked + pick
    out_ref[pl.ds(2 * tok_rows, tok_rows), :] = jnp.dot(picked, held, preferred_element_type=F32).astype(BF)
    n = depth // 16
    row = iota((n, depth), 0)
    want = ((row & (n // 2 - 1)) * 2 + jnp.where(row >= n // 2, 1, 0)) * 16 + 12
    out_ref[pl.ds(3 * tok_rows, n), :] = jnp.dot(
        one(iota((n, depth), 1) == want), held, preferred_element_type=F32
    ).astype(BF)


def final_kernel(part_ref, own_ref, up_ref, down_ref, moe_ref, token_ref, router_ref):
    tok_rows, width = token_ref.shape
    for ref, shift in ((own_ref, 0), (up_ref, 2), (down_ref, 1)):
        part = wrap(part_ref[0] + shift)
        for k in range(ref.shape[0]):

            @pl.when(part + PARTS * k < width // 128)
            def _():
                lanes = pl.ds(pl.multiple_of((part + PARTS * k) * 128, 128), 128)
                moe_ref[:, lanes] = ref[k, 0 : 2 * tok_rows, :]
                token_ref[:, lanes] = ref[k, 2 * tok_rows : 3 * tok_rows, :].astype(F32)
                router_ref[:, lanes] = ref[k, 3 * tok_rows :, :].astype(F32)


def call(kernel, out, specs, name, flops, size, scratch=(), out_specs=None, limit=FULL):
    return pl.pallas_call(
        kernel,
        out_shape=[jax.ShapeDtypeStruct(s, d) for s, d in out],
        in_specs=specs,
        out_specs=out_specs or [VM] * len(out),
        scratch_shapes=list(scratch),
        compiler_params=pltpu.CompilerParams(vmem_limit_bytes=limit),
        cost_estimate=pl.CostEstimate(flops=flops, bytes_accessed=size, transcendentals=0),
        name=name,
    )


def shards(tokens, route_ids, router, w_in, w_out, out_grad):
    members, tok_rows = route_ids.shape[0], route_ids.shape[1]
    experts, width = router.shape[2], router.shape[1]
    hidden = w_in.shape[3]
    places = experts * members
    capacity = 3 * tok_rows // (2 * experts)
    rows = places * capacity
    half = width // 2
    plane = ("dp", "member")
    z_count = lax.axis_size("expert")
    z = lax.axis_index("expert")
    part_index = (z % PARTS).reshape(1)
    ahead = [(k, (k + 1) % z_count) for k in range(z_count)]
    behind = [(k, (k - 1) % z_count) for k in range(z_count)]
    lines = [list(range(k, z_count, PARTS)) for k in range(PARTS)]

    dma = pltpu.SemaphoreType.DMA
    count = rows * 4 // 256
    msg, codes = call(
        dispatch_kernel,
        [((places * 8, half), BF), ((members, tok_rows), jnp.int32)],
        [SM] + [HB] * 3, "dispatch", 3 << 30, 4 << 20,
        scratch=[
            pltpu.VMEM((members, tok_rows), jnp.int32),
            pltpu.VMEM((tok_rows, width), BF),
            pltpu.VMEM((members, tok_rows, width), BF),
            pltpu.VMEM((places * 8, half), BF),
            dma((3,)),
            dma((places * 8 // 256,)),
        ],
        out_specs=[HB, VM],
    )(part_index, route_ids[:, :, 0], tokens, out_grad)
    own = lax.all_to_all(
        msg.reshape(places, 8, half), plane, split_axis=0, concat_axis=0, tiled=True
    ).reshape(places * 8, half)
    arrived = (own, lax.ppermute(own, "expert", ahead), lax.ppermute(own, "expert", behind))
    column = lax.dynamic_slice(
        router, (lax.axis_index("member"), 0, lax.axis_index("dp")), (1, width, 1)
    ).reshape(1, width)
    stride = 2 * rows + 16
    share = stride - 1
    sides = [pltpu.VMEM((rows * 4, half), BF)]
    pair = [pltpu.VMEM((rows, width), BF)] * 2
    part, pre_grad, scaled_act = call(
        functools.partial(expert_kernel, stride),
        [((z_count * share, 128), BF), ((rows, hidden), BF), ((rows, hidden), BF)],
        [SM] + [HB] * 5 + [VM], "expert", 3 << 30, 8 << 20, limit=MOST,
        scratch=sides
        + [pltpu.VMEM((width, hidden), BF), pltpu.VMEM((hidden, width), BF)]
        + pair
        + [dma((count,)), dma((2,))],
    )(part_index, *arrived, w_in[0, 0], w_out[0, 0], column)
    total = lax.psum_scatter(part, "expert", scatter_dimension=0, tiled=True)
    (back,) = call(
        functools.partial(return_kernel, rows),
        [((places * 16, 128), BF)],
        [SM, VM], "to_tokens", 1 << 28, 1 << 20,
        scratch=[pltpu.VMEM((-(-share // 128) * 128, 128), BF)],
        limit=LIMIT,
    )(z.reshape(1), total)
    home = lax.all_to_all(
        back.reshape(places, 16, 128), plane, split_axis=0, concat_axis=0, tiled=True
    ).reshape(places * 16, 128)
    grad_first, grad_second = call(
        weight_kernel,
        [((width, hidden), BF), ((hidden, width), BF)],
        [HB] * 3 + [VM] * 2, "weights", 1 << 30, 6 << 20, limit=LESS,
        scratch=sides + pair + [dma((count,))],
    )(*arrived, pre_grad, scaled_act)
    (compact,) = call(
        collect_kernel,
        [(((members + 1) * tok_rows + places, 128), BF)],
        [VM] * 2, "collect", 1 << 28, 1 << 20, limit=LIMIT,
    )(codes, home)
    line = lax.all_gather(compact, "expert", axis_index_groups=lines)
    moe, token_grad, router_rows = call(
        final_kernel,
        [((members * tok_rows, width), BF), ((tok_rows, width), F32), ((places, width), F32)],
        [SM] + [VM] * 3, "final", 1 << 20, 4 << 20, limit=LIMIT,
    )(
        part_index,
        line,
        lax.ppermute(line, "expert", ahead),
        lax.ppermute(line, "expert", behind),
    )
    router_grad = jnp.transpose(router_rows.reshape(members, experts, width), (0, 2, 1))
    return (
        moe.reshape(members, tok_rows, width),
        token_grad,
        grad_first[None, None],
        grad_second[None, None],
        router_grad,
    )


def solution(mesh):
    in_specs = (
        P(("dp", "member"), None),
        P(None, ("dp", "member"), None),
        P(),
        P("member", "dp", None, "expert"),
        P("member", "dp", "expert", None),
        P(None, ("dp", "member"), None),
    )
    out_specs = (
        P(None, ("dp", "member"), None),
        P(("dp", "member"), None),
        P("member", "dp", None, "expert"),
        P("member", "dp", "expert", None),
        P(),
    )
    return jax.shard_map(shards, mesh=mesh, in_specs=in_specs, out_specs=out_specs, check_vma=False)
```

time: 199 us -> 172 us (0.86)
  waiting for transfers between devices: 52.7 us -> 24.4 us
  local copies, waits for them, and re-layouts: 16 us -> 2.42 us
  blocking collectives: 91.8 us -> 102 us
  Pallas kernels: 11.8 us -> 18.2 us
    all_to_all x2 -> x0, waiting for transfers between devices: 52.7 us -> none  [the longest x1 45.9 us: shards(): lax.all_to_all(msg.reshape(places, 4 * capacity, half), plane, split_axis...]
    all_to_all x0 -> x2, blocking collectives: none -> 50.1 us  [the longest x1 33.2 us: shards(): lax.all_to_all(msg.reshape(places, 8, half), plane, split_axis=0, concat_...]
    all_gather x2 -> x1, blocking collectives: 51.2 us -> 19.2 us  [shards(): line = lax.all_gather(compact, 'expert', axis_index_groups=lines)]
    ppermute x0 -> x4, waiting for transfers between devices: none -> 24.4 us  [the longest x1 13 us: shards(): lax.ppermute(own, 'expert', behind)]
    all_to_all x2 -> x0, starting transfers between devices: 22 us -> none  [the longest x1 13.9 us: shards(): lax.all_to_all(msg.reshape(places, 4 * capacity, half), plane, split_axis...]
    ppermute x0 -> x4, starting transfers between devices: none -> 20.1 us  [the longest x1 11.4 us: shards(): lax.ppermute(own, 'expert', behind)]
    unnamed x30 -> x12, local copies, waits for them, and re-layouts: 16 us -> 2.41 us
    unnamed x1, blocking collectives: 40.6 us -> 32.8 us
  transfers between devices with their start and end apart: 3 -> 5, of which waited for: 2 -> 4; matrix products, arithmetic and copies ran while one was open for 1% -> 1% of each run, Pallas kernels for 1% -> 3%
where the time goes in v2:
time: 172 us
  blocking collectives  102 us (59%)
  waiting for transfers between devices  24.4 us (14%)
  starting transfers between devices  23.3 us (14%)
  Pallas kernels  18.2 us (11%)
  local copies, waits for them, and re-layouts  2.42 us (1%)
    all_to_all x1, blocking collectives, shards(): lax.all_to_all(msg.reshape(places, 8, half), plane, split_axis=0, concat_...  33.2 us
    unnamed x1, blocking collectives  32.8 us
    all_gather x1, blocking collectives, shards(): line = lax.all_gather(compact, 'expert', axis_index_groups=lines)  19.2 us
    all_to_all x1, blocking collectives, shards(): lax.all_to_all(back.reshape(places, 16, 128), plane, split_axis=0, concat...  16.9 us
    ppermute x1, waiting for transfers between devices, shards(): lax.ppermute(own, 'expert', behind)  13 us
    ppermute x1, starting transfers between devices, shards(): lax.ppermute(own, 'expert', behind)  11.4 us
    pallas_call x1, Pallas kernels, shards(): call(functools.partial(expert_kernel, stride), [((z_count * share, 128),...  7.4 us
    ppermute x1, waiting for transfers between devices, shards(): lax.ppermute(own, 'expert', ahead)  5.33 us
  transfers between devices with their start and end apart: 5, of which 4 were waited for; matrix products, arithmetic and copies ran while one was open for 1% of the time, Pallas kernels for 3%

profile of v2, /device:TPU:6, one launch (start us, length us, event | category | flops | bytes accessed | tf_op | source)
XLA Modules:
  0.0 171.9 jit_solution(504408704589570748)
XLA Ops:
  0.6 0.0 copy-start
  0.7 3.4 %dispatch.1 = (bf16[512,640]{1,0:T(8,128)(2,1)}, s32[2,128]{1,0:T(2,128)}) custom-call(s32[1]{0:T(128)} %bitcast.part_ref.part_index_ref, s32[2,128]{1,0:T(2,128)} %bitcast.35, bf16[128,1280]{1,0:T(8,128)(2,1)} %tok_hbm.1, bf16[2,128,1280]{2,1,0:T(8,128)(2,1)} %grad_hbm.1), custom_call_target="tpu_custom_call" | custom-call | flops 3221225472 | bytes 4194304 | tf_op jit(solution)/shard_map/dispatch/pallas_call | solution.py:311
  4.1 33.2 %all_to_all.10 = bf16[64,8,640]{2,1,0:T(8,128)(2,1)S(1)} all-to-all(bf16[64,8,640]{2,1,0:T(8,128)(2,1)} %bitcast.30), channel_id=1, replica_groups=mesh['dp'=32,'member'=2,'expert'=12] {'dp','member'}, dimensions={0} | all-to-all | bytes 1310720 | tf_op jit(solution)/shard_map/all_to_all | solution.py:325
  37.3 11.4 %collective-permute-start.1 = (bf16[512,640]{1,0:T(8,128)(2,1)S(1)}, bf16[512,640]{1,0:T(8,128)(2,1)S(1)}, u32[]{:S(2)}, u32[]{:S(2)}) collective-permute-start(bf16[512,640]{1,0:T(8,128)(2,1)S(1)} %bitcast.24), channel_id=1, source_target_pairs={{0,11},{1,0},{2,1},{3,2},{4,3},{5,4},{6,5},{7,6},{8,7},{9,8},{10,9... | collective-permute-start | bytes 1966088 | tf_op jit(solution)/shard_map/ppermute | solution.py:328
  48.7 1.9 %collective-permute-start = (bf16[512,640]{1,0:T(8,128)(2,1)S(1)}, bf16[512,640]{1,0:T(8,128)(2,1)S(1)}, u32[]{:S(2)}, u32[]{:S(2)}) collective-permute-start(bf16[512,640]{1,0:T(8,128)(2,1)S(1)} %bitcast.25), channel_id=1, source_target_pairs={{0,1},{1,2},{2,3},{3,4},{4,5},{5,6},{6,7},{7,8},{8,9},{9,10},{10,1... | collective-permute-start | bytes 1966088 | tf_op jit(solution)/shard_map/ppermute | solution.py:328
  50.7 13.0 %collective-permute-done.1.down_hbm = bf16[512,640]{1,0:T(8,128)(2,1)S(1)} collective-permute-done((bf16[512,640]{1,0:T(8,128)(2,1)S(1)}, bf16[512,640]{1,0:T(8,128)(2,1)S(1)}, u32[]{:S(2)}, u32[]{:S(2)}) %collective-permute-start.1) | collective-permute-done | bytes 655392 | tf_op jit(solution)/shard_map/ppermute | solution.py:328
  63.7 5.3 %collective-permute-done.up_hbm = bf16[512,640]{1,0:T(8,128)(2,1)S(1)} collective-permute-done((bf16[512,640]{1,0:T(8,128)(2,1)S(1)}, bf16[512,640]{1,0:T(8,128)(2,1)S(1)}, u32[]{:S(2)}, u32[]{:S(2)}) %collective-permute-start) | collective-permute-done | bytes 655392 | tf_op jit(solution)/shard_map/ppermute | solution.py:328
  69.1 7.4 %expert.1 = (bf16[9396,128]{1,0:T(8,128)(2,1)}, bf16[384,384]{1,0:T(8,128)(2,1)S(1)}, bf16[384,384]{1,0:T(8,128)(2,1)S(1)}) custom-call(s32[1]{0:T(128)} %bitcast.part_ref.part_index_ref, bf16[512,640]{1,0:T(8,128)(2,1)S(1)} %bitcast.26, bf16[512,640]{1,0:T(8,128)(2,1)S(1)} %collective-permute-done.up_hbm, bf16[512,640]{1,0:T(8,128)(2,1)} %copy-done.1, ...), custom_call_target="tpu_custom_call" | custom-call | flops 3221225472 | bytes 8388608 | tf_op jit(solution)/shard_map/expert/pallas_call | solution.py:336
  76.5 32.8 %fusion = bf16[784,128]{1,0:T(8,128)(2,1)S(1)} fusion(bf16[9396,128]{1,0:T(8,128)(2,1)} %get-tuple-element.17), kind=kCustom, calls=%all-reduce-scatter | all-reduce-scatter fusion | flops 1204225 | bytes 2610176
  109.3 0.0 copy-start.2
  109.3 3.2 %collective-permute-start.4 = (bf16[11,128]{1,0:T(8,128)(2,1)S(1)}, bf16[11,128]{1,0:T(8,128)(2,1)S(1)}, u32[]{:S(2)}, u32[]{:S(2)}) collective-permute-start(bf16[11,128]{1,0:T(8,128)(2,1)S(1)} %slice), channel_id=1, source_target_pairs={{0,1},{1,2},{2,3},{3,4},{4,5},{5,6},{6,7},{7,8},{8,9},{9,10},{10,1... | collective-permute-start | bytes 8456
  112.5 1.3 dynamic-slice.4
  114.5 1.0 concatenate
  115.5 0.1 constant_dynamic-slice_fusion.sum_ref
  115.6 0.8 to_tokens.1
  116.4 16.9 %all_to_all.11 = bf16[64,16,128]{2,1,0:T(8,128)(2,1)S(1)} all-to-all(bf16[64,16,128]{2,1,0:T(8,128)(2,1)S(1)} %bitcast.29), channel_id=1, replica_groups=mesh['dp'=32,'member'=2,'expert'=12] {'dp','member'}, dimensions={0} | all-to-all | bytes 524288 | tf_op jit(solution)/shard_map/all_to_all | solution.py:353
  133.3 0.6 collect.1
  133.9 19.2 %all-gather = bf16[1792,128]{1,0:T(8,128)(2,1)S(1)} all-gather(bf16[448,128]{1,0:T(8,128)(2,1)S(1)} %collect.1), channel_id=2, replica_groups={{0,3,6,9},{1,4,7,10},{2,5,8,11},{12,15,18,21},{13,16,19,22},{14,17,20,2..., dimensions={0}, use_global_device_ids=true | all-gather | bytes 573440 | tf_op jit(solution)/shard_map/all_gather | solution.py:367
  153.1 3.0 %collective-permute-start.3 = (bf16[4,448,128]{2,1,0:T(8,128)(2,1)S(1)}, bf16[4,448,128]{2,1,0:T(8,128)(2,1)S(1)}, u32[]{:S(2)}, u32[]{:S(2)}) collective-permute-start(bf16[4,448,128]{2,1,0:T(8,128)(2,1)S(1)} %bitcast.21), channel_id=1, source_target_pairs={{0,11},{1,0},{2,1},{3,2},{4,3},{5,4},{6,5},{7,6},{8,7},{9,8},{10,9... | collective-permute-start | bytes 1376264 | tf_op jit(solution)/shard_map/ppermute | solution.py:376
  156.1 3.7 %collective-permute-start.2 = (bf16[4,448,128]{2,1,0:T(8,128)(2,1)S(1)}, bf16[4,448,128]{2,1,0:T(8,128)(2,1)S(1)}, u32[]{:S(2)}, u32[]{:S(2)}) collective-permute-start(bf16[4,448,128]{2,1,0:T(8,128)(2,1)S(1)} %bitcast.22), channel_id=1, source_target_pairs={{0,1},{1,2},{2,3},{3,4},{4,5},{5,6},{6,7},{7,8},{8,9},{9,10},{10,1... | collective-permute-start | bytes 1376264 | tf_op jit(solution)/shard_map/ppermute | solution.py:375
  159.8 4.6 %weights.1 = (bf16[1280,384]{1,0:T(8,128)(2,1)}, bf16[384,1280]{1,0:T(8,128)(2,1)}) custom-call(bf16[512,640]{1,0:T(8,128)(2,1)S(1)} %bitcast.27, bf16[512,640]{1,0:T(8,128)(2,1)S(1)} %collective-permute-done.up_hbm, bf16[512,640]{1,0:T(8,128)(2,1)S(1)} %copy-done.2, bf16[384,384]{1,0:T(8,128)(2,1)S(1)} %get-tuple-element.20.pre_ref, ...), custom_call_target="tpu_custom_call" | custom-call | flops 1073741824 | bytes 6291456 | tf_op jit(solution)/shard_map/weights/pallas_call | solution.py:356
  164.5 3.8 %collective-permute-done.3.down_ref = bf16[4,448,128]{2,1,0:T(8,128)(2,1)S(1)} collective-permute-done((bf16[4,448,128]{2,1,0:T(8,128)(2,1)S(1)}, bf16[4,448,128]{2,1,0:T(8,128)(2,1)S(1)}, u32[]{:S(2)}, u32[]{:S(2)}) %collective-permute-start.3) | collective-permute-done | bytes 458784 | tf_op jit(solution)/shard_map/ppermute | solution.py:376
  168.3 2.2 %collective-permute-done.2.up_ref = bf16[4,448,128]{2,1,0:T(8,128)(2,1)S(1)} collective-permute-done((bf16[4,448,128]{2,1,0:T(8,128)(2,1)S(1)}, bf16[4,448,128]{2,1,0:T(8,128)(2,1)S(1)}, u32[]{:S(2)}, u32[]{:S(2)}) %collective-permute-start.2) | collective-permute-done | bytes 458784 | tf_op jit(solution)/shard_map/ppermute | solution.py:375
  170.5 1.4 final.1
  (9 shorter events, 0.0 us)
Async XLA Ops:
  0.6 50.0 %copy-start = (f32[2,1280,32]{1,2,0:T(8,128)S(1)}, f32[2,1280,32]{1,2,0:T(8,128)}, u32[]{:S(2)}) copy-start(f32[2,1280,32]{1,2,0:T(8,128)} %param.8) | copy-start | bytes 983044
  37.3 26.4 %collective-permute-start.1 = (bf16[512,640]{1,0:T(8,128)(2,1)S(1)}, bf16[512,640]{1,0:T(8,128)(2,1)S(1)}, u32[]{:S(2)}, u32[]{:S(2)}) collective-permute-start(bf16[512,640]{1,0:T(8,128)(2,1)S(1)} %bitcast.24), channel_id=1, source_target_pairs={{0,11},{1,0},{2,1},{3,2},{4,3},{5,4},{6,5},{7,6},{8,7},{9,8},{10,9... | collective-permute-start | bytes 1966088 | tf_op jit(solution)/shard_map/ppermute | solution.py:328
  48.7 20.3 %collective-permute-start = (bf16[512,640]{1,0:T(8,128)(2,1)S(1)}, bf16[512,640]{1,0:T(8,128)(2,1)S(1)}, u32[]{:S(2)}, u32[]{:S(2)}) collective-permute-start(bf16[512,640]{1,0:T(8,128)(2,1)S(1)} %bitcast.25), channel_id=1, source_target_pairs={{0,1},{1,2},{2,3},{3,4},{4,5},{5,6},{6,7},{7,8},{8,9},{9,10},{10,1... | collective-permute-start | bytes 1966088 | tf_op jit(solution)/shard_map/ppermute | solution.py:328
  63.7 5.3 %copy-start.1 = (bf16[512,640]{1,0:T(8,128)(2,1)}, bf16[512,640]{1,0:T(8,128)(2,1)S(1)}, u32[]{:S(2)}) copy-start(bf16[512,640]{1,0:T(8,128)(2,1)S(1)} %collective-permute-done.1.down_hbm) | copy-start | bytes 1966084
  76.5 56.8 %copy-start.3 = (s32[2,128]{1,0:T(2,128)S(1)}, s32[2,128]{1,0:T(2,128)}, u32[]{:S(2)}) copy-start(s32[2,128]{1,0:T(2,128)} %get-tuple-element.15.code_ref) | copy-start | bytes 3076
  109.3 50.5 %copy-start.2 = (bf16[512,640]{1,0:T(8,128)(2,1)S(1)}, bf16[512,640]{1,0:T(8,128)(2,1)}, u32[]{:S(2)}) copy-start(bf16[512,640]{1,0:T(8,128)(2,1)} %copy-done.1) | copy-start | bytes 1966084
  109.3 5.2 %collective-permute-start.4 = (bf16[11,128]{1,0:T(8,128)(2,1)S(1)}, bf16[11,128]{1,0:T(8,128)(2,1)S(1)}, u32[]{:S(2)}, u32[]{:S(2)}) collective-permute-start(bf16[11,128]{1,0:T(8,128)(2,1)S(1)} %slice), channel_id=1, source_target_pairs={{0,1},{1,2},{2,3},{3,4},{4,5},{5,6},{6,7},{7,8},{8,9},{9,10},{10,1... | collective-permute-start | bytes 8456
  153.1 15.2 %collective-permute-start.3 = (bf16[4,448,128]{2,1,0:T(8,128)(2,1)S(1)}, bf16[4,448,128]{2,1,0:T(8,128)(2,1)S(1)}, u32[]{:S(2)}, u32[]{:S(2)}) collective-permute-start(bf16[4,448,128]{2,1,0:T(8,128)(2,1)S(1)} %bitcast.21), channel_id=1, source_target_pairs={{0,11},{1,0},{2,1},{3,2},{4,3},{5,4},{6,5},{7,6},{8,7},{9,8},{10,9... | collective-permute-start | bytes 1376264 | tf_op jit(solution)/shard_map/ppermute | solution.py:376
  156.1 14.4 %collective-permute-start.2 = (bf16[4,448,128]{2,1,0:T(8,128)(2,1)S(1)}, bf16[4,448,128]{2,1,0:T(8,128)(2,1)S(1)}, u32[]{:S(2)}, u32[]{:S(2)}) collective-permute-start(bf16[4,448,128]{2,1,0:T(8,128)(2,1)S(1)} %bitcast.22), channel_id=1, source_target_pairs={{0,1},{1,2},{2,3},{3,4},{4,5},{5,6},{6,7},{7,8},{8,9},{9,10},{10,1... | collective-permute-start | bytes 1376264 | tf_op jit(solution)/shard_map/ppermute | solution.py:375

commit v3 on v2

--- a/solution.py
+++ b/solution.py
@@ -141,26 +141,59 @@
     return jnp.where(part >= PARTS, part - PARTS, part)
 
 
-def expert_kernel(
-    stride, part_index_ref, own_hbm, up_hbm, down_hbm, first_hbm, second_hbm, router_ref, part_ref, pre_ref, act_ref,
-    msg_ref, first_ref, second_ref, x_ref, g_ref, sem, weight_sem,
-):
-    loads = fetch((own_hbm, up_hbm, down_hbm), msg_ref, sem)
+def expert_rows(x, g, first, second, router):
+    xf = x.astype(F32)
+    logit = jnp.sum(xf * router, axis=1, keepdims=True)
+    gate = 1.0 / (1.0 + jnp.exp(-logit))
+    pre = jnp.dot(x, first, preferred_element_type=F32)
+    hidden = nt(g, second)
+    tanh_value = jnp.tanh(tanh_scale * (pre + cubic_term * pre * pre * pre))
+    act = 0.5 * pre * (1.0 + tanh_value)
+    slope = 0.5 * (1.0 + tanh_value) + 0.5 * pre * (
+        1.0 - tanh_value * tanh_value
+    ) * tanh_scale * (1.0 + 3.0 * cubic_term * pre * pre)
+    gate_grad = jnp.sum(act * hidden, axis=1, keepdims=True)
+    logit_grad = gate_grad * gate * (1.0 - gate)
+    pre_grad = (hidden * gate * slope).astype(BF)
+    scaled_act = (act * gate).astype(BF)
+    router_sum = jnp.sum(xf * logit_grad, axis=0, keepdims=True)
+    out = jnp.dot(scaled_act, second, preferred_element_type=F32).astype(BF)
+    dx = (nt(pre_grad, first) + logit_grad * router).astype(BF)
+    return pre_grad, scaled_act, router_sum, out, dx
+
+
+def expert_kernel(blocks, rows, stride, last, *refs):
+    n = len(blocks)
+    index_ref, *messages = refs[: n + 1]
+    refs = refs[n + 1 :]
+    if last:
+        first_hbm, second_hbm, router_ref, before_ref, _, part_hbm, pre_ref, act_ref = refs[:8]
+        refs = refs[8:]
+    else:
+        first_hbm, second_hbm, router_ref, part_hbm, pre_ref, act_ref, sum_ref = refs[:7]
+        refs = refs[7:]
+    msg_ref, first_ref, second_ref, x_ref, g_ref, stage_ref, rest_ref = refs[:7]
+    sem, weight_sem, out_sem, rest_sem = refs[7:]
+    width = x_ref.shape[1]
+    chunks = width // 128
+    block = rows // PARTS
+    loads = fetch(messages, msg_ref, sem)
     weights = [
         pltpu.make_async_copy(first_hbm, first_ref, weight_sem.at[0]),
         pltpu.make_async_copy(second_hbm, second_ref, weight_sem.at[1]),
     ]
     for copy in loads[:2] + weights + loads[2:]:
         copy.start()
-    rows, width = x_ref.shape
-    chunks = width // 128
+    stores = []
+    if not last:
+        rest_ref[...] = jnp.zeros(rest_ref.shape, BF)
+        here = pl.ds(chunks * stride, rest_ref.shape[0])
+        stores.append(pltpu.make_async_copy(rest_ref, part_hbm.at[here], rest_sem.at[0]))
+        stores[-1].start()
     router = router_ref[...]
     sort = sorting()
-    router_sum = jnp.zeros((1, width), F32)
-    block = 128
-    left = part_ref.shape[0] - chunks * stride
-    part_ref[pl.ds(chunks * stride, left), :] = jnp.zeros((left, 128), BF)
-    for b in range(rows // block):
+    router_sum = before_ref[...] if last else jnp.zeros((1, width), F32)
+    for b, shift in enumerate(blocks):
         for k in range(2 * b, 2 * b + 2):
             loads[k].wait()
             unpack(sort, msg_ref, k, x_ref, g_ref)
@@ -170,42 +203,50 @@
             first = first_ref[...]
             second = second_ref[...]
         here = pl.ds(b * block, block)
-        x = x_ref[here, :]
-        g = g_ref[here, :]
-        xf = x.astype(F32)
-        logit = jnp.sum(xf * router, axis=1, keepdims=True)
-        gate = 1.0 / (1.0 + jnp.exp(-logit))
-        pre = jnp.dot(x, first, preferred_element_type=F32)
-        hidden = nt(g, second)
-        tanh_value = jnp.tanh(tanh_scale * (pre + cubic_term * pre * pre * pre))
-        act = 0.5 * pre * (1.0 + tanh_value)
-        slope = 0.5 * (1.0 + tanh_value) + 0.5 * pre * (
-            1.0 - tanh_value * tanh_value
-        ) * tanh_scale * (1.0 + 3.0 * cubic_term * pre * pre)
-        gate_grad = jnp.sum(act * hidden, axis=1, keepdims=True)
-        logit_grad = gate_grad * gate * (1.0 - gate)
-        pre_grad = (hidden * gate * slope).astype(BF)
-        scaled_act = (act * gate).astype(BF)
+        pre_grad, scaled_act, extra, out, dx = expert_rows(
+            x_ref[here, :], g_ref[here, :], first, second, router
+        )
         pre_ref[here, :] = pre_grad
         act_ref[here, :] = scaled_act
-        router_sum = router_sum + jnp.sum(xf * logit_grad, axis=0, keepdims=True)
-        place = wrap(part_index_ref[0] + (0, 2, 1)[b]) * block
-        out = jnp.dot(scaled_act, second, preferred_element_type=F32).astype(BF)
-        dx = (nt(pre_grad, first) + logit_grad * router).astype(BF)
+        router_sum = router_sum + extra
+        place = wrap(index_ref[0] + shift) * block
         for c in range(chunks):
             lanes = slice(c * 128, (c + 1) * 128)
-            at_out = pl.multiple_of(place + c * stride, 16)
-            at_dx = pl.multiple_of(place + c * stride + rows, 16)
-            part_ref[pl.ds(at_out, block), :] = out[:, lanes]
-            part_ref[pl.ds(at_dx, block), :] = dx[:, lanes]
-    for c in range(chunks):
-        lanes = slice(c * 128, (c + 1) * 128)
-        tail = jnp.where(iota((16, 128), 0) == 0, router_sum[:, lanes], 0.0)
-        part_ref[pl.ds(c * stride + 2 * rows, 16), :] = tail.astype(BF)
+            for k, value in enumerate((out, dx)):
+                at = (b * chunks + c) * 2 + k
+                staged = pl.ds(at * block, block)
+                stage_ref[staged, :] = value[:, lanes]
+                there = pl.ds(pl.multiple_of(place + c * stride + k * rows, 8), block)
+                stores.append(
+                    pltpu.make_async_copy(
+                        stage_ref.at[staged], part_hbm.at[there], out_sem.at[at]
+                    )
+                )
+                stores[-1].start()
+    if last:
+        tail = stride - 2 * rows
+        for c in range(chunks):
+            lanes = slice(c * 128, (c + 1) * 128)
+            staged = pl.ds(c * tail, tail)
+            row = jnp.where(iota((tail, 128), 0) == 0, router_sum[:, lanes], 0.0)
+            rest_ref[staged, :] = row.astype(BF)
+            stores.append(
+                pltpu.make_async_copy(
+                    rest_ref.at[staged],
+                    part_hbm.at[pl.ds(c * stride + 2 * rows, tail)],
+                    rest_sem.at[c],
+                )
+            )
+            stores[-1].start()
+    else:
+        sum_ref[...] = router_sum
+    for store in stores:
+        store.wait()
 
 
 def weight_kernel(
-    own_hbm, up_hbm, down_hbm, pre_ref, act_ref, first_ref, second_ref, msg_ref, x_ref, g_ref, sem
+    own_hbm, up_hbm, down_hbm, pre_own, act_own, pre_rest, act_rest,
+    first_ref, second_ref, msg_ref, x_ref, g_ref, sem,
 ):
     loads = fetch((own_hbm, up_hbm, down_hbm), msg_ref, sem)
     for load in loads:
@@ -214,8 +255,10 @@
     for k, load in enumerate(loads):
         load.wait()
         unpack(sort, msg_ref, k, x_ref, g_ref)
-    first_ref[...] = tn(x_ref[...], pre_ref[...]).astype(BF)
-    second_ref[...] = tn(act_ref[...], g_ref[...]).astype(BF)
+    pre_grad = jnp.concatenate([pre_own[...], pre_rest[...]], axis=0)
+    scaled_act = jnp.concatenate([act_own[...], act_rest[...]], axis=0)
+    first_ref[...] = tn(x_ref[...], pre_grad).astype(BF)
+    second_ref[...] = tn(scaled_act, g_ref[...]).astype(BF)
 
 
 def return_kernel(rows, shift_ref, sum_ref, msg_ref, hold_ref):
@@ -277,13 +320,14 @@
                 router_ref[:, lanes] = ref[k, 3 * tok_rows :, :].astype(F32)
 
 
-def call(kernel, out, specs, name, flops, size, scratch=(), out_specs=None, limit=FULL):
+def call(kernel, out, specs, name, flops, size, scratch=(), out_specs=None, limit=FULL, alias=None):
     return pl.pallas_call(
         kernel,
         out_shape=[jax.ShapeDtypeStruct(s, d) for s, d in out],
         in_specs=specs,
         out_specs=out_specs or [VM] * len(out),
         scratch_shapes=list(scratch),
+        input_output_aliases=alias or {},
         compiler_params=pltpu.CompilerParams(vmem_limit_bytes=limit),
         cost_estimate=pl.CostEstimate(flops=flops, bytes_accessed=size, transcendentals=0),
         name=name,
@@ -307,7 +351,6 @@
     lines = [list(range(k, z_count, PARTS)) for k in range(PARTS)]
 
     dma = pltpu.SemaphoreType.DMA
-    count = rows * 4 // 256
     msg, codes = call(
         dispatch_kernel,
         [((places * 8, half), BF), ((members, tok_rows), jnp.int32)],
@@ -329,19 +372,41 @@
     column = lax.dynamic_slice(
         router, (lax.axis_index("member"), 0, lax.axis_index("dp")), (1, width, 1)
     ).reshape(1, width)
-    stride = 2 * rows + 16
-    share = stride - 1
-    sides = [pltpu.VMEM((rows * 4, half), BF)]
-    pair = [pltpu.VMEM((rows, width), BF)] * 2
-    part, pre_grad, scaled_act = call(
-        functools.partial(expert_kernel, stride),
-        [((z_count * share, 128), BF), ((rows, hidden), BF), ((rows, hidden), BF)],
-        [SM] + [HB] * 5 + [VM], "expert", 3 << 30, 8 << 20, limit=MOST,
-        scratch=sides
-        + [pltpu.VMEM((width, hidden), BF), pltpu.VMEM((hidden, width), BF)]
-        + pair
-        + [dma((count,)), dma((2,))],
-    )(part_index, *arrived, w_in[0, 0], w_out[0, 0], column)
+    stride = 2 * rows + 32
+    share = stride - 2
+    chunks = width // 128
+    block = rows // PARTS
+
+    def expert_scratch(n, spare):
+        return [
+            pltpu.VMEM((n * 512, half), BF),
+            pltpu.VMEM((width, hidden), BF),
+            pltpu.VMEM((hidden, width), BF),
+            pltpu.VMEM((n * block, width), BF),
+            pltpu.VMEM((n * block, width), BF),
+            pltpu.VMEM((n * chunks * 2 * block, 128), BF),
+            pltpu.VMEM((spare, 128), BF),
+            dma((2 * n,)),
+            dma((2,)),
+            dma((2 * n * chunks,)),
+            dma((chunks,)),
+        ]
+
+    whole = ((z_count * share, 128), BF)
+    part, pre_own, act_own, router_own = call(
+        functools.partial(expert_kernel, (0,), rows, stride, False),
+        [whole, ((block, hidden), BF), ((block, hidden), BF), ((1, width), F32)],
+        [SM] + [HB] * 3 + [VM], "expert_own", 1 << 30, 6 << 20,
+        scratch=expert_scratch(1, z_count * share - chunks * stride),
+        out_specs=[HB, VM, VM, VM], limit=MOST,
+    )(part_index, own, w_in[0, 0], w_out[0, 0], column)
+    part, pre_rest, act_rest = call(
+        functools.partial(expert_kernel, (2, 1), rows, stride, True),
+        [whole, ((2 * block, hidden), BF), ((2 * block, hidden), BF)],
+        [SM] + [HB] * 4 + [VM] * 2 + [HB], "expert_rest", 2 << 30, 8 << 20,
+        scratch=expert_scratch(2, chunks * (stride - 2 * rows)),
+        out_specs=[HB, VM, VM], limit=MOST, alias={7: 0},
+    )(part_index, *arrived[1:], w_in[0, 0], w_out[0, 0], column, router_own, part)
     total = lax.psum_scatter(part, "expert", scatter_dimension=0, tiled=True)
     (back,) = call(
         functools.partial(return_kernel, rows),
@@ -349,16 +414,18 @@
         [SM, VM], "to_tokens", 1 << 28, 1 << 20,
         scratch=[pltpu.VMEM((-(-share // 128) * 128, 128), BF)],
         limit=LIMIT,
-    )(z.reshape(1), total)
+    )(2 * z.reshape(1), total)
     home = lax.all_to_all(
         back.reshape(places, 16, 128), plane, split_axis=0, concat_axis=0, tiled=True
     ).reshape(places * 16, 128)
     grad_first, grad_second = call(
         weight_kernel,
         [((width, hidden), BF), ((hidden, width), BF)],
-        [HB] * 3 + [VM] * 2, "weights", 1 << 30, 6 << 20, limit=LESS,
-        scratch=sides + pair + [dma((count,))],
-    )(*arrived, pre_grad, scaled_act)
+        [HB] * 3 + [VM] * 4, "weights", 1 << 30, 6 << 20, limit=LESS,
+        scratch=[pltpu.VMEM((rows * 4, half), BF)]
+        + [pltpu.VMEM((rows, width), BF)] * 2
+        + [dma((2 * PARTS,))],
+    )(*arrived, pre_own, act_own, pre_rest, act_rest)
     (compact,) = call(
         collect_kernel,
         [(((members + 1) * tok_rows + places, 128), BF)],

time: 172 us -> 172 us (level)
  waiting for transfers between devices: 24.4 us -> 16.2 us
  blocking collectives: 102 us -> 107 us
  Pallas kernels: 18.2 us -> 20.4 us
    ppermute x1, waiting for transfers between devices: 13 us -> 1.53 us  [shards(): lax.ppermute(own, 'expert', behind)]
    ppermute x1, waiting for transfers between devices: 5.33 us -> 9.46 us  [shards(): lax.ppermute(own, 'expert', ahead)]
    unnamed x1, blocking collectives: 32.8 us -> 35.7 us
    pallas_call x1 -> x2, Pallas kernels: 7.4 us -> 9.57 us  [the longest x1 5.61 us: shards(): call(functools.partial(expert_kernel, (2, 1), rows, stride, True), [whole...]
    all_gather x1, blocking collectives: 19.2 us -> 21.3 us  [shards(): line = lax.all_gather(compact, 'expert', axis_index_groups=lines)]
    ppermute x1, waiting for transfers between devices: 2.23 us -> 0.12 us  [shards(): lax.ppermute(line, 'expert', ahead)]
  transfers between devices with their start and end apart: 5 -> 5, of which waited for: 4 -> 4; matrix products, arithmetic and copies ran while one was open for 1% -> 1% of each run, Pallas kernels for 3% -> 5%
where the time goes in v3:
time: 172 us; the launch traced here: 171 us
  blocking collectives  107 us (62%)
  starting transfers between devices  23.6 us (14%)
  Pallas kernels  20.4 us (12%)
  waiting for transfers between devices  16.2 us (9%)
  local copies, waits for them, and re-layouts  2.44 us (1%)
    unnamed x1, blocking collectives  35.7 us
    all_to_all x1, blocking collectives, shards(): lax.all_to_all(msg.reshape(places, 8, half), plane, split_axis=0, concat_...  33.2 us
    all_gather x1, blocking collectives, shards(): line = lax.all_gather(compact, 'expert', axis_index_groups=lines)  21.3 us
    all_to_all x1, blocking collectives, shards(): lax.all_to_all(back.reshape(places, 16, 128), plane, split_axis=0, concat...  17 us
    ppermute x1, starting transfers between devices, shards(): lax.ppermute(own, 'expert', behind)  11.4 us
    ppermute x1, waiting for transfers between devices, shards(): lax.ppermute(own, 'expert', ahead)  9.46 us
    pallas_call x1, Pallas kernels, shards(): call(functools.partial(expert_kernel, (2, 1), rows, stride, True), [whole...  5.61 us
    ppermute x1, waiting for transfers between devices, shards(): lax.ppermute(line, 'expert', behind)  5.06 us
  transfers between devices with their start and end apart: 5, of which 4 were waited for; matrix products, arithmetic and copies ran while one was open for 1% of the time, Pallas kernels for 5%

profile of v3, /device:TPU:6, one launch (start us, length us, event | category | flops | bytes accessed | tf_op | source)
XLA Modules:
  0.0 171.3 jit_solution(1035358281891809888)
XLA Ops:
  0.6 0.0 copy-start
  0.7 3.4 %dispatch.1 = (bf16[512,640]{1,0:T(8,128)(2,1)}, s32[2,128]{1,0:T(2,128)}) custom-call(s32[1]{0:T(128)} %bitcast.part_ref.refs_0_, s32[2,128]{1,0:T(2,128)} %bitcast.37, bf16[128,1280]{1,0:T(8,128)(2,1)} %tok_hbm.1, bf16[2,128,1280]{2,1,0:T(8,128)(2,1)} %grad_hbm.1), custom_call_target="tpu_custom_call" | custom-call | flops 3221225472 | bytes 4194304 | tf_op jit(solution)/shard_map/dispatch/pallas_call | solution.py:354
  4.1 33.2 %all_to_all.10 = bf16[64,8,640]{2,1,0:T(8,128)(2,1)S(1)} all-to-all(bf16[64,8,640]{2,1,0:T(8,128)(2,1)} %bitcast.32), channel_id=1, replica_groups=mesh['dp'=32,'member'=2,'expert'=12] {'dp','member'}, dimensions={0} | all-to-all | bytes 1310720 | tf_op jit(solution)/shard_map/all_to_all | solution.py:368
  37.4 1.9 %collective-permute-start = (bf16[512,640]{1,0:T(8,128)(2,1)S(1)}, bf16[512,640]{1,0:T(8,128)(2,1)S(1)}, u32[]{:S(2)}, u32[]{:S(2)}) collective-permute-start(bf16[512,640]{1,0:T(8,128)(2,1)S(1)} %bitcast.24), channel_id=1, source_target_pairs={{0,1},{1,2},{2,3},{3,4},{4,5},{5,6},{6,7},{7,8},{8,9},{9,10},{10,1... | collective-permute-start | bytes 1966088 | tf_op jit(solution)/shard_map/ppermute | solution.py:371
  39.3 11.4 %collective-permute-start.1 = (bf16[512,640]{1,0:T(8,128)(2,1)S(1)}, bf16[512,640]{1,0:T(8,128)(2,1)S(1)}, u32[]{:S(2)}, u32[]{:S(2)}) collective-permute-start(bf16[512,640]{1,0:T(8,128)(2,1)S(1)} %bitcast.25), channel_id=1, source_target_pairs={{0,11},{1,0},{2,1},{3,2},{4,3},{5,4},{6,5},{7,6},{8,7},{9,8},{10,9... | collective-permute-start | bytes 1966088 | tf_op jit(solution)/shard_map/ppermute | solution.py:371
  50.8 4.0 %expert_own.1 = (bf16[9576,128]{1,0:T(8,128)(2,1)}, bf16[128,384]{1,0:T(8,128)(2,1)S(1)}, bf16[128,384]{1,0:T(8,128)(2,1)S(1)}, f32[1,1280]{1,0:T(1,128)S(1)}) custom-call(s32[1]{0:T(128)} %bitcast.part_ref.refs_0_, bf16[512,640]{1,0:T(8,128)(2,1)S(1)} %bitcast.26, bf16[1280,384]{1,0:T(8,128)(2,1)S(1)} %bitcast.31, bf16[384,1280]{1,0:T(8,128)(2,1)} %bitcast.33, ...), custom_call_target="tpu_custom_call" | custom-call | flops 1073741824 | bytes 6291456 | tf_op jit(solution)/shard_map/expert_own/pallas_call | solution.py:396
  54.7 9.5 %collective-permute-done.refs_1_.up_hbm = bf16[512,640]{1,0:T(8,128)(2,1)S(1)} collective-permute-done((bf16[512,640]{1,0:T(8,128)(2,1)S(1)}, bf16[512,640]{1,0:T(8,128)(2,1)S(1)}, u32[]{:S(2)}, u32[]{:S(2)}) %collective-permute-start) | collective-permute-done | bytes 655392 | tf_op jit(solution)/shard_map/ppermute | solution.py:371
  64.2 1.5 collective-permute-done.1.refs_2_.down_hbm
  65.7 5.6 %expert_rest.1 = (bf16[9576,128]{1,0:T(8,128)(2,1)}, bf16[256,384]{1,0:T(8,128)(2,1)S(1)}, bf16[256,384]{1,0:T(8,128)(2,1)S(1)}) custom-call(s32[1]{0:T(128)} %bitcast.part_ref.refs_0_, bf16[512,640]{1,0:T(8,128)(2,1)S(1)} %collective-permute-done.refs_1_.up_hbm, ...), custom_call_target="tpu_custom_call", output_to_operand_aliasing={{0}: (7, {})} | custom-call | flops 2147483648 | bytes 8388608 | tf_op jit(solution)/shard_map/expert_rest/pallas_call | solution.py:403
  71.4 35.7 %fusion = bf16[800,128]{1,0:T(8,128)(2,1)S(1)} fusion(bf16[9576,128]{1,0:T(8,128)(2,1)} %get-tuple-element.23), kind=kCustom, calls=%all-reduce-scatter | all-reduce-scatter fusion | flops 1228801 | bytes 2660352
  107.1 3.0 %collective-permute-start.4 = (bf16[22,128]{1,0:T(8,128)(2,1)S(1)}, bf16[22,128]{1,0:T(8,128)(2,1)S(1)}, u32[]{:S(2)}, u32[]{:S(2)}) collective-permute-start(bf16[22,128]{1,0:T(8,128)(2,1)S(1)} %slice), channel_id=1, source_target_pairs={{0,1},{1,2},{2,3},{3,4},{4,5},{5,6},{6,7},{7,8},{8,9},{9,10},{10,1... | collective-permute-start | bytes 16904
  110.1 1.3 dynamic-slice.4
  112.0 1.1 concatenate
  113.1 0.1 constant_dynamic-slice_fusion.sum_ref
  113.2 0.8 to_tokens.1
  114.0 17.0 %all_to_all.11 = bf16[64,16,128]{2,1,0:T(8,128)(2,1)S(1)} all-to-all(bf16[64,16,128]{2,1,0:T(8,128)(2,1)S(1)} %bitcast.29), channel_id=1, replica_groups=mesh['dp'=32,'member'=2,'expert'=12] {'dp','member'}, dimensions={0} | all-to-all | bytes 524288 | tf_op jit(solution)/shard_map/all_to_all | solution.py:418
  131.0 0.6 collect.1
  131.6 21.3 %all-gather = bf16[1792,128]{1,0:T(8,128)(2,1)S(1)} all-gather(bf16[448,128]{1,0:T(8,128)(2,1)S(1)} %collect.1), channel_id=2, replica_groups={{0,3,6,9},{1,4,7,10},{2,5,8,11},{12,15,18,21},{13,16,19,22},{14,17,20,2..., dimensions={0}, use_global_device_ids=true | all-gather | bytes 573440 | tf_op jit(solution)/shard_map/all_gather | solution.py:434
  152.9 2.8 %collective-permute-start.2 = (bf16[4,448,128]{2,1,0:T(8,128)(2,1)S(1)}, bf16[4,448,128]{2,1,0:T(8,128)(2,1)S(1)}, u32[]{:S(2)}, u32[]{:S(2)}) collective-permute-start(bf16[4,448,128]{2,1,0:T(8,128)(2,1)S(1)} %bitcast.21), channel_id=1, source_target_pairs={{0,1},{1,2},{2,3},{3,4},{4,5},{5,6},{6,7},{7,8},{8,9},{9,10},{10,1... | collective-permute-start | bytes 1376264 | tf_op jit(solution)/shard_map/ppermute | solution.py:442
  155.7 4.4 %collective-permute-start.3 = (bf16[4,448,128]{2,1,0:T(8,128)(2,1)S(1)}, bf16[4,448,128]{2,1,0:T(8,128)(2,1)S(1)}, u32[]{:S(2)}, u32[]{:S(2)}) collective-permute-start(bf16[4,448,128]{2,1,0:T(8,128)(2,1)S(1)} %bitcast.22), channel_id=1, source_target_pairs={{0,11},{1,0},{2,1},{3,2},{4,3},{5,4},{6,5},{7,6},{8,7},{9,8},{10,9... | collective-permute-start | bytes 1376264 | tf_op jit(solution)/shard_map/ppermute | solution.py:443
  160.1 4.6 %weights.1 = (bf16[1280,384]{1,0:T(8,128)(2,1)}, bf16[384,1280]{1,0:T(8,128)(2,1)}) custom-call(bf16[512,640]{1,0:T(8,128)(2,1)S(1)} %bitcast.27, bf16[512,640]{1,0:T(8,128)(2,1)S(1)} %collective-permute-done.refs_1_.up_hbm, bf16[512,640]{1,0:T(8,128)(2,1)S(1)} %collective-permute-done.1.refs_2_.down_hbm, bf16[128,384]{1,0:T(8,128)(2,1)S(1)} %get-tuple-element.26.pre_own, ...), custom_call_target="tpu_custom_call" | custom-call | flops 1073741824 | bytes 6291456 | tf_op jit(solution)/shard_map/weights/pallas_call | solution.py:421
  164.7 0.1 collective-permute-done.2.up_ref
  164.9 5.1 %collective-permute-done.3.down_ref = bf16[4,448,128]{2,1,0:T(8,128)(2,1)S(1)} collective-permute-done((bf16[4,448,128]{2,1,0:T(8,128)(2,1)S(1)}, bf16[4,448,128]{2,1,0:T(8,128)(2,1)S(1)}, u32[]{:S(2)}, u32[]{:S(2)}) %collective-permute-start.3) | collective-permute-done | bytes 458784 | tf_op jit(solution)/shard_map/ppermute | solution.py:443
  169.9 1.4 final.1
  (8 shorter events, 0.0 us)
Async XLA Ops:
  0.6 50.1 %copy-start = (f32[2,1280,32]{1,2,0:T(8,128)S(1)}, f32[2,1280,32]{1,2,0:T(8,128)}, u32[]{:S(2)}) copy-start(f32[2,1280,32]{1,2,0:T(8,128)} %param.8) | copy-start | bytes 983044
  0.7 50.1 %copy-start.1 = (bf16[1,1,1280,384]{3,2,1,0:T(8,128)(2,1)S(1)}, bf16[1,1,1280,384]{3,2,1,0:T(8,128)(2,1)}, u32[]{:S(2)}) copy-start(bf16[1,1,1280,384]{3,2,1,0:T(8,128)(2,1)} %param.9) | copy-start | bytes 2949124
  37.4 26.8 %collective-permute-start = (bf16[512,640]{1,0:T(8,128)(2,1)S(1)}, bf16[512,640]{1,0:T(8,128)(2,1)S(1)}, u32[]{:S(2)}, u32[]{:S(2)}) collective-permute-start(bf16[512,640]{1,0:T(8,128)(2,1)S(1)} %bitcast.24), channel_id=1, source_target_pairs={{0,1},{1,2},{2,3},{3,4},{4,5},{5,6},{6,7},{7,8},{8,9},{9,10},{10,1... | collective-permute-start | bytes 1966088 | tf_op jit(solution)/shard_map/ppermute | solution.py:371
  39.3 26.5 %collective-permute-start.1 = (bf16[512,640]{1,0:T(8,128)(2,1)S(1)}, bf16[512,640]{1,0:T(8,128)(2,1)S(1)}, u32[]{:S(2)}, u32[]{:S(2)}) collective-permute-start(bf16[512,640]{1,0:T(8,128)(2,1)S(1)} %bitcast.25), channel_id=1, source_target_pairs={{0,11},{1,0},{2,1},{3,2},{4,3},{5,4},{6,5},{7,6},{8,7},{9,8},{10,9... | collective-permute-start | bytes 1966088 | tf_op jit(solution)/shard_map/ppermute | solution.py:371
  71.3 59.6 %copy-start.2 = (s32[2,128]{1,0:T(2,128)S(1)}, s32[2,128]{1,0:T(2,128)}, u32[]{:S(2)}) copy-start(s32[2,128]{1,0:T(2,128)} %get-tuple-element.19.code_ref) | copy-start | bytes 3076
  107.1 5.0 %collective-permute-start.4 = (bf16[22,128]{1,0:T(8,128)(2,1)S(1)}, bf16[22,128]{1,0:T(8,128)(2,1)S(1)}, u32[]{:S(2)}, u32[]{:S(2)}) collective-permute-start(bf16[22,128]{1,0:T(8,128)(2,1)S(1)} %slice), channel_id=1, source_target_pairs={{0,1},{1,2},{2,3},{3,4},{4,5},{5,6},{6,7},{7,8},{8,9},{9,10},{10,1... | collective-permute-start | bytes 16904
  152.9 12.0 %collective-permute-start.2 = (bf16[4,448,128]{2,1,0:T(8,128)(2,1)S(1)}, bf16[4,448,128]{2,1,0:T(8,128)(2,1)S(1)}, u32[]{:S(2)}, u32[]{:S(2)}) collective-permute-start(bf16[4,448,128]{2,1,0:T(8,128)(2,1)S(1)} %bitcast.21), channel_id=1, source_target_pairs={{0,1},{1,2},{2,3},{3,4},{4,5},{5,6},{6,7},{7,8},{8,9},{9,10},{10,1... | collective-permute-start | bytes 1376264 | tf_op jit(solution)/shard_map/ppermute | solution.py:442
  155.7 14.3 %collective-permute-start.3 = (bf16[4,448,128]{2,1,0:T(8,128)(2,1)S(1)}, bf16[4,448,128]{2,1,0:T(8,128)(2,1)S(1)}, u32[]{:S(2)}, u32[]{:S(2)}) collective-permute-start(bf16[4,448,128]{2,1,0:T(8,128)(2,1)S(1)} %bitcast.22), channel_id=1, source_target_pairs={{0,11},{1,0},{2,1},{3,2},{4,3},{5,4},{6,5},{7,6},{8,7},{9,8},{10,9... | collective-permute-start | bytes 1376264 | tf_op jit(solution)/shard_map/ppermute | solution.py:443

commit v4 on v2

--- a/solution.py
+++ b/solution.py
@@ -13,7 +13,7 @@
 cubic_term = 0.044715
 LIMIT = 44 << 20
 FULL = 60 << 20
-MOST = 52 << 20
+MOST = 44 << 20
 LESS = 24 << 20
 PARTS = 3
 VM = pl.BlockSpec(memory_space=pltpu.VMEM)
@@ -60,37 +60,22 @@
         codes.append(code)
     loads[1].wait()
     loads[2].wait()
-    sides = [
-        jnp.concatenate([v[:, :half], v[:, half:]], axis=0)
-        for v in (tok_ref[...], grad_ref[0], grad_ref[1])
-    ]
-    block = 256
+    token = tok_ref[...]
     stores = []
-    for b in range(msg_ref.shape[0] // block):
-        row = iota((block, tok_rows), 0) + b * block
-        dest = lax.shift_right_logical(row, 3)
-        slot = 2 * part_ref[0] + (row & 1)
+    for m in range(2):
+        grad = grad_ref[m]
+        side = jnp.concatenate(
+            [token[:, :half], token[:, half:], grad[:, :half], grad[:, half:]], axis=0
+        )
+        row = iota((msg_ref.shape[0] * 8, tok_rows), 0)
         kind = lax.shift_right_logical(row & 7, 1)
-        code = lax.shift_right_logical(dest, 1) * 8 + slot
-        member = dest & 1
-        hit0 = (code == codes[0]) & (member == 0)
-        hit1 = (code == codes[1]) & (member == 1)
-        hit = hit0 | hit1
-        parts = (
-            [hit & (kind == 0), hit & (kind == 1)],
-            [hit0 & (kind == 2), hit0 & (kind == 3)],
-            [hit1 & (kind == 2), hit1 & (kind == 3)],
-        )
-        total = None
-        for pair, side in zip(parts, sides):
-            pick = jnp.concatenate([one(p) for p in pair], axis=1)
-            term = jnp.dot(pick, side, preferred_element_type=F32)
-            total = term if total is None else total + term
-        here = pl.ds(b * block, block)
-        msg_ref[here, :] = total.astype(BF)
-        store = pltpu.make_async_copy(msg_ref.at[here], msg_hbm.at[here], out_sem.at[b])
-        store.start()
-        stores.append(store)
+        code = lax.shift_right_logical(row, 3) * 8 + 2 * part_ref[0] + (row & 1)
+        hit = code == codes[m]
+        pick = jnp.concatenate([one(hit & (kind == k)) for k in range(4)], axis=1)
+        rows = jnp.dot(pick, side, preferred_element_type=F32).astype(BF)
+        msg_ref[:, m] = rows.reshape(msg_ref.shape[0], 8, half)
+        stores.append(pltpu.make_async_copy(msg_ref.at[:, m], msg_hbm.at[:, m], out_sem.at[m]))
+        stores[-1].start()
     for store in stores:
         store.wait()
 
@@ -141,71 +126,96 @@
     return jnp.where(part >= PARTS, part - PARTS, part)
 
 
-def expert_kernel(
-    stride, part_index_ref, own_hbm, up_hbm, down_hbm, first_hbm, second_hbm, router_ref, part_ref, pre_ref, act_ref,
-    msg_ref, first_ref, second_ref, x_ref, g_ref, sem, weight_sem,
+def expert_rows(x, g, first, second, router):
+    xf = x.astype(F32)
+    logit = jnp.sum(xf * router, axis=1, keepdims=True)
+    gate = 1.0 / (1.0 + jnp.exp(-logit))
+    pre = jnp.dot(x, first, preferred_element_type=F32)
+    hidden = nt(g, second)
+    tanh_value = jnp.tanh(tanh_scale * (pre + cubic_term * pre * pre * pre))
+    act = 0.5 * pre * (1.0 + tanh_value)
+    slope = 0.5 * (1.0 + tanh_value) + 0.5 * pre * (
+        1.0 - tanh_value * tanh_value
+    ) * tanh_scale * (1.0 + 3.0 * cubic_term * pre * pre)
+    gate_grad = jnp.sum(act * hidden, axis=1, keepdims=True)
+    logit_grad = gate_grad * gate * (1.0 - gate)
+    pre_grad = (hidden * gate * slope).astype(BF)
+    scaled_act = (act * gate).astype(BF)
+    router_sum = jnp.sum(xf * logit_grad, axis=0, keepdims=True)
+    out = jnp.dot(scaled_act, second, preferred_element_type=F32).astype(BF)
+    dx = (nt(pre_grad, first) + logit_grad * router).astype(BF)
+    return pre_grad, scaled_act, router_sum, out, dx
+
+
+def expert_block(shift, b, stride, index_ref, msg_ref, weights, router_ref, refs):
+    part_ref, kept_ref, x_ref, g_ref = refs
+    rows = PARTS * x_ref.shape[0]
+    block, width = x_ref.shape
+    sort = sorting()
+    for k in range(2):
+        unpack(sort, msg_ref, k, x_ref, g_ref)
+    pre_grad, scaled_act, extra, out, dx = expert_rows(
+        x_ref[...], g_ref[...], *weights(), router_ref[...]
+    )
+    here = pl.ds(b * block, block)
+    kept_ref[here, 0 : pre_grad.shape[1]] = pre_grad
+    kept_ref[here, pre_grad.shape[1] :] = scaled_act
+    place = wrap(index_ref[0] + shift) * block
+    for c in range(width // 128):
+        lanes = slice(c * 128, (c + 1) * 128)
+        for k, value in enumerate((out, dx)):
+            there = pl.ds(pl.multiple_of(place + c * stride + k * rows, 16), block)
+            part_ref[there, :] = value[:, lanes]
+    return extra
+
+
+def own_kernel(
+    stride, index_ref, msg_ref, first_hbm, second_hbm, router_ref,
+    part_ref, kept_ref, sum_ref, first_ref, second_ref, x_ref, g_ref, sem,
 ):
-    loads = fetch((own_hbm, up_hbm, down_hbm), msg_ref, sem)
-    weights = [
-        pltpu.make_async_copy(first_hbm, first_ref, weight_sem.at[0]),
-        pltpu.make_async_copy(second_hbm, second_ref, weight_sem.at[1]),
+    loads = [
+        pltpu.make_async_copy(first_hbm, first_ref, sem.at[0]),
+        pltpu.make_async_copy(second_hbm, second_ref, sem.at[1]),
     ]
-    for copy in loads[:2] + weights + loads[2:]:
-        copy.start()
-    rows, width = x_ref.shape
-    chunks = width // 128
-    router = router_ref[...]
-    sort = sorting()
-    router_sum = jnp.zeros((1, width), F32)
-    block = 128
-    left = part_ref.shape[0] - chunks * stride
-    part_ref[pl.ds(chunks * stride, left), :] = jnp.zeros((left, 128), BF)
-    for b in range(rows // block):
-        for k in range(2 * b, 2 * b + 2):
-            loads[k].wait()
-            unpack(sort, msg_ref, k, x_ref, g_ref)
-        if b == 0:
-            for copy in weights:
-                copy.wait()
-            first = first_ref[...]
-            second = second_ref[...]
-        here = pl.ds(b * block, block)
-        x = x_ref[here, :]
-        g = g_ref[here, :]
-        xf = x.astype(F32)
-        logit = jnp.sum(xf * router, axis=1, keepdims=True)
-        gate = 1.0 / (1.0 + jnp.exp(-logit))
-        pre = jnp.dot(x, first, preferred_element_type=F32)
-        hidden = nt(g, second)
-        tanh_value = jnp.tanh(tanh_scale * (pre + cubic_term * pre * pre * pre))
-        act = 0.5 * pre * (1.0 + tanh_value)
-        slope = 0.5 * (1.0 + tanh_value) + 0.5 * pre * (
-            1.0 - tanh_value * tanh_value
-        ) * tanh_scale * (1.0 + 3.0 * cubic_term * pre * pre)
-        gate_grad = jnp.sum(act * hidden, axis=1, keepdims=True)
-        logit_grad = gate_grad * gate * (1.0 - gate)
-        pre_grad = (hidden * gate * slope).astype(BF)
-        scaled_act = (act * gate).astype(BF)
-        pre_ref[here, :] = pre_grad
-        act_ref[here, :] = scaled_act
-        router_sum = router_sum + jnp.sum(xf * logit_grad, axis=0, keepdims=True)
-        place = wrap(part_index_ref[0] + (0, 2, 1)[b]) * block
-        out = jnp.dot(scaled_act, second, preferred_element_type=F32).astype(BF)
-        dx = (nt(pre_grad, first) + logit_grad * router).astype(BF)
-        for c in range(chunks):
-            lanes = slice(c * 128, (c + 1) * 128)
-            at_out = pl.multiple_of(place + c * stride, 16)
-            at_dx = pl.multiple_of(place + c * stride + rows, 16)
-            part_ref[pl.ds(at_out, block), :] = out[:, lanes]
-            part_ref[pl.ds(at_dx, block), :] = dx[:, lanes]
-    for c in range(chunks):
+    for load in loads:
+        load.start()
+    used = x_ref.shape[1] // 128 * stride
+    left = part_ref.shape[0] - used
+    part_ref[pl.ds(used, left), :] = jnp.zeros((left, 128), BF)
+
+    def weights():
+        for load in loads:
+            load.wait()
+        return first_ref[...], second_ref[...]
+
+    sum_ref[...] = expert_block(
+        0, 0, stride, index_ref, msg_ref, weights, router_ref,
+        (part_ref, kept_ref, x_ref, g_ref),
+    )
+
+
+def rest_kernel(
+    stride, index_ref, up_ref, down_ref, first_ref, second_ref, router_ref, before_ref, _,
+    part_ref, kept_ref, x_ref, g_ref,
+):
+    rows = PARTS * x_ref.shape[1]
+    router_sum = before_ref[...]
+    for b, (shift, msg_ref) in enumerate(((2, up_ref), (1, down_ref))):
+        router_sum = router_sum + expert_block(
+            shift, b, stride, index_ref, msg_ref,
+            lambda: (first_ref[...], second_ref[...]), router_ref,
+            (part_ref, kept_ref, x_ref.at[b], g_ref.at[b]),
+        )
+    tail = stride - 2 * rows
+    for c in range(x_ref.shape[2] // 128):
         lanes = slice(c * 128, (c + 1) * 128)
-        tail = jnp.where(iota((16, 128), 0) == 0, router_sum[:, lanes], 0.0)
-        part_ref[pl.ds(c * stride + 2 * rows, 16), :] = tail.astype(BF)
+        row = jnp.where(iota((tail, 128), 0) == 0, router_sum[:, lanes], 0.0)
+        part_ref[pl.ds(c * stride + 2 * rows, tail), :] = row.astype(BF)
 
 
 def weight_kernel(
-    own_hbm, up_hbm, down_hbm, pre_ref, act_ref, first_ref, second_ref, msg_ref, x_ref, g_ref, sem
+    own_hbm, up_hbm, down_hbm, own_ref, rest_ref,
+    first_ref, second_ref, msg_ref, x_ref, g_ref, sem,
 ):
     loads = fetch((own_hbm, up_hbm, down_hbm), msg_ref, sem)
     for load in loads:
@@ -214,8 +224,10 @@
     for k, load in enumerate(loads):
         load.wait()
         unpack(sort, msg_ref, k, x_ref, g_ref)
-    first_ref[...] = tn(x_ref[...], pre_ref[...]).astype(BF)
-    second_ref[...] = tn(act_ref[...], g_ref[...]).astype(BF)
+    kept = jnp.concatenate([own_ref[...], rest_ref[...]], axis=0)
+    pre_grad, scaled_act = jnp.split(kept, 2, axis=1)
+    first_ref[...] = tn(x_ref[...], pre_grad).astype(BF)
+    second_ref[...] = tn(scaled_act, g_ref[...]).astype(BF)
 
 
 def return_kernel(rows, shift_ref, sum_ref, msg_ref, hold_ref):
@@ -277,13 +289,14 @@
                 router_ref[:, lanes] = ref[k, 3 * tok_rows :, :].astype(F32)
 
 
-def call(kernel, out, specs, name, flops, size, scratch=(), out_specs=None, limit=FULL):
+def call(kernel, out, specs, name, flops, size, scratch=(), out_specs=None, limit=FULL, alias=None):
     return pl.pallas_call(
         kernel,
         out_shape=[jax.ShapeDtypeStruct(s, d) for s, d in out],
         in_specs=specs,
         out_specs=out_specs or [VM] * len(out),
         scratch_shapes=list(scratch),
+        input_output_aliases=alias or {},
         compiler_params=pltpu.CompilerParams(vmem_limit_bytes=limit),
         cost_estimate=pl.CostEstimate(flops=flops, bytes_accessed=size, transcendentals=0),
         name=name,
@@ -307,18 +320,17 @@
     lines = [list(range(k, z_count, PARTS)) for k in range(PARTS)]
 
     dma = pltpu.SemaphoreType.DMA
-    count = rows * 4 // 256
     msg, codes = call(
         dispatch_kernel,
-        [((places * 8, half), BF), ((members, tok_rows), jnp.int32)],
+        [((experts, members, 8, half), BF), ((members, tok_rows), jnp.int32)],
         [SM] + [HB] * 3, "dispatch", 3 << 30, 4 << 20,
         scratch=[
             pltpu.VMEM((members, tok_rows), jnp.int32),
             pltpu.VMEM((tok_rows, width), BF),
             pltpu.VMEM((members, tok_rows, width), BF),
-            pltpu.VMEM((places * 8, half), BF),
+            pltpu.VMEM((experts, members, 8, half), BF),
             dma((3,)),
-            dma((places * 8 // 256,)),
+            dma((2,)),
         ],
         out_specs=[HB, VM],
     )(part_index, route_ids[:, :, 0], tokens, out_grad)
@@ -329,19 +341,31 @@
     column = lax.dynamic_slice(
         router, (lax.axis_index("member"), 0, lax.axis_index("dp")), (1, width, 1)
     ).reshape(1, width)
-    stride = 2 * rows + 16
-    share = stride - 1
-    sides = [pltpu.VMEM((rows * 4, half), BF)]
-    pair = [pltpu.VMEM((rows, width), BF)] * 2
-    part, pre_grad, scaled_act = call(
-        functools.partial(expert_kernel, stride),
-        [((z_count * share, 128), BF), ((rows, hidden), BF), ((rows, hidden), BF)],
-        [SM] + [HB] * 5 + [VM], "expert", 3 << 30, 8 << 20, limit=MOST,
-        scratch=sides
-        + [pltpu.VMEM((width, hidden), BF), pltpu.VMEM((hidden, width), BF)]
-        + pair
-        + [dma((count,)), dma((2,))],
-    )(part_index, *arrived, w_in[0, 0], w_out[0, 0], column)
+    stride = 2 * rows + 32
+    share = stride - 2
+    block = rows // PARTS
+
+    whole = ((z_count * share, 128), BF)
+    side = pltpu.VMEM((block, width), BF)
+    part, kept_own, router_own, first, second = call(
+        functools.partial(own_kernel, stride),
+        [
+            whole,
+            ((block, 2 * hidden), BF),
+            ((1, width), F32),
+            ((width, hidden), BF),
+            ((hidden, width), BF),
+        ],
+        [SM, VM, HB, HB, VM], "expert_own", 1 << 30, 6 << 20,
+        scratch=[side, side, dma((2,))], limit=MOST,
+    )(part_index, own, w_in[0, 0], w_out[0, 0], column)
+    sides = pltpu.VMEM((2, block, width), BF)
+    part, kept_rest = call(
+        functools.partial(rest_kernel, stride),
+        [whole, ((2 * block, 2 * hidden), BF)],
+        [SM] + [VM] * 7, "expert_rest", 2 << 30, 8 << 20,
+        scratch=[sides, sides], limit=MOST, alias={7: 0},
+    )(part_index, *arrived[1:], first, second, column, router_own, part)
     total = lax.psum_scatter(part, "expert", scatter_dimension=0, tiled=True)
     (back,) = call(
         functools.partial(return_kernel, rows),
@@ -349,7 +373,7 @@
         [SM, VM], "to_tokens", 1 << 28, 1 << 20,
         scratch=[pltpu.VMEM((-(-share // 128) * 128, 128), BF)],
         limit=LIMIT,
-    )(z.reshape(1), total)
+    )(2 * z.reshape(1), total)
     home = lax.all_to_all(
         back.reshape(places, 16, 128), plane, split_axis=0, concat_axis=0, tiled=True
     ).reshape(places * 16, 128)
@@ -357,8 +381,10 @@
         weight_kernel,
         [((width, hidden), BF), ((hidden, width), BF)],
         [HB] * 3 + [VM] * 2, "weights", 1 << 30, 6 << 20, limit=LESS,
-        scratch=sides + pair + [dma((count,))],
-    )(*arrived, pre_grad, scaled_act)
+        scratch=[pltpu.VMEM((rows * 4, half), BF)]
+        + [pltpu.VMEM((rows, width), BF)] * 2
+        + [dma((2 * PARTS,))],
+    )(*arrived, kept_own, kept_rest)
     (compact,) = call(
         collect_kernel,
         [(((members + 1) * tok_rows + places, 128), BF)],

time: 172 us -> 172 us (level)
  waiting for transfers between devices: 24.4 us -> 15.7 us
  blocking collectives: 102 us -> 107 us
  local copies, waits for them, and re-layouts: 2.42 us -> 6.72 us
    ppermute x1, waiting for transfers between devices: 13 us -> 1.43 us  [shards(): lax.ppermute(own, 'expert', behind)]
    unnamed x12 -> x20, local copies, waits for them, and re-layouts: 2.41 us -> 6.7 us
    ppermute x1, waiting for transfers between devices: 5.33 us -> 8.84 us  [shards(): lax.ppermute(own, 'expert', ahead)]
    unnamed x1, blocking collectives: 32.8 us -> 35.9 us
    all_gather x1, blocking collectives: 19.2 us -> 21.3 us  [shards(): line = lax.all_gather(compact, 'expert', axis_index_groups=lines)]
    ppermute x1, waiting for transfers between devices: 2.23 us -> 0.41 us  [shards(): lax.ppermute(line, 'expert', ahead)]
    pallas_call x2 -> x3, Pallas kernels: 10.8 us -> 9.28 us  [the longest x1 3.87 us: shards(): call(functools.partial(rest_kernel, stride), [whole, ((2 * block, 2 * hid...]
  transfers between devices with their start and end apart: 5 -> 5, of which waited for: 4 -> 4; matrix products, arithmetic and copies ran while one was open for 1% -> 1% of each run, Pallas kernels for 3% -> 4%
where the time goes in v4:
time: 172 us; the launch traced here: 171 us
  blocking collectives  107 us (62%)
  starting transfers between devices  23.4 us (14%)
  Pallas kernels  16.6 us (10%)
  waiting for transfers between devices  15.7 us (9%)
  local copies, waits for them, and re-layouts  6.72 us (4%)
    unnamed x1, blocking collectives  35.9 us
    all_to_all x1, blocking collectives, shards(): lax.all_to_all(msg.reshape(places, 8, half), plane, split_axis=0, concat_...  33.2 us
    all_gather x1, blocking collectives, shards(): line = lax.all_gather(compact, 'expert', axis_index_groups=lines)  21.3 us
    all_to_all x1, blocking collectives, shards(): lax.all_to_all(back.reshape(places, 16, 128), plane, split_axis=0, concat...  17 us
    ppermute x1, starting transfers between devices, shards(): lax.ppermute(own, 'expert', behind)  11.4 us
    ppermute x1, waiting for transfers between devices, shards(): lax.ppermute(own, 'expert', ahead)  8.84 us
    unnamed x20, local copies, waits for them, and re-layouts  6.7 us
    ppermute x1, waiting for transfers between devices, shards(): lax.ppermute(line, 'expert', behind)  4.98 us
  transfers between devices with their start and end apart: 5, of which 4 were waited for; matrix products, arithmetic and copies ran while one was open for 1% of the time, Pallas kernels for 4%

profile of v4, /device:TPU:6, one launch (start us, length us, event | category | flops | bytes accessed | tf_op | source)
XLA Modules:
  0.0 171.2 jit_solution(14940718872746225234)
XLA Ops:
  0.7 3.2 %dispatch.1 = (bf16[32,2,8,640]{3,2,1,0:T(8,128)(2,1)}, s32[2,128]{1,0:T(2,128)}) custom-call(s32[1]{0:T(128)} %bitcast.part_ref.index_ref, s32[2,128]{1,0:T(2,128)} %bitcast.35, bf16[128,1280]{1,0:T(8,128)(2,1)} %tok_hbm.1, bf16[2,128,1280]{2,1,0:T(8,128)(2,1)} %grad_hbm.1), custom_call_target="tpu_custom_call" | custom-call | flops 3221225472 | bytes 4194304 | tf_op jit(solution)/shard_map/dispatch/pallas_call | solution.py:323
  3.8 33.2 %all_to_all.10 = bf16[64,8,640]{2,1,0:T(8,128)(2,1)S(1)} all-to-all(bf16[64,8,640]{2,1,0:T(8,128)(2,1)} %bitcast.32), channel_id=1, replica_groups=mesh['dp'=32,'member'=2,'expert'=12] {'dp','member'}, dimensions={0} | all-to-all | bytes 1310720 | tf_op jit(solution)/shard_map/all_to_all | solution.py:337
  37.1 1.9 %collective-permute-start = (bf16[512,640]{1,0:T(8,128)(2,1)S(1)}, bf16[512,640]{1,0:T(8,128)(2,1)}, u32[]{:S(2)}, u32[]{:S(2)}) collective-permute-start(bf16[512,640]{1,0:T(8,128)(2,1)S(1)} %bitcast.24), channel_id=1, source_target_pairs={{0,1},{1,2},{2,3},{3,4},{4,5},{5,6},{6,7},{7,8},{8,9},{9,10},{10,1... | collective-permute-start | bytes 1966088 | tf_op jit(solution)/shard_map/ppermute | solution.py:340
  39.0 11.4 %collective-permute-start.1 = (bf16[512,640]{1,0:T(8,128)(2,1)S(1)}, bf16[512,640]{1,0:T(8,128)(2,1)}, u32[]{:S(2)}, u32[]{:S(2)}) collective-permute-start(bf16[512,640]{1,0:T(8,128)(2,1)S(1)} %bitcast.25), channel_id=1, source_target_pairs={{0,11},{1,0},{2,1},{3,2},{4,3},{5,4},{6,5},{7,6},{8,7},{9,8},{10,9... | collective-permute-start | bytes 1966088 | tf_op jit(solution)/shard_map/ppermute | solution.py:340
  50.5 1.2 copy-done.1
  51.7 1.2 copy-done.2
  52.9 2.3 %expert_own.1 = (bf16[9576,128]{1,0:T(8,128)(2,1)S(1)}, bf16[128,768]{1,0:T(8,128)(2,1)S(1)}, f32[1,1280]{1,0:T(1,128)S(1)}, bf16[1280,384]{1,0:T(8,128)(2,1)S(1)}, bf16[384,1280]{1,0:T(8,128)(2,1)S(1)}) custom-call(s32[1]{0:T(128)} %bitcast.part_ref.index_ref, bf16[512,640]{1,0:T(8,128)(2,1)S(1)} %bitcast.26, bf16[1280,384]{1,0:T(8,128)(2,1)S(1)} %bitcast.30, ...), custom_call_target="tpu_custom_call" | custom-call | flops 1073741824 | bytes 6291456 | tf_op jit(solution)/shard_map/expert_own/pallas_call | solution.py:350
  55.2 8.8 %collective-permute-done.up_ref.up_hbm = bf16[512,640]{1,0:T(8,128)(2,1)} collective-permute-done((bf16[512,640]{1,0:T(8,128)(2,1)S(1)}, bf16[512,640]{1,0:T(8,128)(2,1)}, u32[]{:S(2)}, u32[]{:S(2)}) %collective-permute-start) | collective-permute-done | bytes 655392 | tf_op jit(solution)/shard_map/ppermute | solution.py:340
  64.0 1.4 collective-permute-done.1.down_ref.down_hbm
  65.4 3.9 %expert_rest.1 = (bf16[9576,128]{1,0:T(8,128)(2,1)S(1)}, bf16[256,768]{1,0:T(8,128)(2,1)S(1)}) custom-call(s32[1]{0:T(128)} %bitcast.part_ref.index_ref, bf16[512,640]{1,0:T(8,128)(2,1)} %collective-permute-done.up_ref.up_hbm, bf16[512,640]{1,0:T(8,128)(2,1)} %collective-permute-done.1.down_ref.down_hbm, ...), custom_call_target="tpu_custom_call", output_to_operand_aliasing={{0}: (7, {})} | custom-call | flops 2147483648 | bytes 8388608 | tf_op jit(solution)/shard_map/expert_rest/pallas_call | solution.py:363
  69.3 0.7 copy-done.3
  70.1 35.9 %fusion = bf16[800,128]{1,0:T(8,128)(2,1)} fusion(bf16[9576,128]{1,0:T(8,128)(2,1)S(1)} %get-tuple-element.25), kind=kCustom, calls=%all-reduce-scatter | all-reduce-scatter fusion | flops 1228801 | bytes 2660352
  106.0 0.8 slice
  106.7 3.0 %collective-permute-start.4 = (bf16[22,128]{1,0:T(8,128)(2,1)S(1)}, bf16[22,128]{1,0:T(8,128)(2,1)S(1)}, u32[]{:S(2)}, u32[]{:S(2)}) collective-permute-start(bf16[22,128]{1,0:T(8,128)(2,1)S(1)} %slice), channel_id=1, source_target_pairs={{0,1},{1,2},{2,3},{3,4},{4,5},{5,6},{6,7},{7,8},{8,9},{9,10},{10,1... | collective-permute-start | bytes 16904
  109.7 1.3 dynamic-slice.4
  111.7 1.4 concatenate
  113.2 0.8 to_tokens.1
  114.0 17.0 %all_to_all.11 = bf16[64,16,128]{2,1,0:T(8,128)(2,1)S(1)} all-to-all(bf16[64,16,128]{2,1,0:T(8,128)(2,1)S(1)} %bitcast.29), channel_id=1, replica_groups=mesh['dp'=32,'member'=2,'expert'=12] {'dp','member'}, dimensions={0} | all-to-all | bytes 524288 | tf_op jit(solution)/shard_map/all_to_all | solution.py:377
  131.6 21.3 %all-gather = bf16[1792,128]{1,0:T(8,128)(2,1)S(1)} all-gather(bf16[448,128]{1,0:T(8,128)(2,1)S(1)} %collect.1), channel_id=2, replica_groups={{0,3,6,9},{1,4,7,10},{2,5,8,11},{12,15,18,21},{13,16,19,22},{14,17,20,2..., dimensions={0}, use_global_device_ids=true | all-gather | bytes 573440 | tf_op jit(solution)/shard_map/all_gather | solution.py:393
  152.9 2.7 %collective-permute-start.2 = (bf16[4,448,128]{2,1,0:T(8,128)(2,1)S(1)}, bf16[4,448,128]{2,1,0:T(8,128)(2,1)S(1)}, u32[]{:S(2)}, u32[]{:S(2)}) collective-permute-start(bf16[4,448,128]{2,1,0:T(8,128)(2,1)S(1)} %bitcast.21), channel_id=1, source_target_pairs={{0,1},{1,2},{2,3},{3,4},{4,5},{5,6},{6,7},{7,8},{8,9},{9,10},{10,1... | collective-permute-start | bytes 1376264 | tf_op jit(solution)/shard_map/ppermute | solution.py:401
  155.6 4.3 %collective-permute-start.3 = (bf16[4,448,128]{2,1,0:T(8,128)(2,1)S(1)}, bf16[4,448,128]{2,1,0:T(8,128)(2,1)S(1)}, u32[]{:S(2)}, u32[]{:S(2)}) collective-permute-start(bf16[4,448,128]{2,1,0:T(8,128)(2,1)S(1)} %bitcast.22), channel_id=1, source_target_pairs={{0,11},{1,0},{2,1},{3,2},{4,3},{5,4},{6,5},{7,6},{8,7},{9,8},{10,9... | collective-permute-start | bytes 1376264 | tf_op jit(solution)/shard_map/ppermute | solution.py:402
  159.9 4.5 %weights.1 = (bf16[1280,384]{1,0:T(8,128)(2,1)}, bf16[384,1280]{1,0:T(8,128)(2,1)}) custom-call(bf16[512,640]{1,0:T(8,128)(2,1)S(1)} %bitcast.27, bf16[512,640]{1,0:T(8,128)(2,1)} %collective-permute-done.up_ref.up_hbm, bf16[512,640]{1,0:T(8,128)(2,1)} %collective-permute-done.1.down_ref.down_hbm, bf16[128,768]{1,0:T(8,128)(2,1)S(1)} %copy-done.6, ...), custom_call_target="tpu_custom_call" | custom-call | flops 1073741824 | bytes 6291456 | tf_op jit(solution)/shard_map/weights/pallas_call | solution.py:380
  164.9 5.0 %collective-permute-done.3.down_ref = bf16[4,448,128]{2,1,0:T(8,128)(2,1)S(1)} collective-permute-done((bf16[4,448,128]{2,1,0:T(8,128)(2,1)S(1)}, bf16[4,448,128]{2,1,0:T(8,128)(2,1)S(1)}, u32[]{:S(2)}, u32[]{:S(2)}) %collective-permute-start.3) | collective-permute-done | bytes 458784 | tf_op jit(solution)/shard_map/ppermute | solution.py:402
  169.9 1.4 final.1
  (18 shorter events, 1.2 us)
Async XLA Ops:
  0.6 49.8 %copy-start = (f32[2,1280,32]{1,2,0:T(8,128)S(1)}, f32[2,1280,32]{1,2,0:T(8,128)}, u32[]{:S(2)}) copy-start(f32[2,1280,32]{1,2,0:T(8,128)} %param.8) | copy-start | bytes 983044
  37.1 26.9 %collective-permute-start = (bf16[512,640]{1,0:T(8,128)(2,1)S(1)}, bf16[512,640]{1,0:T(8,128)(2,1)}, u32[]{:S(2)}, u32[]{:S(2)}) collective-permute-start(bf16[512,640]{1,0:T(8,128)(2,1)S(1)} %bitcast.24), channel_id=1, source_target_pairs={{0,1},{1,2},{2,3},{3,4},{4,5},{5,6},{6,7},{7,8},{8,9},{9,10},{10,1... | collective-permute-start | bytes 1966088 | tf_op jit(solution)/shard_map/ppermute | solution.py:340
  39.0 26.5 %collective-permute-start.1 = (bf16[512,640]{1,0:T(8,128)(2,1)S(1)}, bf16[512,640]{1,0:T(8,128)(2,1)}, u32[]{:S(2)}, u32[]{:S(2)}) collective-permute-start(bf16[512,640]{1,0:T(8,128)(2,1)S(1)} %bitcast.25), channel_id=1, source_target_pairs={{0,11},{1,0},{2,1},{3,2},{4,3},{5,4},{6,5},{7,6},{8,7},{9,8},{10,9... | collective-permute-start | bytes 1966088 | tf_op jit(solution)/shard_map/ppermute | solution.py:340
  50.5 1.2 copy-start.1
  51.7 1.2 copy-start.2
  55.1 14.2 %copy-start.5 = (bf16[128,768]{1,0:T(8,128)(2,1)}, bf16[128,768]{1,0:T(8,128)(2,1)S(1)}, u32[]{:S(2)}) copy-start(bf16[128,768]{1,0:T(8,128)(2,1)S(1)} %get-tuple-element.28.own_ref) | copy-start | bytes 589828
  69.3 0.7 copy-start.3
  70.1 60.9 %copy-start.7 = (s32[2,128]{1,0:T(2,128)S(1)}, s32[2,128]{1,0:T(2,128)}, u32[]{:S(2)}) copy-start(s32[2,128]{1,0:T(2,128)} %get-tuple-element.19.code_ref) | copy-start | bytes 3076
  106.0 54.0 %copy-start.4 = (bf16[256,768]{1,0:T(8,128)(2,1)S(1)}, bf16[256,768]{1,0:T(8,128)(2,1)}, u32[]{:S(2)}) copy-start(bf16[256,768]{1,0:T(8,128)(2,1)} %copy-done.3) | copy-start | bytes 1179652
  106.0 54.0 %copy-start.6 = (bf16[128,768]{1,0:T(8,128)(2,1)S(1)}, bf16[128,768]{1,0:T(8,128)(2,1)}, u32[]{:S(2)}) copy-start(bf16[128,768]{1,0:T(8,128)(2,1)} %copy-done.5) | copy-start | bytes 589828
  106.7 5.0 %collective-permute-start.4 = (bf16[22,128]{1,0:T(8,128)(2,1)S(1)}, bf16[22,128]{1,0:T(8,128)(2,1)S(1)}, u32[]{:S(2)}, u32[]{:S(2)}) collective-permute-start(bf16[22,128]{1,0:T(8,128)(2,1)S(1)} %slice), channel_id=1, source_target_pairs={{0,1},{1,2},{2,3},{3,4},{4,5},{5,6},{6,7},{7,8},{8,9},{9,10},{10,1... | collective-permute-start | bytes 16904
  152.9 12.0 %collective-permute-start.2 = (bf16[4,448,128]{2,1,0:T(8,128)(2,1)S(1)}, bf16[4,448,128]{2,1,0:T(8,128)(2,1)S(1)}, u32[]{:S(2)}, u32[]{:S(2)}) collective-permute-start(bf16[4,448,128]{2,1,0:T(8,128)(2,1)S(1)} %bitcast.21), channel_id=1, source_target_pairs={{0,1},{1,2},{2,3},{3,4},{4,5},{5,6},{6,7},{7,8},{8,9},{9,10},{10,1... | collective-permute-start | bytes 1376264 | tf_op jit(solution)/shard_map/ppermute | solution.py:401
  155.6 14.3 %collective-permute-start.3 = (bf16[4,448,128]{2,1,0:T(8,128)(2,1)S(1)}, bf16[4,448,128]{2,1,0:T(8,128)(2,1)S(1)}, u32[]{:S(2)}, u32[]{:S(2)}) collective-permute-start(bf16[4,448,128]{2,1,0:T(8,128)(2,1)S(1)} %bitcast.22), channel_id=1, source_target_pairs={{0,11},{1,0},{2,1},{3,2},{4,3},{5,4},{6,5},{7,6},{8,7},{9,8},{10,9... | collective-permute-start | bytes 1376264 | tf_op jit(solution)/shard_map/ppermute | solution.py:402

commit v5 on v4

--- a/solution.py
+++ b/solution.py
@@ -13,7 +13,7 @@
 cubic_term = 0.044715
 LIMIT = 44 << 20
 FULL = 60 << 20
-MOST = 44 << 20
+MOST = 50 << 20
 LESS = 24 << 20
 PARTS = 3
 VM = pl.BlockSpec(memory_space=pltpu.VMEM)
@@ -126,62 +126,67 @@
     return jnp.where(part >= PARTS, part - PARTS, part)
 
 
-def expert_rows(x, g, first, second, router):
+def expert_block(shift, b, stride, index_ref, msg_ref, weights, router_ref, refs, stores):
+    part_hbm, kept_ref, x_ref, g_ref, stage_ref, sem = refs
+    block, width = x_ref.shape
+    rows = PARTS * block
+    chunks = width // 128
+    sort = sorting()
+    for k in range(2):
+        unpack(sort, msg_ref, k, x_ref, g_ref)
+    x, g, router = x_ref[...], g_ref[...], router_ref[...]
+    place = wrap(index_ref[0] + shift) * block
+
+    def send(value, k):
+        for c in range(chunks):
+            at = (b * 2 + k) * chunks + c
+            staged = pl.ds(at * block, block)
+            stage_ref[staged, :] = value[:, c * 128 : (c + 1) * 128]
+            there = pl.ds(pl.multiple_of(place + c * stride + k * rows, 16), block)
+            stores.append(
+                pltpu.make_async_copy(stage_ref.at[staged], part_hbm.at[there], sem.at[at])
+            )
+            stores[-1].start()
+
     xf = x.astype(F32)
     logit = jnp.sum(xf * router, axis=1, keepdims=True)
     gate = 1.0 / (1.0 + jnp.exp(-logit))
+    first, second = weights()
     pre = jnp.dot(x, first, preferred_element_type=F32)
-    hidden = nt(g, second)
+    hidden_grad = nt(g, second)
     tanh_value = jnp.tanh(tanh_scale * (pre + cubic_term * pre * pre * pre))
     act = 0.5 * pre * (1.0 + tanh_value)
+    scaled_act = (act * gate).astype(BF)
+    send(jnp.dot(scaled_act, second, preferred_element_type=F32).astype(BF), 0)
     slope = 0.5 * (1.0 + tanh_value) + 0.5 * pre * (
         1.0 - tanh_value * tanh_value
     ) * tanh_scale * (1.0 + 3.0 * cubic_term * pre * pre)
-    gate_grad = jnp.sum(act * hidden, axis=1, keepdims=True)
+    gate_grad = jnp.sum(act * hidden_grad, axis=1, keepdims=True)
     logit_grad = gate_grad * gate * (1.0 - gate)
-    pre_grad = (hidden * gate * slope).astype(BF)
-    scaled_act = (act * gate).astype(BF)
-    router_sum = jnp.sum(xf * logit_grad, axis=0, keepdims=True)
-    out = jnp.dot(scaled_act, second, preferred_element_type=F32).astype(BF)
-    dx = (nt(pre_grad, first) + logit_grad * router).astype(BF)
-    return pre_grad, scaled_act, router_sum, out, dx
-
-
-def expert_block(shift, b, stride, index_ref, msg_ref, weights, router_ref, refs):
-    part_ref, kept_ref, x_ref, g_ref = refs
-    rows = PARTS * x_ref.shape[0]
-    block, width = x_ref.shape
-    sort = sorting()
-    for k in range(2):
-        unpack(sort, msg_ref, k, x_ref, g_ref)
-    pre_grad, scaled_act, extra, out, dx = expert_rows(
-        x_ref[...], g_ref[...], *weights(), router_ref[...]
-    )
+    pre_grad = (hidden_grad * gate * slope).astype(BF)
+    send((nt(pre_grad, first) + logit_grad * router).astype(BF), 1)
     here = pl.ds(b * block, block)
-    kept_ref[here, 0 : pre_grad.shape[1]] = pre_grad
-    kept_ref[here, pre_grad.shape[1] :] = scaled_act
-    place = wrap(index_ref[0] + shift) * block
-    for c in range(width // 128):
-        lanes = slice(c * 128, (c + 1) * 128)
-        for k, value in enumerate((out, dx)):
-            there = pl.ds(pl.multiple_of(place + c * stride + k * rows, 16), block)
-            part_ref[there, :] = value[:, lanes]
-    return extra
+    hidden = pre_grad.shape[1]
+    kept_ref[here, 0:hidden] = pre_grad
+    kept_ref[here, hidden:] = scaled_act
+    return jnp.sum(xf * logit_grad, axis=0, keepdims=True)
 
 
 def own_kernel(
     stride, index_ref, msg_ref, first_hbm, second_hbm, router_ref,
-    part_ref, kept_ref, sum_ref, first_ref, second_ref, x_ref, g_ref, sem,
+    part_hbm, kept_ref, sum_ref, first_ref, second_ref,
+    x_ref, g_ref, stage_ref, zero_ref, sem, load_sem, zero_sem,
 ):
     loads = [
-        pltpu.make_async_copy(first_hbm, first_ref, sem.at[0]),
-        pltpu.make_async_copy(second_hbm, second_ref, sem.at[1]),
+        pltpu.make_async_copy(first_hbm, first_ref, load_sem.at[0]),
+        pltpu.make_async_copy(second_hbm, second_ref, load_sem.at[1]),
     ]
     for load in loads:
         load.start()
-    used = x_ref.shape[1] // 128 * stride
-    left = part_ref.shape[0] - used
-    part_ref[pl.ds(used, left), :] = jnp.zeros((left, 128), BF)
+    zero_ref[...] = jnp.zeros(zero_ref.shape, BF)
+    there = pl.ds(x_ref.shape[1] // 128 * stride, zero_ref.shape[0])
+    stores = [pltpu.make_async_copy(zero_ref, part_hbm.at[there], zero_sem)]
+    stores[0].start()
 
     def weights():
         for load in loads:
@@ -190,27 +195,38 @@
 
     sum_ref[...] = expert_block(
         0, 0, stride, index_ref, msg_ref, weights, router_ref,
-        (part_ref, kept_ref, x_ref, g_ref),
-    )
+        (part_hbm, kept_ref, x_ref, g_ref, stage_ref, sem), stores,
+    )
+    for store in stores:
+        store.wait()
 
 
 def rest_kernel(
     stride, index_ref, up_ref, down_ref, first_ref, second_ref, router_ref, before_ref, _,
-    part_ref, kept_ref, x_ref, g_ref,
+    part_hbm, kept_ref, x_ref, g_ref, stage_ref, tail_ref, sem, tail_sem,
 ):
     rows = PARTS * x_ref.shape[1]
     router_sum = before_ref[...]
+    stores = []
     for b, (shift, msg_ref) in enumerate(((2, up_ref), (1, down_ref))):
         router_sum = router_sum + expert_block(
             shift, b, stride, index_ref, msg_ref,
             lambda: (first_ref[...], second_ref[...]), router_ref,
-            (part_ref, kept_ref, x_ref.at[b], g_ref.at[b]),
+            (part_hbm, kept_ref, x_ref.at[b], g_ref.at[b], stage_ref, sem), stores,
         )
     tail = stride - 2 * rows
     for c in range(x_ref.shape[2] // 128):
         lanes = slice(c * 128, (c + 1) * 128)
         row = jnp.where(iota((tail, 128), 0) == 0, router_sum[:, lanes], 0.0)
-        part_ref[pl.ds(c * stride + 2 * rows, tail), :] = row.astype(BF)
+        staged = pl.ds(c * tail, tail)
+        tail_ref[staged, :] = row.astype(BF)
+        there = pl.ds(c * stride + 2 * rows, tail)
+        stores.append(
+            pltpu.make_async_copy(tail_ref.at[staged], part_hbm.at[there], tail_sem.at[c])
+        )
+        stores[-1].start()
+    for store in stores:
+        store.wait()
 
 
 def weight_kernel(
@@ -344,7 +360,7 @@
     stride = 2 * rows + 32
     share = stride - 2
     block = rows // PARTS
-
+    chunks = width // 128
     whole = ((z_count * share, 128), BF)
     side = pltpu.VMEM((block, width), BF)
     part, kept_own, router_own, first, second = call(
@@ -357,14 +373,31 @@
             ((hidden, width), BF),
         ],
         [SM, VM, HB, HB, VM], "expert_own", 1 << 30, 6 << 20,
-        scratch=[side, side, dma((2,))], limit=MOST,
+        scratch=[
+            side,
+            side,
+            pltpu.VMEM((2 * chunks * block, 128), BF),
+            pltpu.VMEM((z_count * share - chunks * stride, 128), BF),
+            dma((2 * chunks,)),
+            dma((2,)),
+            dma(()),
+        ],
+        out_specs=[HB] + [VM] * 4, limit=MOST,
     )(part_index, own, w_in[0, 0], w_out[0, 0], column)
     sides = pltpu.VMEM((2, block, width), BF)
     part, kept_rest = call(
         functools.partial(rest_kernel, stride),
         [whole, ((2 * block, 2 * hidden), BF)],
-        [SM] + [VM] * 7, "expert_rest", 2 << 30, 8 << 20,
-        scratch=[sides, sides], limit=MOST, alias={7: 0},
+        [SM] + [VM] * 6 + [HB], "expert_rest", 2 << 30, 8 << 20,
+        scratch=[
+            sides,
+            sides,
+            pltpu.VMEM((4 * chunks * block, 128), BF),
+            pltpu.VMEM((chunks * (stride - 2 * rows), 128), BF),
+            dma((4 * chunks,)),
+            dma((chunks,)),
+        ],
+        out_specs=[HB, VM], limit=MOST, alias={7: 0},
     )(part_index, *arrived[1:], first, second, column, router_own, part)
     total = lax.psum_scatter(part, "expert", scatter_dimension=0, tiled=True)
     (back,) = call(

time: 172 us -> 170 us (0.988)
  local copies, waits for them, and re-layouts: 6.72 us -> 2.43 us
    unnamed x20 -> x10, local copies, waits for them, and re-layouts: 6.7 us -> 2.42 us
  transfers between devices with their start and end apart: 5 -> 5, of which waited for: 4 -> 4; matrix products, arithmetic and copies ran while one was open for 1% -> 1% of each run, Pallas kernels for 4% -> 5%
where the time goes in v5:
time: 170 us; the launch traced here: 169 us
  blocking collectives  107 us (63%)
  starting transfers between devices  23.6 us (14%)
  Pallas kernels  18.1 us (11%)
  waiting for transfers between devices  16.5 us (10%)
  local copies, waits for them, and re-layouts  2.43 us (1%)
    unnamed x1, blocking collectives  35.7 us
    all_to_all x1, blocking collectives, shards(): lax.all_to_all(msg.reshape(places, 8, half), plane, split_axis=0, concat_...  33.2 us
    all_gather x1, blocking collectives, shards(): line = lax.all_gather(compact, 'expert', axis_index_groups=lines)  21.3 us
    all_to_all x1, blocking collectives, shards(): lax.all_to_all(back.reshape(places, 16, 128), plane, split_axis=0, concat...  17 us
    ppermute x1, starting transfers between devices, shards(): lax.ppermute(own, 'expert', behind)  11.4 us
    ppermute x1, waiting for transfers between devices, shards(): lax.ppermute(own, 'expert', ahead)  9.79 us
    ppermute x1, waiting for transfers between devices, shards(): lax.ppermute(line, 'expert', behind)  4.97 us
    pallas_call x1, Pallas kernels, shards(): call(weight_kernel, [((width, hidden), BF), ((hidden, width), BF)], [HB]...  4.64 us
  transfers between devices with their start and end apart: 5, of which 4 were waited for; matrix products, arithmetic and copies ran while one was open for 1% of the time, Pallas kernels for 5%

profile of v5, /device:TPU:6, one launch (start us, length us, event | category | flops | bytes accessed | tf_op | source)
XLA Modules:
  0.0 169.2 jit_solution(6745984851018717041)
XLA Ops:
  0.6 0.0 copy-start
  0.7 3.2 %dispatch.1 = (bf16[32,2,8,640]{3,2,1,0:T(8,128)(2,1)}, s32[2,128]{1,0:T(2,128)}) custom-call(s32[1]{0:T(128)} %bitcast.part_ref.index_ref, s32[2,128]{1,0:T(2,128)} %bitcast.35, bf16[128,1280]{1,0:T(8,128)(2,1)} %tok_hbm.1, bf16[2,128,1280]{2,1,0:T(8,128)(2,1)} %grad_hbm.1), custom_call_target="tpu_custom_call" | custom-call | flops 3221225472 | bytes 4194304 | tf_op jit(solution)/shard_map/dispatch/pallas_call | solution.py:339
  3.9 33.2 %all_to_all.10 = bf16[64,8,640]{2,1,0:T(8,128)(2,1)S(1)} all-to-all(bf16[64,8,640]{2,1,0:T(8,128)(2,1)} %bitcast.31), channel_id=1, replica_groups=mesh['dp'=32,'member'=2,'expert'=12] {'dp','member'}, dimensions={0} | all-to-all | bytes 1310720 | tf_op jit(solution)/shard_map/all_to_all | solution.py:353
  37.1 1.9 %collective-permute-start = (bf16[512,640]{1,0:T(8,128)(2,1)S(1)}, bf16[512,640]{1,0:T(8,128)(2,1)S(1)}, u32[]{:S(2)}, u32[]{:S(2)}) collective-permute-start(bf16[512,640]{1,0:T(8,128)(2,1)S(1)} %bitcast.24), channel_id=1, source_target_pairs={{0,1},{1,2},{2,3},{3,4},{4,5},{5,6},{6,7},{7,8},{8,9},{9,10},{10,1... | collective-permute-start | bytes 1966088 | tf_op jit(solution)/shard_map/ppermute | solution.py:356
  39.0 11.4 %collective-permute-start.1 = (bf16[512,640]{1,0:T(8,128)(2,1)S(1)}, bf16[512,640]{1,0:T(8,128)(2,1)S(1)}, u32[]{:S(2)}, u32[]{:S(2)}) collective-permute-start(bf16[512,640]{1,0:T(8,128)(2,1)S(1)} %bitcast.25), channel_id=1, source_target_pairs={{0,11},{1,0},{2,1},{3,2},{4,3},{5,4},{6,5},{7,6},{8,7},{9,8},{10,9... | collective-permute-start | bytes 1966088 | tf_op jit(solution)/shard_map/ppermute | solution.py:356
  50.5 3.6 %expert_own.1 = (bf16[9576,128]{1,0:T(8,128)(2,1)}, bf16[128,768]{1,0:T(8,128)(2,1)S(1)}, f32[1,1280]{1,0:T(1,128)S(1)}, bf16[1280,384]{1,0:T(8,128)(2,1)S(1)}, bf16[384,1280]{1,0:T(8,128)(2,1)S(1)}) custom-call(s32[1]{0:T(128)} %bitcast.part_ref.index_ref, bf16[512,640]{1,0:T(8,128)(2,1)S(1)} %bitcast.26, bf16[1280,384]{1,0:T(8,128)(2,1)S(1)} %bitcast.30, ...), custom_call_target="tpu_custom_call" | custom-call | flops 1073741824 | bytes 6291456 | tf_op jit(solution)/shard_map/expert_own/pallas_call | solution.py:366
  54.2 9.8 %collective-permute-done.up_ref.up_hbm = bf16[512,640]{1,0:T(8,128)(2,1)S(1)} collective-permute-done((bf16[512,640]{1,0:T(8,128)(2,1)S(1)}, bf16[512,640]{1,0:T(8,128)(2,1)S(1)}, u32[]{:S(2)}, u32[]{:S(2)}) %collective-permute-start) | collective-permute-done | bytes 655392 | tf_op jit(solution)/shard_map/ppermute | solution.py:356
  64.0 1.5 collective-permute-done.1.down_ref.down_hbm
  65.5 3.8 %expert_rest.1 = (bf16[9576,128]{1,0:T(8,128)(2,1)}, bf16[256,768]{1,0:T(8,128)(2,1)S(1)}) custom-call(s32[1]{0:T(128)} %bitcast.part_ref.index_ref, bf16[512,640]{1,0:T(8,128)(2,1)S(1)} %collective-permute-done.up_ref.up_hbm, bf16[512,640]{1,0:T(8,128)(2,1)S(1)} %collective-permute-done.1.down_ref.down_hbm, ...), custom_call_target="tpu_custom_call", output_to_operand_aliasing={{0}: (7, {})} | custom-call | flops 2147483648 | bytes 8388608 | tf_op jit(solution)/shard_map/expert_rest/pallas_call | solution.py:388
  69.3 35.7 %fusion = bf16[800,128]{1,0:T(8,128)(2,1)S(1)} fusion(bf16[9576,128]{1,0:T(8,128)(2,1)} %get-tuple-element.25), kind=kCustom, calls=%all-reduce-scatter | all-reduce-scatter fusion | flops 1228801 | bytes 2660352
  105.0 3.0 %collective-permute-start.4 = (bf16[22,128]{1,0:T(8,128)(2,1)S(1)}, bf16[22,128]{1,0:T(8,128)(2,1)S(1)}, u32[]{:S(2)}, u32[]{:S(2)}) collective-permute-start(bf16[22,128]{1,0:T(8,128)(2,1)S(1)} %slice), channel_id=1, source_target_pairs={{0,1},{1,2},{2,3},{3,4},{4,5},{5,6},{6,7},{7,8},{8,9},{9,10},{10,1... | collective-permute-start | bytes 16904
  108.0 1.3 dynamic-slice.4
  110.0 1.1 concatenate
  111.0 0.1 constant_dynamic-slice_fusion.sum_ref
  111.1 0.8 to_tokens.1
  111.9 17.0 %all_to_all.11 = bf16[64,16,128]{2,1,0:T(8,128)(2,1)S(1)} all-to-all(bf16[64,16,128]{2,1,0:T(8,128)(2,1)S(1)} %bitcast.29), channel_id=1, replica_groups=mesh['dp'=32,'member'=2,'expert'=12] {'dp','member'}, dimensions={0} | all-to-all | bytes 524288 | tf_op jit(solution)/shard_map/all_to_all | solution.py:410
  128.9 0.6 collect.1
  129.5 21.3 %all-gather = bf16[1792,128]{1,0:T(8,128)(2,1)S(1)} all-gather(bf16[448,128]{1,0:T(8,128)(2,1)S(1)} %collect.1), channel_id=2, replica_groups={{0,3,6,9},{1,4,7,10},{2,5,8,11},{12,15,18,21},{13,16,19,22},{14,17,20,2..., dimensions={0}, use_global_device_ids=true | all-gather | bytes 573440 | tf_op jit(solution)/shard_map/all_gather | solution.py:426
  150.8 2.7 %collective-permute-start.2 = (bf16[4,448,128]{2,1,0:T(8,128)(2,1)S(1)}, bf16[4,448,128]{2,1,0:T(8,128)(2,1)S(1)}, u32[]{:S(2)}, u32[]{:S(2)}) collective-permute-start(bf16[4,448,128]{2,1,0:T(8,128)(2,1)S(1)} %bitcast.21), channel_id=1, source_target_pairs={{0,1},{1,2},{2,3},{3,4},{4,5},{5,6},{6,7},{7,8},{8,9},{9,10},{10,1... | collective-permute-start | bytes 1376264 | tf_op jit(solution)/shard_map/ppermute | solution.py:434
  153.5 4.6 %collective-permute-start.3 = (bf16[4,448,128]{2,1,0:T(8,128)(2,1)S(1)}, bf16[4,448,128]{2,1,0:T(8,128)(2,1)S(1)}, u32[]{:S(2)}, u32[]{:S(2)}) collective-permute-start(bf16[4,448,128]{2,1,0:T(8,128)(2,1)S(1)} %bitcast.22), channel_id=1, source_target_pairs={{0,11},{1,0},{2,1},{3,2},{4,3},{5,4},{6,5},{7,6},{8,7},{9,8},{10,9... | collective-permute-start | bytes 1376264 | tf_op jit(solution)/shard_map/ppermute | solution.py:435
  158.0 4.6 %weights.1 = (bf16[1280,384]{1,0:T(8,128)(2,1)}, bf16[384,1280]{1,0:T(8,128)(2,1)}) custom-call(bf16[512,640]{1,0:T(8,128)(2,1)S(1)} %bitcast.27, bf16[512,640]{1,0:T(8,128)(2,1)S(1)} %collective-permute-done.up_ref.up_hbm, bf16[512,640]{1,0:T(8,128)(2,1)S(1)} %collective-permute-done.1.down_ref.down_hbm, bf16[128,768]{1,0:T(8,128)(2,1)S(1)} %get-tuple-element.28.own_ref, ...), custom_call_target="tpu_custom_call" | custom-call | flops 1073741824 | bytes 6291456 | tf_op jit(solution)/shard_map/weights/pallas_call | solution.py:413
  162.7 0.2 collective-permute-done.2.up_ref
  162.8 5.0 %collective-permute-done.3.down_ref = bf16[4,448,128]{2,1,0:T(8,128)(2,1)S(1)} collective-permute-done((bf16[4,448,128]{2,1,0:T(8,128)(2,1)S(1)}, bf16[4,448,128]{2,1,0:T(8,128)(2,1)S(1)}, u32[]{:S(2)}, u32[]{:S(2)}) %collective-permute-start.3) | collective-permute-done | bytes 458784 | tf_op jit(solution)/shard_map/ppermute | solution.py:435
  167.8 1.4 final.1
  (8 shorter events, 0.0 us)
Async XLA Ops:
  0.6 49.9 %copy-start = (f32[2,1280,32]{1,2,0:T(8,128)S(1)}, f32[2,1280,32]{1,2,0:T(8,128)}, u32[]{:S(2)}) copy-start(f32[2,1280,32]{1,2,0:T(8,128)} %param.8) | copy-start | bytes 983044
  0.7 49.9 %copy-start.1 = (bf16[1,1,1280,384]{3,2,1,0:T(8,128)(2,1)S(1)}, bf16[1,1,1280,384]{3,2,1,0:T(8,128)(2,1)}, u32[]{:S(2)}) copy-start(bf16[1,1,1280,384]{3,2,1,0:T(8,128)(2,1)} %param.9) | copy-start | bytes 2949124
  37.1 26.8 %collective-permute-start = (bf16[512,640]{1,0:T(8,128)(2,1)S(1)}, bf16[512,640]{1,0:T(8,128)(2,1)S(1)}, u32[]{:S(2)}, u32[]{:S(2)}) collective-permute-start(bf16[512,640]{1,0:T(8,128)(2,1)S(1)} %bitcast.24), channel_id=1, source_target_pairs={{0,1},{1,2},{2,3},{3,4},{4,5},{5,6},{6,7},{7,8},{8,9},{9,10},{10,1... | collective-permute-start | bytes 1966088 | tf_op jit(solution)/shard_map/ppermute | solution.py:356
  39.0 26.5 %collective-permute-start.1 = (bf16[512,640]{1,0:T(8,128)(2,1)S(1)}, bf16[512,640]{1,0:T(8,128)(2,1)S(1)}, u32[]{:S(2)}, u32[]{:S(2)}) collective-permute-start(bf16[512,640]{1,0:T(8,128)(2,1)S(1)} %bitcast.25), channel_id=1, source_target_pairs={{0,11},{1,0},{2,1},{3,2},{4,3},{5,4},{6,5},{7,6},{8,7},{9,8},{10,9... | collective-permute-start | bytes 1966088 | tf_op jit(solution)/shard_map/ppermute | solution.py:356
  69.3 59.6 %copy-start.2 = (s32[2,128]{1,0:T(2,128)S(1)}, s32[2,128]{1,0:T(2,128)}, u32[]{:S(2)}) copy-start(s32[2,128]{1,0:T(2,128)} %get-tuple-element.19.code_ref) | copy-start | bytes 3076
  105.0 5.0 %collective-permute-start.4 = (bf16[22,128]{1,0:T(8,128)(2,1)S(1)}, bf16[22,128]{1,0:T(8,128)(2,1)S(1)}, u32[]{:S(2)}, u32[]{:S(2)}) collective-permute-start(bf16[22,128]{1,0:T(8,128)(2,1)S(1)} %slice), channel_id=1, source_target_pairs={{0,1},{1,2},{2,3},{3,4},{4,5},{5,6},{6,7},{7,8},{8,9},{9,10},{10,1... | collective-permute-start | bytes 16904
  150.8 12.0 %collective-permute-start.2 = (bf16[4,448,128]{2,1,0:T(8,128)(2,1)S(1)}, bf16[4,448,128]{2,1,0:T(8,128)(2,1)S(1)}, u32[]{:S(2)}, u32[]{:S(2)}) collective-permute-start(bf16[4,448,128]{2,1,0:T(8,128)(2,1)S(1)} %bitcast.21), channel_id=1, source_target_pairs={{0,1},{1,2},{2,3},{3,4},{4,5},{5,6},{6,7},{7,8},{8,9},{9,10},{10,1... | collective-permute-start | bytes 1376264 | tf_op jit(solution)/shard_map/ppermute | solution.py:434
  153.5 14.3 %collective-permute-start.3 = (bf16[4,448,128]{2,1,0:T(8,128)(2,1)S(1)}, bf16[4,448,128]{2,1,0:T(8,128)(2,1)S(1)}, u32[]{:S(2)}, u32[]{:S(2)}) collective-permute-start(bf16[4,448,128]{2,1,0:T(8,128)(2,1)S(1)} %bitcast.22), channel_id=1, source_target_pairs={{0,11},{1,0},{2,1},{3,2},{4,3},{5,4},{6,5},{7,6},{8,7},{9,8},{10,9... | collective-permute-start | bytes 1376264 | tf_op jit(solution)/shard_map/ppermute | solution.py:435

commit v6 on v5

--- a/solution.py
+++ b/solution.py
@@ -41,7 +41,12 @@
     loads = [
         pltpu.make_async_copy(src, dst, sem.at[k])
         for k, (src, dst) in enumerate(
-            ((ids_hbm, ids_ref), (tok_hbm, tok_ref), (grad_hbm, grad_ref))
+            (
+                (ids_hbm, ids_ref),
+                (tok_hbm, tok_ref),
+                (grad_hbm.at[0], grad_ref.at[0]),
+                (grad_hbm.at[1], grad_ref.at[1]),
+            )
         )
     ]
     for load in loads:
@@ -59,10 +64,10 @@
         code_ref[m : m + 1, :] = code
         codes.append(code)
     loads[1].wait()
-    loads[2].wait()
     token = tok_ref[...]
     stores = []
     for m in range(2):
+        loads[2 + m].wait()
         grad = grad_ref[m]
         side = jnp.concatenate(
             [token[:, :half], token[:, half:], grad[:, :half], grad[:, half:]], axis=0
@@ -126,27 +131,30 @@
     return jnp.where(part >= PARTS, part - PARTS, part)
 
 
-def expert_block(shift, b, stride, index_ref, msg_ref, weights, router_ref, refs, stores):
+def expert_block(rows, stride, index_ref, messages, weights, router_ref, refs, stores):
     part_hbm, kept_ref, x_ref, g_ref, stage_ref, sem = refs
-    block, width = x_ref.shape
-    rows = PARTS * block
-    chunks = width // 128
+    block = rows // PARTS
+    chunks = x_ref.shape[1] // 128
     sort = sorting()
-    for k in range(2):
-        unpack(sort, msg_ref, k, x_ref, g_ref)
+    for n, (_, msg_ref) in enumerate(messages):
+        for k in range(2):
+            unpack(sort, msg_ref, k, x_ref.at[pl.ds(n * block, block)], g_ref.at[pl.ds(n * block, block)])
     x, g, router = x_ref[...], g_ref[...], router_ref[...]
-    place = wrap(index_ref[0] + shift) * block
 
     def send(value, k):
-        for c in range(chunks):
-            at = (b * 2 + k) * chunks + c
-            staged = pl.ds(at * block, block)
-            stage_ref[staged, :] = value[:, c * 128 : (c + 1) * 128]
-            there = pl.ds(pl.multiple_of(place + c * stride + k * rows, 16), block)
-            stores.append(
-                pltpu.make_async_copy(stage_ref.at[staged], part_hbm.at[there], sem.at[at])
-            )
-            stores[-1].start()
+        for n, (shift, _) in enumerate(messages):
+            place = wrap(index_ref[0] + shift) * block
+            for c in range(chunks):
+                at = (n * 2 + k) * chunks + c
+                staged = pl.ds(at * block, block)
+                stage_ref[staged, :] = value[
+                    n * block : (n + 1) * block, c * 128 : (c + 1) * 128
+                ]
+                there = pl.ds(pl.multiple_of(place + c * stride + k * rows, 16), block)
+                stores.append(
+                    pltpu.make_async_copy(stage_ref.at[staged], part_hbm.at[there], sem.at[at])
+                )
+                stores[-1].start()
 
     xf = x.astype(F32)
     logit = jnp.sum(xf * router, axis=1, keepdims=True)
@@ -165,10 +173,9 @@
     logit_grad = gate_grad * gate * (1.0 - gate)
     pre_grad = (hidden_grad * gate * slope).astype(BF)
     send((nt(pre_grad, first) + logit_grad * router).astype(BF), 1)
-    here = pl.ds(b * block, block)
     hidden = pre_grad.shape[1]
-    kept_ref[here, 0:hidden] = pre_grad
-    kept_ref[here, hidden:] = scaled_act
+    kept_ref[:, 0:hidden] = pre_grad
+    kept_ref[:, hidden:] = scaled_act
     return jnp.sum(xf * logit_grad, axis=0, keepdims=True)
 
 
@@ -194,7 +201,7 @@
         return first_ref[...], second_ref[...]
 
     sum_ref[...] = expert_block(
-        0, 0, stride, index_ref, msg_ref, weights, router_ref,
+        PARTS * x_ref.shape[0], stride, index_ref, [(0, msg_ref)], weights, router_ref,
         (part_hbm, kept_ref, x_ref, g_ref, stage_ref, sem), stores,
     )
     for store in stores:
@@ -205,17 +212,15 @@
     stride, index_ref, up_ref, down_ref, first_ref, second_ref, router_ref, before_ref, _,
     part_hbm, kept_ref, x_ref, g_ref, stage_ref, tail_ref, sem, tail_sem,
 ):
-    rows = PARTS * x_ref.shape[1]
-    router_sum = before_ref[...]
+    rows = PARTS * x_ref.shape[0] // 2
     stores = []
-    for b, (shift, msg_ref) in enumerate(((2, up_ref), (1, down_ref))):
-        router_sum = router_sum + expert_block(
-            shift, b, stride, index_ref, msg_ref,
-            lambda: (first_ref[...], second_ref[...]), router_ref,
-            (part_hbm, kept_ref, x_ref.at[b], g_ref.at[b], stage_ref, sem), stores,
-        )
+    router_sum = before_ref[...] + expert_block(
+        rows, stride, index_ref, [(2, up_ref), (1, down_ref)],
+        lambda: (first_ref[...], second_ref[...]), router_ref,
+        (part_hbm, kept_ref, x_ref, g_ref, stage_ref, sem), stores,
+    )
     tail = stride - 2 * rows
-    for c in range(x_ref.shape[2] // 128):
+    for c in range(x_ref.shape[1] // 128):
         lanes = slice(c * 128, (c + 1) * 128)
         row = jnp.where(iota((tail, 128), 0) == 0, router_sum[:, lanes], 0.0)
         staged = pl.ds(c * tail, tail)
@@ -345,7 +350,7 @@
             pltpu.VMEM((tok_rows, width), BF),
             pltpu.VMEM((members, tok_rows, width), BF),
             pltpu.VMEM((experts, members, 8, half), BF),
-            dma((3,)),
+            dma((4,)),
             dma((2,)),
         ],
         out_specs=[HB, VM],
@@ -384,7 +389,7 @@
         ],
         out_specs=[HB] + [VM] * 4, limit=MOST,
     )(part_index, own, w_in[0, 0], w_out[0, 0], column)
-    sides = pltpu.VMEM((2, block, width), BF)
+    sides = pltpu.VMEM((2 * block, width), BF)
     part, kept_rest = call(
         functools.partial(rest_kernel, stride),
         [whole, ((2 * block, 2 * hidden), BF)],

time: 170 us -> 170 us (level)
  no operation moved by 1% of the time
where the time goes in v6:
time: 170 us; the launch traced here: 169 us
  blocking collectives  107 us (63%)
  starting transfers between devices  23.4 us (14%)
  Pallas kernels  17.9 us (11%)
  waiting for transfers between devices  16.8 us (10%)
  local copies, waits for them, and re-layouts  2.43 us (1%)
    unnamed x1, blocking collectives  35.7 us
    all_to_all x1, blocking collectives, shards(): lax.all_to_all(msg.reshape(places, 8, half), plane, split_axis=0, concat_...  33.2 us
    all_gather x1, blocking collectives, shards(): line = lax.all_gather(compact, 'expert', axis_index_groups=lines)  21.4 us
    all_to_all x1, blocking collectives, shards(): lax.all_to_all(back.reshape(places, 16, 128), plane, split_axis=0, concat...  17 us
    ppermute x1, starting transfers between devices, shards(): lax.ppermute(own, 'expert', behind)  11.4 us
    ppermute x1, waiting for transfers between devices, shards(): lax.ppermute(own, 'expert', ahead)  9.8 us
    ppermute x1, waiting for transfers between devices, shards(): lax.ppermute(line, 'expert', behind)  5.11 us
    pallas_call x1, Pallas kernels, shards(): call(weight_kernel, [((width, hidden), BF), ((hidden, width), BF)], [HB]...  4.64 us
  transfers between devices with their start and end apart: 5, of which 4 were waited for; matrix products, arithmetic and copies ran while one was open for 1% of the time, Pallas kernels for 5%

profile of v6, /device:TPU:6, one launch (start us, length us, event | category | flops | bytes accessed | tf_op | source)
XLA Modules:
  0.0 169.3 jit_solution(9325077810693445267)
XLA Ops:
  0.6 0.0 copy-start
  0.7 3.3 %dispatch.1 = (bf16[32,2,8,640]{3,2,1,0:T(8,128)(2,1)}, s32[2,128]{1,0:T(2,128)}) custom-call(s32[1]{0:T(128)} %bitcast.part_ref.index_ref, s32[2,128]{1,0:T(2,128)} %bitcast.35, bf16[128,1280]{1,0:T(8,128)(2,1)} %tok_hbm.1, bf16[2,128,1280]{2,1,0:T(8,128)(2,1)} %grad_hbm.1), custom_call_target="tpu_custom_call" | custom-call | flops 3221225472 | bytes 4194304 | tf_op jit(solution)/shard_map/dispatch/pallas_call | solution.py:344
  4.0 33.2 %all_to_all.10 = bf16[64,8,640]{2,1,0:T(8,128)(2,1)S(1)} all-to-all(bf16[64,8,640]{2,1,0:T(8,128)(2,1)} %bitcast.31), channel_id=1, replica_groups=mesh['dp'=32,'member'=2,'expert'=12] {'dp','member'}, dimensions={0} | all-to-all | bytes 1310720 | tf_op jit(solution)/shard_map/all_to_all | solution.py:358
  37.2 1.9 %collective-permute-start = (bf16[512,640]{1,0:T(8,128)(2,1)S(1)}, bf16[512,640]{1,0:T(8,128)(2,1)S(1)}, u32[]{:S(2)}, u32[]{:S(2)}) collective-permute-start(bf16[512,640]{1,0:T(8,128)(2,1)S(1)} %bitcast.24), channel_id=1, source_target_pairs={{0,1},{1,2},{2,3},{3,4},{4,5},{5,6},{6,7},{7,8},{8,9},{9,10},{10,1... | collective-permute-start | bytes 1966088 | tf_op jit(solution)/shard_map/ppermute | solution.py:361
  39.1 11.4 %collective-permute-start.1 = (bf16[512,640]{1,0:T(8,128)(2,1)S(1)}, bf16[512,640]{1,0:T(8,128)(2,1)S(1)}, u32[]{:S(2)}, u32[]{:S(2)}) collective-permute-start(bf16[512,640]{1,0:T(8,128)(2,1)S(1)} %bitcast.25), channel_id=1, source_target_pairs={{0,11},{1,0},{2,1},{3,2},{4,3},{5,4},{6,5},{7,6},{8,7},{9,8},{10,9... | collective-permute-start | bytes 1966088 | tf_op jit(solution)/shard_map/ppermute | solution.py:361
  50.6 3.6 %expert_own.1 = (bf16[9576,128]{1,0:T(8,128)(2,1)}, bf16[128,768]{1,0:T(8,128)(2,1)S(1)}, f32[1,1280]{1,0:T(1,128)S(1)}, bf16[1280,384]{1,0:T(8,128)(2,1)S(1)}, bf16[384,1280]{1,0:T(8,128)(2,1)S(1)}) custom-call(s32[1]{0:T(128)} %bitcast.part_ref.index_ref, bf16[512,640]{1,0:T(8,128)(2,1)S(1)} %bitcast.26, bf16[1280,384]{1,0:T(8,128)(2,1)S(1)} %bitcast.30, ...), custom_call_target="tpu_custom_call" | custom-call | flops 1073741824 | bytes 6291456 | tf_op jit(solution)/shard_map/expert_own/pallas_call | solution.py:371
  54.2 9.8 %collective-permute-done.up_ref.up_hbm = bf16[512,640]{1,0:T(8,128)(2,1)S(1)} collective-permute-done((bf16[512,640]{1,0:T(8,128)(2,1)S(1)}, bf16[512,640]{1,0:T(8,128)(2,1)S(1)}, u32[]{:S(2)}, u32[]{:S(2)}) %collective-permute-start) | collective-permute-done | bytes 655392 | tf_op jit(solution)/shard_map/ppermute | solution.py:361
  64.0 1.5 collective-permute-done.1.down_ref.down_hbm
  65.6 3.5 %expert_rest.1 = (bf16[9576,128]{1,0:T(8,128)(2,1)}, bf16[256,768]{1,0:T(8,128)(2,1)S(1)}) custom-call(s32[1]{0:T(128)} %bitcast.part_ref.index_ref, bf16[512,640]{1,0:T(8,128)(2,1)S(1)} %collective-permute-done.up_ref.up_hbm, bf16[512,640]{1,0:T(8,128)(2,1)S(1)} %collective-permute-done.1.down_ref.down_hbm, ...), custom_call_target="tpu_custom_call", output_to_operand_aliasing={{0}: (7, {})} | custom-call | flops 2147483648 | bytes 8388608 | tf_op jit(solution)/shard_map/expert_rest/pallas_call | solution.py:393
  69.1 35.7 %fusion = bf16[800,128]{1,0:T(8,128)(2,1)S(1)} fusion(bf16[9576,128]{1,0:T(8,128)(2,1)} %get-tuple-element.25), kind=kCustom, calls=%all-reduce-scatter | all-reduce-scatter fusion | flops 1228801 | bytes 2660352
  104.8 3.0 %collective-permute-start.4 = (bf16[22,128]{1,0:T(8,128)(2,1)S(1)}, bf16[22,128]{1,0:T(8,128)(2,1)S(1)}, u32[]{:S(2)}, u32[]{:S(2)}) collective-permute-start(bf16[22,128]{1,0:T(8,128)(2,1)S(1)} %slice), channel_id=1, source_target_pairs={{0,1},{1,2},{2,3},{3,4},{4,5},{5,6},{6,7},{7,8},{8,9},{9,10},{10,1... | collective-permute-start | bytes 16904
  107.9 1.3 dynamic-slice.4
  109.8 1.1 concatenate
  110.9 0.1 constant_dynamic-slice_fusion.sum_ref
  110.9 0.8 to_tokens.1
  111.7 17.0 %all_to_all.11 = bf16[64,16,128]{2,1,0:T(8,128)(2,1)S(1)} all-to-all(bf16[64,16,128]{2,1,0:T(8,128)(2,1)S(1)} %bitcast.29), channel_id=1, replica_groups=mesh['dp'=32,'member'=2,'expert'=12] {'dp','member'}, dimensions={0} | all-to-all | bytes 524288 | tf_op jit(solution)/shard_map/all_to_all | solution.py:415
  128.7 0.6 collect.1
  129.3 21.4 %all-gather = bf16[1792,128]{1,0:T(8,128)(2,1)S(1)} all-gather(bf16[448,128]{1,0:T(8,128)(2,1)S(1)} %collect.1), channel_id=2, replica_groups={{0,3,6,9},{1,4,7,10},{2,5,8,11},{12,15,18,21},{13,16,19,22},{14,17,20,2..., dimensions={0}, use_global_device_ids=true | all-gather | bytes 573440 | tf_op jit(solution)/shard_map/all_gather | solution.py:431
  150.8 2.6 %collective-permute-start.2 = (bf16[4,448,128]{2,1,0:T(8,128)(2,1)S(1)}, bf16[4,448,128]{2,1,0:T(8,128)(2,1)S(1)}, u32[]{:S(2)}, u32[]{:S(2)}) collective-permute-start(bf16[4,448,128]{2,1,0:T(8,128)(2,1)S(1)} %bitcast.21), channel_id=1, source_target_pairs={{0,1},{1,2},{2,3},{3,4},{4,5},{5,6},{6,7},{7,8},{8,9},{9,10},{10,1... | collective-permute-start | bytes 1376264 | tf_op jit(solution)/shard_map/ppermute | solution.py:439
  153.3 4.5 %collective-permute-start.3 = (bf16[4,448,128]{2,1,0:T(8,128)(2,1)S(1)}, bf16[4,448,128]{2,1,0:T(8,128)(2,1)S(1)}, u32[]{:S(2)}, u32[]{:S(2)}) collective-permute-start(bf16[4,448,128]{2,1,0:T(8,128)(2,1)S(1)} %bitcast.22), channel_id=1, source_target_pairs={{0,11},{1,0},{2,1},{3,2},{4,3},{5,4},{6,5},{7,6},{8,7},{9,8},{10,9... | collective-permute-start | bytes 1376264 | tf_op jit(solution)/shard_map/ppermute | solution.py:440
  157.8 4.6 %weights.1 = (bf16[1280,384]{1,0:T(8,128)(2,1)}, bf16[384,1280]{1,0:T(8,128)(2,1)}) custom-call(bf16[512,640]{1,0:T(8,128)(2,1)S(1)} %bitcast.27, bf16[512,640]{1,0:T(8,128)(2,1)S(1)} %collective-permute-done.up_ref.up_hbm, bf16[512,640]{1,0:T(8,128)(2,1)S(1)} %collective-permute-done.1.down_ref.down_hbm, bf16[128,768]{1,0:T(8,128)(2,1)S(1)} %get-tuple-element.28.own_ref, ...), custom_call_target="tpu_custom_call" | custom-call | flops 1073741824 | bytes 6291456 | tf_op jit(solution)/shard_map/weights/pallas_call | solution.py:418
  162.5 0.3 collective-permute-done.2.up_ref
  162.8 5.1 %collective-permute-done.3.down_ref = bf16[4,448,128]{2,1,0:T(8,128)(2,1)S(1)} collective-permute-done((bf16[4,448,128]{2,1,0:T(8,128)(2,1)S(1)}, bf16[4,448,128]{2,1,0:T(8,128)(2,1)S(1)}, u32[]{:S(2)}, u32[]{:S(2)}) %collective-permute-start.3) | collective-permute-done | bytes 458784 | tf_op jit(solution)/shard_map/ppermute | solution.py:440
  167.9 1.4 final.1
  (8 shorter events, 0.0 us)
Async XLA Ops:
  0.6 50.0 %copy-start = (f32[2,1280,32]{1,2,0:T(8,128)S(1)}, f32[2,1280,32]{1,2,0:T(8,128)}, u32[]{:S(2)}) copy-start(f32[2,1280,32]{1,2,0:T(8,128)} %param.8) | copy-start | bytes 983044
  0.7 49.9 %copy-start.1 = (bf16[1,1,1280,384]{3,2,1,0:T(8,128)(2,1)S(1)}, bf16[1,1,1280,384]{3,2,1,0:T(8,128)(2,1)}, u32[]{:S(2)}) copy-start(bf16[1,1,1280,384]{3,2,1,0:T(8,128)(2,1)} %param.9) | copy-start | bytes 2949124
  37.2 26.8 %collective-permute-start = (bf16[512,640]{1,0:T(8,128)(2,1)S(1)}, bf16[512,640]{1,0:T(8,128)(2,1)S(1)}, u32[]{:S(2)}, u32[]{:S(2)}) collective-permute-start(bf16[512,640]{1,0:T(8,128)(2,1)S(1)} %bitcast.24), channel_id=1, source_target_pairs={{0,1},{1,2},{2,3},{3,4},{4,5},{5,6},{6,7},{7,8},{8,9},{9,10},{10,1... | collective-permute-start | bytes 1966088 | tf_op jit(solution)/shard_map/ppermute | solution.py:361
  39.1 26.5 %collective-permute-start.1 = (bf16[512,640]{1,0:T(8,128)(2,1)S(1)}, bf16[512,640]{1,0:T(8,128)(2,1)S(1)}, u32[]{:S(2)}, u32[]{:S(2)}) collective-permute-start(bf16[512,640]{1,0:T(8,128)(2,1)S(1)} %bitcast.25), channel_id=1, source_target_pairs={{0,11},{1,0},{2,1},{3,2},{4,3},{5,4},{6,5},{7,6},{8,7},{9,8},{10,9... | collective-permute-start | bytes 1966088 | tf_op jit(solution)/shard_map/ppermute | solution.py:361
  69.1 59.6 %copy-start.2 = (s32[2,128]{1,0:T(2,128)S(1)}, s32[2,128]{1,0:T(2,128)}, u32[]{:S(2)}) copy-start(s32[2,128]{1,0:T(2,128)} %get-tuple-element.19.code_ref) | copy-start | bytes 3076
  104.8 5.0 %collective-permute-start.4 = (bf16[22,128]{1,0:T(8,128)(2,1)S(1)}, bf16[22,128]{1,0:T(8,128)(2,1)S(1)}, u32[]{:S(2)}, u32[]{:S(2)}) collective-permute-start(bf16[22,128]{1,0:T(8,128)(2,1)S(1)} %slice), channel_id=1, source_target_pairs={{0,1},{1,2},{2,3},{3,4},{4,5},{5,6},{6,7},{7,8},{8,9},{9,10},{10,1... | collective-permute-start | bytes 16904
  150.8 12.1 %collective-permute-start.2 = (bf16[4,448,128]{2,1,0:T(8,128)(2,1)S(1)}, bf16[4,448,128]{2,1,0:T(8,128)(2,1)S(1)}, u32[]{:S(2)}, u32[]{:S(2)}) collective-permute-start(bf16[4,448,128]{2,1,0:T(8,128)(2,1)S(1)} %bitcast.21), channel_id=1, source_target_pairs={{0,1},{1,2},{2,3},{3,4},{4,5},{5,6},{6,7},{7,8},{8,9},{9,10},{10,1... | collective-permute-start | bytes 1376264 | tf_op jit(solution)/shard_map/ppermute | solution.py:439
  153.3 14.6 %collective-permute-start.3 = (bf16[4,448,128]{2,1,0:T(8,128)(2,1)S(1)}, bf16[4,448,128]{2,1,0:T(8,128)(2,1)S(1)}, u32[]{:S(2)}, u32[]{:S(2)}) collective-permute-start(bf16[4,448,128]{2,1,0:T(8,128)(2,1)S(1)} %bitcast.22), channel_id=1, source_target_pairs={{0,11},{1,0},{2,1},{3,2},{4,3},{5,4},{6,5},{7,6},{8,7},{9,8},{10,9... | collective-permute-start | bytes 1376264 | tf_op jit(solution)/shard_map/ppermute | solution.py:440

commit v7 on v6

--- a/solution.py
+++ b/solution.py
@@ -423,6 +423,7 @@
         + [pltpu.VMEM((rows, width), BF)] * 2
         + [dma((2 * PARTS,))],
     )(*arrived, kept_own, kept_rest)
+    home, grad_first, grad_second = lax.optimization_barrier((home, grad_first, grad_second))
     (compact,) = call(
         collect_kernel,
         [(((members + 1) * tok_rows + places, 128), BF)],

time: 170 us -> 171 us (level)
  blocking collectives: 107 us -> 90.1 us
  waiting for transfers between devices: 16.8 us -> 28.2 us
  starting transfers between devices: 23.4 us -> 29.2 us
    all_to_all x1 -> x0, blocking collectives: 17 us -> none  [shards(): lax.all_to_all(back.reshape(places, 16, 128), plane, split_axis=0, concat...]
    all_to_all x0 -> x1, waiting for transfers between devices: none -> 6.91 us  [shards(): lax.all_to_all(back.reshape(places, 16, 128), plane, split_axis=0, concat...]
    all_to_all x0 -> x1, starting transfers between devices: none -> 5.8 us  [shards(): lax.all_to_all(back.reshape(places, 16, 128), plane, split_axis=0, concat...]
    ppermute x1, waiting for transfers between devices: 0.35 us -> 4.94 us  [shards(): lax.ppermute(line, 'expert', ahead)]
  transfers between devices with their start and end apart: 5 -> 6, of which waited for: 4 -> 5; matrix products, arithmetic and copies ran while one was open for 1% -> 1% of each run, Pallas kernels for 5% -> 5%
where the time goes in v7:
time: 171 us; the launch traced here: 170 us
  blocking collectives  90.1 us (53%)
  starting transfers between devices  29.2 us (17%)
  waiting for transfers between devices  28.2 us (16%)
  Pallas kernels  18.6 us (11%)
  local copies, waits for them, and re-layouts  2.43 us (1%)
    unnamed x1, blocking collectives  35.6 us
    all_to_all x1, blocking collectives, shards(): lax.all_to_all(msg.reshape(places, 8, half), plane, split_axis=0, concat_...  33.2 us
    all_gather x1, blocking collectives, shards(): line = lax.all_gather(compact, 'expert', axis_index_groups=lines)  21.3 us
    ppermute x1, starting transfers between devices, shards(): lax.ppermute(own, 'expert', behind)  11.4 us
    ppermute x1, waiting for transfers between devices, shards(): lax.ppermute(own, 'expert', ahead)  9.8 us
    all_to_all x1, waiting for transfers between devices, shards(): lax.all_to_all(back.reshape(places, 16, 128), plane, split_axis=0, concat...  6.91 us
    all_to_all x1, starting transfers between devices, shards(): lax.all_to_all(back.reshape(places, 16, 128), plane, split_axis=0, concat...  5.8 us
    ppermute x1, waiting for transfers between devices, shards(): lax.ppermute(line, 'expert', behind)  5.02 us
  transfers between devices with their start and end apart: 6, of which 5 were waited for; matrix products, arithmetic and copies ran while one was open for 1% of the time, Pallas kernels for 5%

profile of v7, /device:TPU:6, one launch (start us, length us, event | category | flops | bytes accessed | tf_op | source)
XLA Modules:
  0.0 170.0 jit_solution(7163814027253165051)
XLA Ops:
  0.7 3.3 %dispatch.1 = (bf16[32,2,8,640]{3,2,1,0:T(8,128)(2,1)}, s32[2,128]{1,0:T(2,128)}) custom-call(s32[1]{0:T(128)} %bitcast.part_ref.index_ref, s32[2,128]{1,0:T(2,128)} %bitcast.34, bf16[128,1280]{1,0:T(8,128)(2,1)} %tok_hbm.1, bf16[2,128,1280]{2,1,0:T(8,128)(2,1)} %grad_hbm.1), custom_call_target="tpu_custom_call" | custom-call | flops 3221225472 | bytes 4194304 | tf_op jit(solution)/shard_map/dispatch/pallas_call | solution.py:344
  4.0 33.2 %all_to_all.10 = bf16[64,8,640]{2,1,0:T(8,128)(2,1)S(1)} all-to-all(bf16[64,8,640]{2,1,0:T(8,128)(2,1)} %bitcast.30), channel_id=1, replica_groups=mesh['dp'=32,'member'=2,'expert'=12] {'dp','member'}, dimensions={0} | all-to-all | bytes 1310720 | tf_op jit(solution)/shard_map/all_to_all | solution.py:358
  37.2 1.9 %collective-permute-start = (bf16[512,640]{1,0:T(8,128)(2,1)S(1)}, bf16[512,640]{1,0:T(8,128)(2,1)S(1)}, u32[]{:S(2)}, u32[]{:S(2)}) collective-permute-start(bf16[512,640]{1,0:T(8,128)(2,1)S(1)} %bitcast.24), channel_id=1, source_target_pairs={{0,1},{1,2},{2,3},{3,4},{4,5},{5,6},{6,7},{7,8},{8,9},{9,10},{10,1... | collective-permute-start | bytes 1966088 | tf_op jit(solution)/shard_map/ppermute | solution.py:361
  39.1 11.4 %collective-permute-start.1 = (bf16[512,640]{1,0:T(8,128)(2,1)S(1)}, bf16[512,640]{1,0:T(8,128)(2,1)S(1)}, u32[]{:S(2)}, u32[]{:S(2)}) collective-permute-start(bf16[512,640]{1,0:T(8,128)(2,1)S(1)} %bitcast.25), channel_id=1, source_target_pairs={{0,11},{1,0},{2,1},{3,2},{4,3},{5,4},{6,5},{7,6},{8,7},{9,8},{10,9... | collective-permute-start | bytes 1966088 | tf_op jit(solution)/shard_map/ppermute | solution.py:361
  50.6 3.6 %expert_own.1 = (bf16[9576,128]{1,0:T(8,128)(2,1)}, bf16[128,768]{1,0:T(8,128)(2,1)S(1)}, f32[1,1280]{1,0:T(1,128)S(1)}, bf16[1280,384]{1,0:T(8,128)(2,1)S(1)}, bf16[384,1280]{1,0:T(8,128)(2,1)S(1)}) custom-call(s32[1]{0:T(128)} %bitcast.part_ref.index_ref, bf16[512,640]{1,0:T(8,128)(2,1)S(1)} %bitcast.26, bf16[1280,384]{1,0:T(8,128)(2,1)S(1)} %bitcast.29, ...), custom_call_target="tpu_custom_call" | custom-call | flops 1073741824 | bytes 6291456 | tf_op jit(solution)/shard_map/expert_own/pallas_call | solution.py:371
  54.2 9.8 %collective-permute-done.up_ref.up_hbm = bf16[512,640]{1,0:T(8,128)(2,1)S(1)} collective-permute-done((bf16[512,640]{1,0:T(8,128)(2,1)S(1)}, bf16[512,640]{1,0:T(8,128)(2,1)S(1)}, u32[]{:S(2)}, u32[]{:S(2)}) %collective-permute-start) | collective-permute-done | bytes 655392 | tf_op jit(solution)/shard_map/ppermute | solution.py:361
  64.0 1.5 collective-permute-done.1.down_ref.down_hbm
  65.6 3.6 %expert_rest.1 = (bf16[9576,128]{1,0:T(8,128)(2,1)}, bf16[256,768]{1,0:T(8,128)(2,1)S(1)}) custom-call(s32[1]{0:T(128)} %bitcast.part_ref.index_ref, bf16[512,640]{1,0:T(8,128)(2,1)S(1)} %collective-permute-done.up_ref.up_hbm, bf16[512,640]{1,0:T(8,128)(2,1)S(1)} %collective-permute-done.1.down_ref.down_hbm, ...), custom_call_target="tpu_custom_call", output_to_operand_aliasing={{0}: (7, {})} | custom-call | flops 2147483648 | bytes 8388608 | tf_op jit(solution)/shard_map/expert_rest/pallas_call | solution.py:393
  69.1 35.6 %fusion = bf16[800,128]{1,0:T(8,128)(2,1)S(1)} fusion(bf16[9576,128]{1,0:T(8,128)(2,1)} %get-tuple-element.28), kind=kCustom, calls=%all-reduce-scatter | all-reduce-scatter fusion | flops 1228801 | bytes 2660352
  104.8 3.0 %collective-permute-start.4 = (bf16[22,128]{1,0:T(8,128)(2,1)S(1)}, bf16[22,128]{1,0:T(8,128)(2,1)S(1)}, u32[]{:S(2)}, u32[]{:S(2)}) collective-permute-start(bf16[22,128]{1,0:T(8,128)(2,1)S(1)} %slice), channel_id=1, source_target_pairs={{0,1},{1,2},{2,3},{3,4},{4,5},{5,6},{6,7},{7,8},{8,9},{9,10},{10,1... | collective-permute-start | bytes 16904
  107.8 1.3 dynamic-slice.4
  109.8 1.1 concatenate
  110.8 0.1 constant_dynamic-slice_fusion.sum_ref
  110.9 1.5 to_tokens.1
  112.4 5.8 %all-to-all-start.1 = ((bf16[64,16,128]{2,1,0:T(8,128)(2,1)}), bf16[64,16,128]{2,1,0:T(8,128)(2,1)S(1)}, u32[]{:S(2)}, u32[]{:S(2)}) async-start(bf16[64,16,128]{2,1,0:T(8,128)(2,1)} %bitcast.9), calls=%async_computation.1 | async-start | bytes 524288 | tf_op jit(solution)/shard_map/all_to_all | solution.py:415
  118.2 4.6 %weights.1 = (bf16[1280,384]{1,0:T(8,128)(2,1)}, bf16[384,1280]{1,0:T(8,128)(2,1)}) custom-call(bf16[512,640]{1,0:T(8,128)(2,1)S(1)} %bitcast.27, bf16[512,640]{1,0:T(8,128)(2,1)S(1)} %collective-permute-done.up_ref.up_hbm, bf16[512,640]{1,0:T(8,128)(2,1)S(1)} %collective-permute-done.1.down_ref.down_hbm, bf16[128,768]{1,0:T(8,128)(2,1)S(1)} %get-tuple-element.29.own_ref, ...), custom_call_target="tpu_custom_call" | custom-call | flops 1073741824 | bytes 6291456 | tf_op jit(solution)/shard_map/weights/pallas_call | solution.py:418
  122.8 6.9 %all-to-all-done.1 = bf16[64,16,128]{2,1,0:T(8,128)(2,1)S(1)} async-done(((bf16[64,16,128]{2,1,0:T(8,128)(2,1)}), bf16[64,16,128]{2,1,0:T(8,128)(2,1)S(1)}, u32[]{:S(2)}, u32[]{:S(2)}) %all-to-all-start.1) | async-done | bytes 262176 | tf_op jit(solution)/shard_map/all_to_all | solution.py:415
  129.8 0.6 collect.1
  130.4 21.3 %all-gather = bf16[1792,128]{1,0:T(8,128)(2,1)S(1)} all-gather(bf16[448,128]{1,0:T(8,128)(2,1)S(1)} %collect.1), channel_id=2, replica_groups={{0,3,6,9},{1,4,7,10},{2,5,8,11},{12,15,18,21},{13,16,19,22},{14,17,20,2..., dimensions={0}, use_global_device_ids=true | all-gather | bytes 573440 | tf_op jit(solution)/shard_map/all_gather | solution.py:432
  151.7 2.6 %collective-permute-start.2 = (bf16[4,448,128]{2,1,0:T(8,128)(2,1)S(1)}, bf16[4,448,128]{2,1,0:T(8,128)(2,1)S(1)}, u32[]{:S(2)}, u32[]{:S(2)}) collective-permute-start(bf16[4,448,128]{2,1,0:T(8,128)(2,1)S(1)} %bitcast.21), channel_id=1, source_target_pairs={{0,1},{1,2},{2,3},{3,4},{4,5},{5,6},{6,7},{7,8},{8,9},{9,10},{10,1... | collective-permute-start | bytes 1376264 | tf_op jit(solution)/shard_map/ppermute | solution.py:440
  154.2 4.5 %collective-permute-start.3 = (bf16[4,448,128]{2,1,0:T(8,128)(2,1)S(1)}, bf16[4,448,128]{2,1,0:T(8,128)(2,1)S(1)}, u32[]{:S(2)}, u32[]{:S(2)}) collective-permute-start(bf16[4,448,128]{2,1,0:T(8,128)(2,1)S(1)} %bitcast.22), channel_id=1, source_target_pairs={{0,11},{1,0},{2,1},{3,2},{4,3},{5,4},{6,5},{7,6},{8,7},{9,8},{10,9... | collective-permute-start | bytes 1376264 | tf_op jit(solution)/shard_map/ppermute | solution.py:441
  158.7 4.9 %collective-permute-done.2.up_ref = bf16[4,448,128]{2,1,0:T(8,128)(2,1)S(1)} collective-permute-done((bf16[4,448,128]{2,1,0:T(8,128)(2,1)S(1)}, bf16[4,448,128]{2,1,0:T(8,128)(2,1)S(1)}, u32[]{:S(2)}, u32[]{:S(2)}) %collective-permute-start.2) | collective-permute-done | bytes 458784 | tf_op jit(solution)/shard_map/ppermute | solution.py:440
  163.7 5.0 %collective-permute-done.3.down_ref = bf16[4,448,128]{2,1,0:T(8,128)(2,1)S(1)} collective-permute-done((bf16[4,448,128]{2,1,0:T(8,128)(2,1)S(1)}, bf16[4,448,128]{2,1,0:T(8,128)(2,1)S(1)}, u32[]{:S(2)}, u32[]{:S(2)}) %collective-permute-start.3) | collective-permute-done | bytes 458784 | tf_op jit(solution)/shard_map/ppermute | solution.py:441
  168.7 1.4 final.1
  (9 shorter events, 0.0 us)
Async XLA Ops:
  0.6 50.0 %copy-start = (f32[2,1280,32]{1,2,0:T(8,128)S(1)}, f32[2,1280,32]{1,2,0:T(8,128)}, u32[]{:S(2)}) copy-start(f32[2,1280,32]{1,2,0:T(8,128)} %param.8) | copy-start | bytes 983044
  0.7 49.9 %copy-start.1 = (bf16[1,1,1280,384]{3,2,1,0:T(8,128)(2,1)S(1)}, bf16[1,1,1280,384]{3,2,1,0:T(8,128)(2,1)}, u32[]{:S(2)}) copy-start(bf16[1,1,1280,384]{3,2,1,0:T(8,128)(2,1)} %param.9) | copy-start | bytes 2949124
  37.2 26.8 %collective-permute-start = (bf16[512,640]{1,0:T(8,128)(2,1)S(1)}, bf16[512,640]{1,0:T(8,128)(2,1)S(1)}, u32[]{:S(2)}, u32[]{:S(2)}) collective-permute-start(bf16[512,640]{1,0:T(8,128)(2,1)S(1)} %bitcast.24), channel_id=1, source_target_pairs={{0,1},{1,2},{2,3},{3,4},{4,5},{5,6},{6,7},{7,8},{8,9},{9,10},{10,1... | collective-permute-start | bytes 1966088 | tf_op jit(solution)/shard_map/ppermute | solution.py:361
  39.1 26.5 %collective-permute-start.1 = (bf16[512,640]{1,0:T(8,128)(2,1)S(1)}, bf16[512,640]{1,0:T(8,128)(2,1)S(1)}, u32[]{:S(2)}, u32[]{:S(2)}) collective-permute-start(bf16[512,640]{1,0:T(8,128)(2,1)S(1)} %bitcast.25), channel_id=1, source_target_pairs={{0,11},{1,0},{2,1},{3,2},{4,3},{5,4},{6,5},{7,6},{8,7},{9,8},{10,9... | collective-permute-start | bytes 1966088 | tf_op jit(solution)/shard_map/ppermute | solution.py:361
  104.8 5.0 %collective-permute-start.4 = (bf16[22,128]{1,0:T(8,128)(2,1)S(1)}, bf16[22,128]{1,0:T(8,128)(2,1)S(1)}, u32[]{:S(2)}, u32[]{:S(2)}) collective-permute-start(bf16[22,128]{1,0:T(8,128)(2,1)S(1)} %slice), channel_id=1, source_target_pairs={{0,1},{1,2},{2,3},{3,4},{4,5},{5,6},{6,7},{7,8},{8,9},{9,10},{10,1... | collective-permute-start | bytes 16904
  112.4 17.4 %copy-start.2 = (s32[2,128]{1,0:T(2,128)S(1)}, s32[2,128]{1,0:T(2,128)}, u32[]{:S(2)}) copy-start(s32[2,128]{1,0:T(2,128)} %get-tuple-element.22.code_ref) | copy-start | bytes 3076
  112.4 17.4 %all-to-all-start.1 = ((bf16[64,16,128]{2,1,0:T(8,128)(2,1)}), bf16[64,16,128]{2,1,0:T(8,128)(2,1)S(1)}, u32[]{:S(2)}, u32[]{:S(2)}) async-start(bf16[64,16,128]{2,1,0:T(8,128)(2,1)} %bitcast.9), calls=%async_computation.1 | async-start | bytes 524288 | tf_op jit(solution)/shard_map/all_to_all | solution.py:415
  151.7 12.0 %collective-permute-start.2 = (bf16[4,448,128]{2,1,0:T(8,128)(2,1)S(1)}, bf16[4,448,128]{2,1,0:T(8,128)(2,1)S(1)}, u32[]{:S(2)}, u32[]{:S(2)}) collective-permute-start(bf16[4,448,128]{2,1,0:T(8,128)(2,1)S(1)} %bitcast.21), channel_id=1, source_target_pairs={{0,1},{1,2},{2,3},{3,4},{4,5},{5,6},{6,7},{7,8},{8,9},{9,10},{10,1... | collective-permute-start | bytes 1376264 | tf_op jit(solution)/shard_map/ppermute | solution.py:440
  154.2 14.4 %collective-permute-start.3 = (bf16[4,448,128]{2,1,0:T(8,128)(2,1)S(1)}, bf16[4,448,128]{2,1,0:T(8,128)(2,1)S(1)}, u32[]{:S(2)}, u32[]{:S(2)}) collective-permute-start(bf16[4,448,128]{2,1,0:T(8,128)(2,1)S(1)} %bitcast.22), channel_id=1, source_target_pairs={{0,11},{1,0},{2,1},{3,2},{4,3},{5,4},{6,5},{7,6},{8,7},{9,8},{10,9... | collective-permute-start | bytes 1376264 | tf_op jit(solution)/shard_map/ppermute | solution.py:441

commit v8 on v6

--- a/solution.py
+++ b/solution.py
@@ -134,7 +134,8 @@
 def expert_block(rows, stride, index_ref, messages, weights, router_ref, refs, stores):
     part_hbm, kept_ref, x_ref, g_ref, stage_ref, sem = refs
     block = rows // PARTS
-    chunks = x_ref.shape[1] // 128
+    places = -(-part_hbm.shape[0] // stride)
+    last = x_ref.shape[1] // 128 - 1
     sort = sorting()
     for n, (_, msg_ref) in enumerate(messages):
         for k in range(2):
@@ -144,13 +145,14 @@
     def send(value, k):
         for n, (shift, _) in enumerate(messages):
             place = wrap(index_ref[0] + shift) * block
-            for c in range(chunks):
-                at = (n * 2 + k) * chunks + c
-                staged = pl.ds(at * block, block)
-                stage_ref[staged, :] = value[
-                    n * block : (n + 1) * block, c * 128 : (c + 1) * 128
-                ]
+            for c in range(places):
+                staged = pl.ds(((n * 2 + k) * (last + 1) + min(c, last)) * block, block)
+                if c <= last:
+                    stage_ref[staged, :] = value[
+                        n * block : (n + 1) * block, c * 128 : (c + 1) * 128
+                    ]
                 there = pl.ds(pl.multiple_of(place + c * stride + k * rows, 16), block)
+                at = (n * 2 + k) * places + c
                 stores.append(
                     pltpu.make_async_copy(stage_ref.at[staged], part_hbm.at[there], sem.at[at])
                 )
@@ -182,7 +184,7 @@
 def own_kernel(
     stride, index_ref, msg_ref, first_hbm, second_hbm, router_ref,
     part_hbm, kept_ref, sum_ref, first_ref, second_ref,
-    x_ref, g_ref, stage_ref, zero_ref, sem, load_sem, zero_sem,
+    x_ref, g_ref, stage_ref, sem, load_sem,
 ):
     loads = [
         pltpu.make_async_copy(first_hbm, first_ref, load_sem.at[0]),
@@ -190,10 +192,7 @@
     ]
     for load in loads:
         load.start()
-    zero_ref[...] = jnp.zeros(zero_ref.shape, BF)
-    there = pl.ds(x_ref.shape[1] // 128 * stride, zero_ref.shape[0])
-    stores = [pltpu.make_async_copy(zero_ref, part_hbm.at[there], zero_sem)]
-    stores[0].start()
+    stores = []
 
     def weights():
         for load in loads:
@@ -220,14 +219,22 @@
         (part_hbm, kept_ref, x_ref, g_ref, stage_ref, sem), stores,
     )
     tail = stride - 2 * rows
-    for c in range(x_ref.shape[1] // 128):
-        lanes = slice(c * 128, (c + 1) * 128)
-        row = jnp.where(iota((tail, 128), 0) == 0, router_sum[:, lanes], 0.0)
-        staged = pl.ds(c * tail, tail)
-        tail_ref[staged, :] = row.astype(BF)
-        there = pl.ds(c * stride + 2 * rows, tail)
+    last = x_ref.shape[1] // 128 - 1
+    total = part_hbm.shape[0]
+    for c in range(-(-total // stride)):
+        if c <= last:
+            row = jnp.where(
+                iota((tail, 128), 0) == 0, router_sum[:, c * 128 : (c + 1) * 128], 0.0
+            )
+            tail_ref[pl.ds(c * tail, tail), :] = row.astype(BF)
+        start = c * stride + 2 * rows
+        size = min(tail, total - start)
         stores.append(
-            pltpu.make_async_copy(tail_ref.at[staged], part_hbm.at[there], tail_sem.at[c])
+            pltpu.make_async_copy(
+                tail_ref.at[pl.ds(min(c, last) * tail, size)],
+                part_hbm.at[pl.ds(start, size)],
+                tail_sem.at[c],
+            )
         )
         stores[-1].start()
     for store in stores:
@@ -298,16 +305,18 @@
 
 def final_kernel(part_ref, own_ref, up_ref, down_ref, moe_ref, token_ref, router_ref):
     tok_rows, width = token_ref.shape
+
+    def place(block, lanes):
+        moe_ref[:, lanes] = block[0 : 2 * tok_rows, :]
+        token_ref[:, lanes] = block[2 * tok_rows : 3 * tok_rows, :].astype(F32)
+        router_ref[:, lanes] = block[3 * tok_rows :, :].astype(F32)
+
     for ref, shift in ((own_ref, 0), (up_ref, 2), (down_ref, 1)):
         part = wrap(part_ref[0] + shift)
-        for k in range(ref.shape[0]):
-
-            @pl.when(part + PARTS * k < width // 128)
-            def _():
-                lanes = pl.ds(pl.multiple_of((part + PARTS * k) * 128, 128), 128)
-                moe_ref[:, lanes] = ref[k, 0 : 2 * tok_rows, :]
-                token_ref[:, lanes] = ref[k, 2 * tok_rows : 3 * tok_rows, :].astype(F32)
-                router_ref[:, lanes] = ref[k, 3 * tok_rows :, :].astype(F32)
+        for k in range(up_ref.shape[0]):
+            lanes = pl.ds(pl.multiple_of((part + PARTS * k) * 128, 128), 128)
+            place(ref.at[k], lanes)
+    place(own_ref.at[own_ref.shape[0] - 1], slice(width - 128, width))
 
 
 def call(kernel, out, specs, name, flops, size, scratch=(), out_specs=None, limit=FULL, alias=None):
@@ -382,10 +391,8 @@
             side,
             side,
             pltpu.VMEM((2 * chunks * block, 128), BF),
-            pltpu.VMEM((z_count * share - chunks * stride, 128), BF),
-            dma((2 * chunks,)),
+            dma((2 * z_count,)),
             dma((2,)),
-            dma(()),
         ],
         out_specs=[HB] + [VM] * 4, limit=MOST,
     )(part_index, own, w_in[0, 0], w_out[0, 0], column)
@@ -399,8 +406,8 @@
             sides,
             pltpu.VMEM((4 * chunks * block, 128), BF),
             pltpu.VMEM((chunks * (stride - 2 * rows), 128), BF),
-            dma((4 * chunks,)),
-            dma((chunks,)),
+            dma((4 * z_count,)),
+            dma((z_count,)),
         ],
         out_specs=[HB, VM], limit=MOST, alias={7: 0},
     )(part_index, *arrived[1:], first, second, column, router_own, part)
@@ -436,8 +443,8 @@
     )(
         part_index,
         line,
-        lax.ppermute(line, "expert", ahead),
-        lax.ppermute(line, "expert", behind),
+        lax.ppermute(line[:-1], "expert", ahead),
+        lax.ppermute(line[:-1], "expert", behind),
     )
     router_grad = jnp.transpose(router_rows.reshape(members, experts, width), (0, 2, 1))
     return (

time: 170 us -> 168 us (0.988)
  waiting for transfers between devices: 16.8 us -> 14.4 us
    ppermute x2, waiting for transfers between devices: 5.46 us -> 3.14 us  [the longest x1 3.13 us: shards(): lax.ppermute(line[:-1], 'expert', behind)]
  transfers between devices with their start and end apart: 5 -> 5, of which waited for: 4 -> 3; matrix products, arithmetic and copies ran while one was open for 1% -> 1% of each run, Pallas kernels for 5% -> 5%
where the time goes in v8:
time: 168 us; the launch traced here: 167 us
  blocking collectives  107 us (64%)
  starting transfers between devices  23.4 us (14%)
  Pallas kernels  18 us (11%)
  waiting for transfers between devices  14.4 us (9%)
  local copies, waits for them, and re-layouts  2.46 us (1%)
    unnamed x1, blocking collectives  35.7 us
    all_to_all x1, blocking collectives, shards(): lax.all_to_all(msg.reshape(places, 8, half), plane, split_axis=0, concat_...  33.2 us
    all_gather x1, blocking collectives, shards(): line = lax.all_gather(compact, 'expert', axis_index_groups=lines)  21 us
    all_to_all x1, blocking collectives, shards(): lax.all_to_all(back.reshape(places, 16, 128), plane, split_axis=0, concat...  17 us
    ppermute x1, starting transfers between devices, shards(): lax.ppermute(own, 'expert', behind)  11.4 us
    ppermute x1, waiting for transfers between devices, shards(): lax.ppermute(own, 'expert', ahead)  9.74 us
    pallas_call x1, Pallas kernels, shards(): call(weight_kernel, [((width, hidden), BF), ((hidden, width), BF)], [HB]...  4.64 us
    ppermute x1, starting transfers between devices, shards(): lax.ppermute(line[:-1], 'expert', behind)  4.11 us
  transfers between devices with their start and end apart: 5, of which 3 were waited for; matrix products, arithmetic and copies ran while one was open for 1% of the time, Pallas kernels for 5%

profile of v8, /device:TPU:6, one launch (start us, length us, event | category | flops | bytes accessed | tf_op | source)
XLA Modules:
  0.0 166.7 jit_solution(5732722816024647926)
XLA Ops:
  0.6 0.0 copy-start
  0.7 3.3 %dispatch.1 = (bf16[32,2,8,640]{3,2,1,0:T(8,128)(2,1)}, s32[2,128]{1,0:T(2,128)}) custom-call(s32[1]{0:T(128)} %bitcast.part_ref.index_ref, s32[2,128]{1,0:T(2,128)} %bitcast.36, bf16[128,1280]{1,0:T(8,128)(2,1)} %tok_hbm.1, bf16[2,128,1280]{2,1,0:T(8,128)(2,1)} %grad_hbm.1), custom_call_target="tpu_custom_call" | custom-call | flops 3221225472 | bytes 4194304 | tf_op jit(solution)/shard_map/dispatch/pallas_call | solution.py:353
  4.0 33.2 %all_to_all.10 = bf16[64,8,640]{2,1,0:T(8,128)(2,1)S(1)} all-to-all(bf16[64,8,640]{2,1,0:T(8,128)(2,1)} %bitcast.30), channel_id=1, replica_groups=mesh['dp'=32,'member'=2,'expert'=12] {'dp','member'}, dimensions={0} | all-to-all | bytes 1310720 | tf_op jit(solution)/shard_map/all_to_all | solution.py:367
  37.2 1.9 %collective-permute-start = (bf16[512,640]{1,0:T(8,128)(2,1)S(1)}, bf16[512,640]{1,0:T(8,128)(2,1)S(1)}, u32[]{:S(2)}, u32[]{:S(2)}) collective-permute-start(bf16[512,640]{1,0:T(8,128)(2,1)S(1)} %bitcast.23), channel_id=1, source_target_pairs={{0,1},{1,2},{2,3},{3,4},{4,5},{5,6},{6,7},{7,8},{8,9},{9,10},{10,1... | collective-permute-start | bytes 1966088 | tf_op jit(solution)/shard_map/ppermute | solution.py:370
  39.1 11.4 %collective-permute-start.1 = (bf16[512,640]{1,0:T(8,128)(2,1)S(1)}, bf16[512,640]{1,0:T(8,128)(2,1)S(1)}, u32[]{:S(2)}, u32[]{:S(2)}) collective-permute-start(bf16[512,640]{1,0:T(8,128)(2,1)S(1)} %bitcast.24), channel_id=1, source_target_pairs={{0,11},{1,0},{2,1},{3,2},{4,3},{5,4},{6,5},{7,6},{8,7},{9,8},{10,9... | collective-permute-start | bytes 1966088 | tf_op jit(solution)/shard_map/ppermute | solution.py:370
  50.6 3.7 %expert_own.1 = (bf16[9576,128]{1,0:T(8,128)(2,1)}, bf16[128,768]{1,0:T(8,128)(2,1)S(1)}, f32[1,1280]{1,0:T(1,128)S(1)}, bf16[1280,384]{1,0:T(8,128)(2,1)S(1)}, bf16[384,1280]{1,0:T(8,128)(2,1)S(1)}) custom-call(s32[1]{0:T(128)} %bitcast.part_ref.index_ref, bf16[512,640]{1,0:T(8,128)(2,1)S(1)} %bitcast.25, bf16[1280,384]{1,0:T(8,128)(2,1)S(1)} %bitcast.29, ...), custom_call_target="tpu_custom_call" | custom-call | flops 1073741824 | bytes 6291456 | tf_op jit(solution)/shard_map/expert_own/pallas_call | solution.py:380
  54.3 9.7 %collective-permute-done.up_ref.up_hbm = bf16[512,640]{1,0:T(8,128)(2,1)S(1)} collective-permute-done((bf16[512,640]{1,0:T(8,128)(2,1)S(1)}, bf16[512,640]{1,0:T(8,128)(2,1)S(1)}, u32[]{:S(2)}, u32[]{:S(2)}) %collective-permute-start) | collective-permute-done | bytes 655392 | tf_op jit(solution)/shard_map/ppermute | solution.py:370
  64.0 1.5 collective-permute-done.1.down_ref.down_hbm
  65.6 3.6 %expert_rest.1 = (bf16[9576,128]{1,0:T(8,128)(2,1)}, bf16[256,768]{1,0:T(8,128)(2,1)S(1)}) custom-call(s32[1]{0:T(128)} %bitcast.part_ref.index_ref, bf16[512,640]{1,0:T(8,128)(2,1)S(1)} %collective-permute-done.up_ref.up_hbm, bf16[512,640]{1,0:T(8,128)(2,1)S(1)} %collective-permute-done.1.down_ref.down_hbm, ...), custom_call_target="tpu_custom_call", output_to_operand_aliasing={{0}: (7, {})} | custom-call | flops 2147483648 | bytes 8388608 | tf_op jit(solution)/shard_map/expert_rest/pallas_call | solution.py:400
  69.2 0.0 copy-start.2
  69.2 35.7 %fusion = bf16[800,128]{1,0:T(8,128)(2,1)S(1)} fusion(bf16[9576,128]{1,0:T(8,128)(2,1)} %get-tuple-element.25), kind=kCustom, calls=%all-reduce-scatter | all-reduce-scatter fusion | flops 1228801 | bytes 2660352
  104.9 3.0 %collective-permute-start.4 = (bf16[22,128]{1,0:T(8,128)(2,1)S(1)}, bf16[22,128]{1,0:T(8,128)(2,1)S(1)}, u32[]{:S(2)}, u32[]{:S(2)}) collective-permute-start(bf16[22,128]{1,0:T(8,128)(2,1)S(1)} %slice.7), channel_id=1, source_target_pairs={{0,1},{1,2},{2,3},{3,4},{4,5},{5,6},{6,7},{7,8},{8,9},{9,10},{10,1... | collective-permute-start | bytes 16904
  108.0 1.3 dynamic-slice.4
  109.9 1.1 concatenate
  111.0 0.1 constant_dynamic-slice_fusion.sum_ref
  111.0 0.8 to_tokens.1
  111.8 17.0 %all_to_all.11 = bf16[64,16,128]{2,1,0:T(8,128)(2,1)S(1)} all-to-all(bf16[64,16,128]{2,1,0:T(8,128)(2,1)S(1)} %bitcast.28), channel_id=1, replica_groups=mesh['dp'=32,'member'=2,'expert'=12] {'dp','member'}, dimensions={0} | all-to-all | bytes 524288 | tf_op jit(solution)/shard_map/all_to_all | solution.py:422
  128.8 0.6 collect.1
  129.5 21.0 %all-gather = bf16[1792,128]{1,0:T(8,128)(2,1)S(1)} all-gather(bf16[448,128]{1,0:T(8,128)(2,1)S(1)} %collect.1), channel_id=2, replica_groups={{0,3,6,9},{1,4,7,10},{2,5,8,11},{12,15,18,21},{13,16,19,22},{14,17,20,2..., dimensions={0}, use_global_device_ids=true | all-gather | bytes 573440 | tf_op jit(solution)/shard_map/all_gather | solution.py:438
  150.5 2.9 %collective-permute-start.2 = (bf16[3,448,128]{2,1,0:T(8,128)(2,1)S(1)}, bf16[3,448,128]{2,1,0:T(8,128)(2,1)S(1)}, u32[]{:S(2)}, u32[]{:S(2)}) collective-permute-start(bf16[3,448,128]{2,1,0:T(8,128)(2,1)S(1)} %bitcast.31), channel_id=1, source_target_pairs={{0,1},{1,2},{2,3},{3,4},{4,5},{5,6},{6,7},{7,8},{8,9},{9,10},{10,1... | collective-permute-start | bytes 1032200 | tf_op jit(solution)/shard_map/ppermute | solution.py:446
  153.5 4.1 %collective-permute-start.3 = (bf16[3,448,128]{2,1,0:T(8,128)(2,1)S(1)}, bf16[3,448,128]{2,1,0:T(8,128)(2,1)S(1)}, u32[]{:S(2)}, u32[]{:S(2)}) collective-permute-start(bf16[3,448,128]{2,1,0:T(8,128)(2,1)S(1)} %bitcast.32), channel_id=1, source_target_pairs={{0,11},{1,0},{2,1},{3,2},{4,3},{5,4},{6,5},{7,6},{8,7},{9,8},{10,9... | collective-permute-start | bytes 1032200 | tf_op jit(solution)/shard_map/ppermute | solution.py:447
  157.6 4.6 %weights.1 = (bf16[1280,384]{1,0:T(8,128)(2,1)}, bf16[384,1280]{1,0:T(8,128)(2,1)}) custom-call(bf16[512,640]{1,0:T(8,128)(2,1)S(1)} %bitcast.26, bf16[512,640]{1,0:T(8,128)(2,1)S(1)} %collective-permute-done.up_ref.up_hbm, bf16[512,640]{1,0:T(8,128)(2,1)S(1)} %collective-permute-done.1.down_ref.down_hbm, bf16[128,768]{1,0:T(8,128)(2,1)S(1)} %get-tuple-element.28.own_ref, ...), custom_call_target="tpu_custom_call" | custom-call | flops 1073741824 | bytes 6291456 | tf_op jit(solution)/shard_map/weights/pallas_call | solution.py:425
  162.3 3.1 %collective-permute-done.3.down_ref = bf16[3,448,128]{2,1,0:T(8,128)(2,1)S(1)} collective-permute-done((bf16[3,448,128]{2,1,0:T(8,128)(2,1)S(1)}, bf16[3,448,128]{2,1,0:T(8,128)(2,1)S(1)}, u32[]{:S(2)}, u32[]{:S(2)}) %collective-permute-start.3) | collective-permute-done | bytes 344096 | tf_op jit(solution)/shard_map/ppermute | solution.py:447
  165.4 1.3 final.1
  (9 shorter events, 0.1 us)
Async XLA Ops:
  0.6 50.0 %copy-start = (f32[2,1280,32]{1,2,0:T(8,128)S(1)}, f32[2,1280,32]{1,2,0:T(8,128)}, u32[]{:S(2)}) copy-start(f32[2,1280,32]{1,2,0:T(8,128)} %param.8) | copy-start | bytes 983044
  0.7 49.9 %copy-start.1 = (bf16[1,1,1280,384]{3,2,1,0:T(8,128)(2,1)S(1)}, bf16[1,1,1280,384]{3,2,1,0:T(8,128)(2,1)}, u32[]{:S(2)}) copy-start(bf16[1,1,1280,384]{3,2,1,0:T(8,128)(2,1)} %param.9) | copy-start | bytes 2949124
  37.2 26.8 %collective-permute-start = (bf16[512,640]{1,0:T(8,128)(2,1)S(1)}, bf16[512,640]{1,0:T(8,128)(2,1)S(1)}, u32[]{:S(2)}, u32[]{:S(2)}) collective-permute-start(bf16[512,640]{1,0:T(8,128)(2,1)S(1)} %bitcast.23), channel_id=1, source_target_pairs={{0,1},{1,2},{2,3},{3,4},{4,5},{5,6},{6,7},{7,8},{8,9},{9,10},{10,1... | collective-permute-start | bytes 1966088 | tf_op jit(solution)/shard_map/ppermute | solution.py:370
  39.1 26.5 %collective-permute-start.1 = (bf16[512,640]{1,0:T(8,128)(2,1)S(1)}, bf16[512,640]{1,0:T(8,128)(2,1)S(1)}, u32[]{:S(2)}, u32[]{:S(2)}) collective-permute-start(bf16[512,640]{1,0:T(8,128)(2,1)S(1)} %bitcast.24), channel_id=1, source_target_pairs={{0,11},{1,0},{2,1},{3,2},{4,3},{5,4},{6,5},{7,6},{8,7},{9,8},{10,9... | collective-permute-start | bytes 1966088 | tf_op jit(solution)/shard_map/ppermute | solution.py:370
  69.2 59.6 %copy-start.2 = (s32[2,128]{1,0:T(2,128)S(1)}, s32[2,128]{1,0:T(2,128)}, u32[]{:S(2)}) copy-start(s32[2,128]{1,0:T(2,128)} %get-tuple-element.19.code_ref) | copy-start | bytes 3076
  104.9 5.0 %collective-permute-start.4 = (bf16[22,128]{1,0:T(8,128)(2,1)S(1)}, bf16[22,128]{1,0:T(8,128)(2,1)S(1)}, u32[]{:S(2)}, u32[]{:S(2)}) collective-permute-start(bf16[22,128]{1,0:T(8,128)(2,1)S(1)} %slice.7), channel_id=1, source_target_pairs={{0,1},{1,2},{2,3},{3,4},{4,5},{5,6},{6,7},{7,8},{8,9},{9,10},{10,1... | collective-permute-start | bytes 16904
  150.5 11.7 %collective-permute-start.2 = (bf16[3,448,128]{2,1,0:T(8,128)(2,1)S(1)}, bf16[3,448,128]{2,1,0:T(8,128)(2,1)S(1)}, u32[]{:S(2)}, u32[]{:S(2)}) collective-permute-start(bf16[3,448,128]{2,1,0:T(8,128)(2,1)S(1)} %bitcast.31), channel_id=1, source_target_pairs={{0,1},{1,2},{2,3},{3,4},{4,5},{5,6},{6,7},{7,8},{8,9},{9,10},{10,1... | collective-permute-start | bytes 1032200 | tf_op jit(solution)/shard_map/ppermute | solution.py:446
  153.5 11.9 %collective-permute-start.3 = (bf16[3,448,128]{2,1,0:T(8,128)(2,1)S(1)}, bf16[3,448,128]{2,1,0:T(8,128)(2,1)S(1)}, u32[]{:S(2)}, u32[]{:S(2)}) collective-permute-start(bf16[3,448,128]{2,1,0:T(8,128)(2,1)S(1)} %bitcast.32), channel_id=1, source_target_pairs={{0,11},{1,0},{2,1},{3,2},{4,3},{5,4},{6,5},{7,6},{8,7},{9,8},{10,9... | collective-permute-start | bytes 1032200 | tf_op jit(solution)/shard_map/ppermute | solution.py:447

commit v9 on v8

--- a/solution.py
+++ b/solution.py
@@ -303,20 +303,28 @@
     ).astype(BF)
 
 
-def final_kernel(part_ref, own_ref, up_ref, down_ref, moe_ref, token_ref, router_ref):
+def final_kernel(part_ref, own_ref, up_ref, down_ref, moe_hbm, token_ref, router_ref, sem):
     tok_rows, width = token_ref.shape
-
-    def place(block, lanes):
-        moe_ref[:, lanes] = block[0 : 2 * tok_rows, :]
-        token_ref[:, lanes] = block[2 * tok_rows : 3 * tok_rows, :].astype(F32)
-        router_ref[:, lanes] = block[3 * tok_rows :, :].astype(F32)
-
+    pieces = []
     for ref, shift in ((own_ref, 0), (up_ref, 2), (down_ref, 1)):
         part = wrap(part_ref[0] + shift)
         for k in range(up_ref.shape[0]):
             lanes = pl.ds(pl.multiple_of((part + PARTS * k) * 128, 128), 128)
-            place(ref.at[k], lanes)
-    place(own_ref.at[own_ref.shape[0] - 1], slice(width - 128, width))
+            pieces.append((ref.at[k], lanes))
+    pieces.append((own_ref.at[own_ref.shape[0] - 1], pl.ds(width - 128, 128)))
+    stores = []
+    for k, (block, lanes) in enumerate(pieces):
+        stores.append(
+            pltpu.make_async_copy(
+                block.at[pl.ds(0, 2 * tok_rows)], moe_hbm.at[:, lanes], sem.at[k]
+            )
+        )
+        stores[-1].start()
+    for block, lanes in pieces:
+        token_ref[:, lanes] = block[2 * tok_rows : 3 * tok_rows, :].astype(F32)
+        router_ref[:, lanes] = block[3 * tok_rows :, :].astype(F32)
+    for store in stores:
+        store.wait()
 
 
 def call(kernel, out, specs, name, flops, size, scratch=(), out_specs=None, limit=FULL, alias=None):
@@ -440,6 +448,7 @@
         final_kernel,
         [((members * tok_rows, width), BF), ((tok_rows, width), F32), ((places, width), F32)],
         [SM] + [VM] * 3, "final", 1 << 20, 4 << 20, limit=LIMIT,
+        scratch=[dma((chunks,))], out_specs=[HB, VM, VM],
     )(
         part_index,
         line,

time: 168 us -> 168 us (level)
  no operation moved by 1% of the time
where the time goes in v9:
time: 168 us; the launch traced here: 167 us
  blocking collectives  107 us (64%)
  starting transfers between devices  23.4 us (14%)
  Pallas kernels  18.5 us (11%)
  waiting for transfers between devices  14.4 us (9%)
  local copies, waits for them, and re-layouts  2.46 us (1%)
    unnamed x1, blocking collectives  35.7 us
    all_to_all x1, blocking collectives, shards(): lax.all_to_all(msg.reshape(places, 8, half), plane, split_axis=0, concat_...  33.2 us
    all_gather x1, blocking collectives, shards(): line = lax.all_gather(compact, 'expert', axis_index_groups=lines)  21 us
    all_to_all x1, blocking collectives, shards(): lax.all_to_all(back.reshape(places, 16, 128), plane, split_axis=0, concat...  17 us
    ppermute x1, starting transfers between devices, shards(): lax.ppermute(own, 'expert', behind)  11.4 us
    ppermute x1, waiting for transfers between devices, shards(): lax.ppermute(own, 'expert', ahead)  9.74 us
    pallas_call x1, Pallas kernels, shards(): call(weight_kernel, [((width, hidden), BF), ((hidden, width), BF)], [HB]...  4.64 us
    ppermute x1, starting transfers between devices, shards(): lax.ppermute(line[:-1], 'expert', behind)  4.11 us
  transfers between devices with their start and end apart: 5, of which 3 were waited for; matrix products, arithmetic and copies ran while one was open for 1% of the time, Pallas kernels for 5%

profile of v9, /device:TPU:6, one launch (start us, length us, event | category | flops | bytes accessed | tf_op | source)
XLA Modules:
  0.0 167.2 jit_solution(714566222800918148)
XLA Ops:
  0.6 0.0 copy-start
  0.7 3.3 %dispatch.1 = (bf16[32,2,8,640]{3,2,1,0:T(8,128)(2,1)}, s32[2,128]{1,0:T(2,128)}) custom-call(s32[1]{0:T(128)} %bitcast.part_ref.index_ref, s32[2,128]{1,0:T(2,128)} %bitcast.36, bf16[128,1280]{1,0:T(8,128)(2,1)} %tok_hbm.1, bf16[2,128,1280]{2,1,0:T(8,128)(2,1)} %grad_hbm.1), custom_call_target="tpu_custom_call" | custom-call | flops 3221225472 | bytes 4194304 | tf_op jit(solution)/shard_map/dispatch/pallas_call | solution.py:361
  4.0 33.2 %all_to_all.10 = bf16[64,8,640]{2,1,0:T(8,128)(2,1)S(1)} all-to-all(bf16[64,8,640]{2,1,0:T(8,128)(2,1)} %bitcast.30), channel_id=1, replica_groups=mesh['dp'=32,'member'=2,'expert'=12] {'dp','member'}, dimensions={0} | all-to-all | bytes 1310720 | tf_op jit(solution)/shard_map/all_to_all | solution.py:375
  37.2 1.9 %collective-permute-start = (bf16[512,640]{1,0:T(8,128)(2,1)S(1)}, bf16[512,640]{1,0:T(8,128)(2,1)S(1)}, u32[]{:S(2)}, u32[]{:S(2)}) collective-permute-start(bf16[512,640]{1,0:T(8,128)(2,1)S(1)} %bitcast.23), channel_id=1, source_target_pairs={{0,1},{1,2},{2,3},{3,4},{4,5},{5,6},{6,7},{7,8},{8,9},{9,10},{10,1... | collective-permute-start | bytes 1966088 | tf_op jit(solution)/shard_map/ppermute | solution.py:378
  39.1 11.4 %collective-permute-start.1 = (bf16[512,640]{1,0:T(8,128)(2,1)S(1)}, bf16[512,640]{1,0:T(8,128)(2,1)S(1)}, u32[]{:S(2)}, u32[]{:S(2)}) collective-permute-start(bf16[512,640]{1,0:T(8,128)(2,1)S(1)} %bitcast.24), channel_id=1, source_target_pairs={{0,11},{1,0},{2,1},{3,2},{4,3},{5,4},{6,5},{7,6},{8,7},{9,8},{10,9... | collective-permute-start | bytes 1966088 | tf_op jit(solution)/shard_map/ppermute | solution.py:378
  50.6 3.7 %expert_own.1 = (bf16[9576,128]{1,0:T(8,128)(2,1)}, bf16[128,768]{1,0:T(8,128)(2,1)S(1)}, f32[1,1280]{1,0:T(1,128)S(1)}, bf16[1280,384]{1,0:T(8,128)(2,1)S(1)}, bf16[384,1280]{1,0:T(8,128)(2,1)S(1)}) custom-call(s32[1]{0:T(128)} %bitcast.part_ref.index_ref, bf16[512,640]{1,0:T(8,128)(2,1)S(1)} %bitcast.25, bf16[1280,384]{1,0:T(8,128)(2,1)S(1)} %bitcast.29, ...), custom_call_target="tpu_custom_call" | custom-call | flops 1073741824 | bytes 6291456 | tf_op jit(solution)/shard_map/expert_own/pallas_call | solution.py:388
  54.3 9.7 %collective-permute-done.up_ref.up_hbm = bf16[512,640]{1,0:T(8,128)(2,1)S(1)} collective-permute-done((bf16[512,640]{1,0:T(8,128)(2,1)S(1)}, bf16[512,640]{1,0:T(8,128)(2,1)S(1)}, u32[]{:S(2)}, u32[]{:S(2)}) %collective-permute-start) | collective-permute-done | bytes 655392 | tf_op jit(solution)/shard_map/ppermute | solution.py:378
  64.0 1.5 collective-permute-done.1.down_ref.down_hbm
  65.6 3.6 %expert_rest.1 = (bf16[9576,128]{1,0:T(8,128)(2,1)}, bf16[256,768]{1,0:T(8,128)(2,1)S(1)}) custom-call(s32[1]{0:T(128)} %bitcast.part_ref.index_ref, bf16[512,640]{1,0:T(8,128)(2,1)S(1)} %collective-permute-done.up_ref.up_hbm, bf16[512,640]{1,0:T(8,128)(2,1)S(1)} %collective-permute-done.1.down_ref.down_hbm, ...), custom_call_target="tpu_custom_call", output_to_operand_aliasing={{0}: (7, {})} | custom-call | flops 2147483648 | bytes 8388608 | tf_op jit(solution)/shard_map/expert_rest/pallas_call | solution.py:408
  69.2 0.0 copy-start.2
  69.2 35.7 %fusion = bf16[800,128]{1,0:T(8,128)(2,1)S(1)} fusion(bf16[9576,128]{1,0:T(8,128)(2,1)} %get-tuple-element.25), kind=kCustom, calls=%all-reduce-scatter | all-reduce-scatter fusion | flops 1228801 | bytes 2660352
  104.9 3.0 %collective-permute-start.4 = (bf16[22,128]{1,0:T(8,128)(2,1)S(1)}, bf16[22,128]{1,0:T(8,128)(2,1)S(1)}, u32[]{:S(2)}, u32[]{:S(2)}) collective-permute-start(bf16[22,128]{1,0:T(8,128)(2,1)S(1)} %slice.7), channel_id=1, source_target_pairs={{0,1},{1,2},{2,3},{3,4},{4,5},{5,6},{6,7},{7,8},{8,9},{9,10},{10,1... | collective-permute-start | bytes 16904
  108.0 1.3 dynamic-slice.4
  109.9 1.1 concatenate
  111.0 0.1 constant_dynamic-slice_fusion.sum_ref
  111.0 0.8 to_tokens.1
  111.8 17.0 %all_to_all.11 = bf16[64,16,128]{2,1,0:T(8,128)(2,1)S(1)} all-to-all(bf16[64,16,128]{2,1,0:T(8,128)(2,1)S(1)} %bitcast.28), channel_id=1, replica_groups=mesh['dp'=32,'member'=2,'expert'=12] {'dp','member'}, dimensions={0} | all-to-all | bytes 524288 | tf_op jit(solution)/shard_map/all_to_all | solution.py:430
  128.8 0.6 collect.1
  129.5 21.0 %all-gather = bf16[1792,128]{1,0:T(8,128)(2,1)S(1)} all-gather(bf16[448,128]{1,0:T(8,128)(2,1)S(1)} %collect.1), channel_id=2, replica_groups={{0,3,6,9},{1,4,7,10},{2,5,8,11},{12,15,18,21},{13,16,19,22},{14,17,20,2..., dimensions={0}, use_global_device_ids=true | all-gather | bytes 573440 | tf_op jit(solution)/shard_map/all_gather | solution.py:446
  150.5 2.9 %collective-permute-start.2 = (bf16[3,448,128]{2,1,0:T(8,128)(2,1)S(1)}, bf16[3,448,128]{2,1,0:T(8,128)(2,1)S(1)}, u32[]{:S(2)}, u32[]{:S(2)}) collective-permute-start(bf16[3,448,128]{2,1,0:T(8,128)(2,1)S(1)} %bitcast.31), channel_id=1, source_target_pairs={{0,1},{1,2},{2,3},{3,4},{4,5},{5,6},{6,7},{7,8},{8,9},{9,10},{10,1... | collective-permute-start | bytes 1032200 | tf_op jit(solution)/shard_map/ppermute | solution.py:455
  153.5 4.1 %collective-permute-start.3 = (bf16[3,448,128]{2,1,0:T(8,128)(2,1)S(1)}, bf16[3,448,128]{2,1,0:T(8,128)(2,1)S(1)}, u32[]{:S(2)}, u32[]{:S(2)}) collective-permute-start(bf16[3,448,128]{2,1,0:T(8,128)(2,1)S(1)} %bitcast.32), channel_id=1, source_target_pairs={{0,11},{1,0},{2,1},{3,2},{4,3},{5,4},{6,5},{7,6},{8,7},{9,8},{10,9... | collective-permute-start | bytes 1032200 | tf_op jit(solution)/shard_map/ppermute | solution.py:456
  157.6 4.6 %weights.1 = (bf16[1280,384]{1,0:T(8,128)(2,1)}, bf16[384,1280]{1,0:T(8,128)(2,1)}) custom-call(bf16[512,640]{1,0:T(8,128)(2,1)S(1)} %bitcast.26, bf16[512,640]{1,0:T(8,128)(2,1)S(1)} %collective-permute-done.up_ref.up_hbm, bf16[512,640]{1,0:T(8,128)(2,1)S(1)} %collective-permute-done.1.down_ref.down_hbm, bf16[128,768]{1,0:T(8,128)(2,1)S(1)} %get-tuple-element.28.own_ref, ...), custom_call_target="tpu_custom_call" | custom-call | flops 1073741824 | bytes 6291456 | tf_op jit(solution)/shard_map/weights/pallas_call | solution.py:433
  162.3 3.1 %collective-permute-done.3.down_ref = bf16[3,448,128]{2,1,0:T(8,128)(2,1)S(1)} collective-permute-done((bf16[3,448,128]{2,1,0:T(8,128)(2,1)S(1)}, bf16[3,448,128]{2,1,0:T(8,128)(2,1)S(1)}, u32[]{:S(2)}, u32[]{:S(2)}) %collective-permute-start.3) | collective-permute-done | bytes 344096 | tf_op jit(solution)/shard_map/ppermute | solution.py:456
  165.4 1.9 %final.1 = (bf16[256,1280]{1,0:T(8,128)(2,1)}, f32[128,1280]{1,0:T(8,128)}, f32[64,1280]{1,0:T(8,128)}) custom-call(s32[1]{0:T(128)} %bitcast.part_ref.index_ref, bf16[4,448,128]{2,1,0:T(8,128)(2,1)S(1)} %bitcast.22, bf16[3,448,128]{2,1,0:T(8,128)(2,1)S(1)} %collective-permute-done.2.up_ref, bf16[3,448,128]{2,1,0:T(8,128)(2,1)S(1)} %collective-permute-done.3.down_ref), custom_call_target="tpu_custom_call" | custom-call | flops 1048576 | bytes 4194304 | tf_op jit(solution)/shard_map/final/pallas_call | solution.py:447
  (9 shorter events, 0.1 us)
Async XLA Ops:
  0.6 50.0 %copy-start = (f32[2,1280,32]{1,2,0:T(8,128)S(1)}, f32[2,1280,32]{1,2,0:T(8,128)}, u32[]{:S(2)}) copy-start(f32[2,1280,32]{1,2,0:T(8,128)} %param.8) | copy-start | bytes 983044
  0.7 49.9 %copy-start.1 = (bf16[1,1,1280,384]{3,2,1,0:T(8,128)(2,1)S(1)}, bf16[1,1,1280,384]{3,2,1,0:T(8,128)(2,1)}, u32[]{:S(2)}) copy-start(bf16[1,1,1280,384]{3,2,1,0:T(8,128)(2,1)} %param.9) | copy-start | bytes 2949124
  37.2 26.8 %collective-permute-start = (bf16[512,640]{1,0:T(8,128)(2,1)S(1)}, bf16[512,640]{1,0:T(8,128)(2,1)S(1)}, u32[]{:S(2)}, u32[]{:S(2)}) collective-permute-start(bf16[512,640]{1,0:T(8,128)(2,1)S(1)} %bitcast.23), channel_id=1, source_target_pairs={{0,1},{1,2},{2,3},{3,4},{4,5},{5,6},{6,7},{7,8},{8,9},{9,10},{10,1... | collective-permute-start | bytes 1966088 | tf_op jit(solution)/shard_map/ppermute | solution.py:378
  39.1 26.5 %collective-permute-start.1 = (bf16[512,640]{1,0:T(8,128)(2,1)S(1)}, bf16[512,640]{1,0:T(8,128)(2,1)S(1)}, u32[]{:S(2)}, u32[]{:S(2)}) collective-permute-start(bf16[512,640]{1,0:T(8,128)(2,1)S(1)} %bitcast.24), channel_id=1, source_target_pairs={{0,11},{1,0},{2,1},{3,2},{4,3},{5,4},{6,5},{7,6},{8,7},{9,8},{10,9... | collective-permute-start | bytes 1966088 | tf_op jit(solution)/shard_map/ppermute | solution.py:378
  69.2 59.6 %copy-start.2 = (s32[2,128]{1,0:T(2,128)S(1)}, s32[2,128]{1,0:T(2,128)}, u32[]{:S(2)}) copy-start(s32[2,128]{1,0:T(2,128)} %get-tuple-element.19.code_ref) | copy-start | bytes 3076
  104.9 5.0 %collective-permute-start.4 = (bf16[22,128]{1,0:T(8,128)(2,1)S(1)}, bf16[22,128]{1,0:T(8,128)(2,1)S(1)}, u32[]{:S(2)}, u32[]{:S(2)}) collective-permute-start(bf16[22,128]{1,0:T(8,128)(2,1)S(1)} %slice.7), channel_id=1, source_target_pairs={{0,1},{1,2},{2,3},{3,4},{4,5},{5,6},{6,7},{7,8},{8,9},{9,10},{10,1... | collective-permute-start | bytes 16904
  150.5 11.7 %collective-permute-start.2 = (bf16[3,448,128]{2,1,0:T(8,128)(2,1)S(1)}, bf16[3,448,128]{2,1,0:T(8,128)(2,1)S(1)}, u32[]{:S(2)}, u32[]{:S(2)}) collective-permute-start(bf16[3,448,128]{2,1,0:T(8,128)(2,1)S(1)} %bitcast.31), channel_id=1, source_target_pairs={{0,1},{1,2},{2,3},{3,4},{4,5},{5,6},{6,7},{7,8},{8,9},{9,10},{10,1... | collective-permute-start | bytes 1032200 | tf_op jit(solution)/shard_map/ppermute | solution.py:455
  153.5 11.9 %collective-permute-start.3 = (bf16[3,448,128]{2,1,0:T(8,128)(2,1)S(1)}, bf16[3,448,128]{2,1,0:T(8,128)(2,1)S(1)}, u32[]{:S(2)}, u32[]{:S(2)}) collective-permute-start(bf16[3,448,128]{2,1,0:T(8,128)(2,1)S(1)} %bitcast.32), channel_id=1, source_target_pairs={{0,11},{1,0},{2,1},{3,2},{4,3},{5,4},{6,5},{7,6},{8,7},{9,8},{10,9... | collective-permute-start | bytes 1032200 | tf_op jit(solution)/shard_map/ppermute | solution.py:456
